TPU v7x, 32 devices: a whole 2x2x4 slice. The times are simulated.
32 devices in a mesh: lat: 4 (over z), lon: 8 (over y, x, core).
Axes of the slice: x: 2, y: 2, z: 4, core: 2. Of those that a mesh axis runs over, the one named last changes fastest.
Arguments:
- lat_coef: float32 [4, 256, 1024], P(None, 'lat', 'lon'), may hold values from 0.02 to 0.12
- lon_coef: float32 [4, 256, 1024], P(None, 'lat', 'lon'), may hold values from 0.02 to 0.12
- std_scale: float32 [4, 256, 1024], P(None, 'lat', 'lon'), may hold values from 0.5 to 2
- land_mask: int32 [256, 1024], P('lat', 'lon'), may hold values 0 or 1
- lst_weights: float32 [4], replicated, may hold values from 0.1 to 0.6
- innovation: float32 [16384, 128], P(('lat', 'lon')), may hold values from -6 to 6
- inv_var: float32 [16384, 128], P(('lat', 'lon')), may hold values from 0.2 to 5
- owner: int32 [16384, 1], P(('lat', 'lon')), may hold values from 0 to 31; in each aligned block of 512 rows (0 to 511, 512 to 1023, ...) at most 32 rows name the same one
- row_ids: int32 [16384], P(('lat', 'lon')), may hold values from 0 to 63
- offsets: int32 [16384, 128], P(('lat', 'lon')), may hold values from 0 to 127
Outputs:
- increment: float32 [4, 256, 1024], P(None, 'lat', 'lon')
- departure: float32 [16384, 128], P(('lat', 'lon'))
Inputs may be any that keep to these rules, and one draw needn't show every extreme that they name: Within the 512 tiles of one device no owner is named more than 32 times.
All inputs are finite; a program needn't handle non-finite values. No bound on the sum of `land_mask` on one device may be relied on, other than what follows from the above.
Results may differ from a plain program's by a relative error of at most 0.00026.
Values sent between devices are 32-bit elements; how exact they have to be, the bound alone decides.
No kernel may reach another device: no remote copies, remote signals or barrier semaphores. Data moves between devices by JAX's collectives and lax.ppermute only.
A program may use at most 64 MiB of HBM per device.

v0:
```python
import math

import jax
import jax.numpy as jnp
from jax import lax
from jax.sharding import PartitionSpec as P

PASSES = 8
ITERS = 2


def with_halo(block, sides, width, periodic):
    for axis, dim in sides:
        count = lax.axis_size(axis)
        forward = [(i, i + 1) for i in range(count - 1)]
        if periodic:
            forward.append((count - 1, 0))
        backward = [(target, source) for source, target in forward]
        low = lax.ppermute(
            lax.slice_in_dim(block, block.shape[dim] - width, None, axis=dim), axis, forward
        )
        high = lax.ppermute(lax.slice_in_dim(block, 0, width, axis=dim), axis, backward)
        block = jnp.concatenate([low, block, high], axis=dim)
    return block


def lst_of(weights, field):
    total = weights[0] * field[0]
    for index in range(1, field.shape[0]):
        total = total + weights[index] * field[index]
    return total


def extend(field, width):
    taller = with_halo(field, (("lat", 1),), width, False)
    return with_halo(taller, (("lon", 2),), width, True)


def pass_step(field, north_face, east_face):
    centre = field[:, 1:-1, 1:-1]
    north = field[:, 2:, 1:-1]
    south = field[:, :-2, 1:-1]
    east = field[:, 1:-1, 2:]
    west = field[:, 1:-1, :-2]
    face_north = north_face[:, 1:-1, 1:-1]
    face_south = north_face[:, :-2, 1:-1]
    face_east = east_face[:, 1:-1, 1:-1]
    face_west = east_face[:, 1:-1, :-2]
    return (
        centre
        + face_north * (north - centre)
        - face_south * (centre - south)
        + face_east * (east - centre)
        - face_west * (centre - west)
    )


def diffuse(field, faces, rim_depth):
    fields = field.shape[0]
    for block in range(PASSES // rim_depth):
        grown = extend(field, rim_depth)
        for inner in range(rim_depth):
            window = faces[:, inner : faces.shape[1] - inner, inner : faces.shape[2] - inner]
            grown = pass_step(grown, window[:fields], window[fields:])
        field = grown
    return field


def total_sum(value):
    return lax.psum(value, ("lat", "lon"))


def cells_to_rows(values, offsets):
    columns = lax.broadcasted_iota(jnp.int32, (1, 1, offsets.shape[1]), 2)
    return jnp.sum(jnp.where(offsets[:, :, None] == columns, values[:, :, None], 0.0), axis=1)


def rows_to_cells(rows, offsets):
    columns = lax.broadcasted_iota(jnp.int32, (1, 1, offsets.shape[1]), 2)
    return jnp.sum(jnp.where(offsets[:, :, None] == columns, rows[:, None, :], 0.0), axis=2)


def blockwise(func, first, offsets):
    count, width = first.shape
    block_rows = math.gcd(count, 64)
    shaped = (count // block_rows, block_rows, width)

    def apply_block(pair):
        return func(pair[0], pair[1])

    result = lax.map(apply_block, (first.reshape(shaped), offsets.reshape(shaped)))
    return result.reshape(count, width)


def contract_first(left, right):
    return lax.dot_general(
        left,
        right,
        (((0,), (0,)), ((), ())),
        precision=lax.Precision.HIGHEST,
        preferred_element_type=jnp.float32,
    )


def on_device(
    lat_coef,
    lon_coef,
    std_scale,
    land_mask,
    lst_weights,
    innovation,
    inv_var,
    owner,
    row_ids,
    offsets,
):
    fields, tile_rows, tile_cols = lat_coef.shape
    tiles_here, row_width = innovation.shape
    devices = lax.axis_size("lat") * lax.axis_size("lon")
    capacity = max(2, 2 * tiles_here // devices)
    rows_here = tile_rows * tile_cols // row_width
    global_row = lax.axis_index("lat") * tile_rows + lax.broadcasted_iota(
        jnp.int32, (1, tile_rows, 1), 1
    )
    north_face = jnp.where(global_row == lax.axis_size("lat") * tile_rows - 1, 0.0, lat_coef)
    rim_depth = 4
    faces = extend(jnp.concatenate([north_face, lon_coef], 0), rim_depth)
    mask_field = land_mask.astype(jnp.float32)

    def forward(vector):
        return mask_field * std_scale * diffuse(vector, faces, rim_depth)

    def adjoint(vector):
        return diffuse(mask_field * std_scale * vector, faces, rim_depth)

    def spread(grid):
        return lst_weights[:, None, None] * grid[None]

    destination = owner[:, 0]
    hits = (destination[:, None] == jnp.arange(devices, dtype=jnp.int32)[None, :]).astype(jnp.int32)
    bucket_rank = jnp.sum(jnp.cumsum(hits, axis=0) * hits, axis=1) - 1
    slot_index = destination * capacity + bucket_rank
    slot_range = jnp.arange(devices * capacity, dtype=jnp.int32)
    placement = (slot_range[:, None] == slot_index[None, :]).astype(jnp.float32)
    send_ids = (
        jnp.sum(
            jnp.where(slot_range[:, None] == slot_index[None, :], row_ids[None, :] + 1, 0), axis=1
        )
        - 1
    )
    got_ids = lax.all_to_all(send_ids, ("lat", "lon"), split_axis=0, concat_axis=0, tiled=True)
    ownership = (got_ids[:, None] == jnp.arange(rows_here, dtype=jnp.int32)[None, :]).astype(
        jnp.float32
    )

    def to_rows(values):
        return blockwise(cells_to_rows, values, offsets)

    def pack(rows):
        return jnp.dot(
            placement, rows, precision=lax.Precision.HIGHEST, preferred_element_type=jnp.float32
        )

    def collect(buffer):
        return contract_first(ownership, buffer)

    def send_back(values):
        arrived = lax.all_to_all(
            pack(to_rows(values)), ("lat", "lon"), split_axis=0, concat_axis=0, tiled=True
        )
        return spread(collect(arrived))

    residual = adjoint(send_back(inv_var * innovation))
    direction = residual
    norm_now = total_sum(jnp.sum(residual * residual))
    increment = jnp.zeros_like(residual)
    analysed = jnp.zeros_like(innovation)
    for index in range(ITERS):
        image = forward(direction)
        returned = lax.all_to_all(
            jnp.dot(
                ownership,
                lst_of(lst_weights, image),
                precision=lax.Precision.HIGHEST,
                preferred_element_type=jnp.float32,
            ),
            ("lat", "lon"),
            split_axis=0,
            concat_axis=0,
            tiled=True,
        )
        seen = blockwise(rows_to_cells, contract_first(placement, returned), offsets)
        product = direction + adjoint(send_back(inv_var * seen))
        step_size = norm_now / total_sum(jnp.sum(direction * product))
        increment = increment + step_size * image
        analysed = analysed + step_size * seen
        if index + 1 < ITERS:
            residual = residual - step_size * product
            norm_next = total_sum(jnp.sum(residual * residual))
            direction = residual + norm_next / norm_now * direction
            norm_now = norm_next
    return (increment, innovation - analysed)


def solution(mesh):
    in_specs = (
        P(None, "lat", "lon"),
        P(None, "lat", "lon"),
        P(None, "lat", "lon"),
        P("lat", "lon"),
        P(),
        P(("lat", "lon"), None),
        P(("lat", "lon"), None),
        P(("lat", "lon"), None),
        P(("lat", "lon")),
        P(("lat", "lon"), None),
    )
    out_specs = (P(None, "lat", "lon"), P(("lat", "lon"), None))
    return jax.shard_map(
        on_device, mesh=mesh, in_specs=in_specs, out_specs=out_specs, check_vma=False
    )
```

profile of v0, /device:TPU:0, one launch (start us, length us, event | category | flops | bytes accessed | tf_op | source)
XLA Modules:
  0.0 555.0 jit_solution(16266994151909909597)
XLA Ops:
  5.3 7.3 %all-to-all-start = ((s32[32,32,1]{1,2,0:T(1,128)}), s32[32,32,1]{1,2,0:T(1,128)S(1)}, u32[]{:S(2)}, u32[]{:S(2)}) async-start(s32[32,32,1]{1,2,0:T(1,128)} %sub.738), calls=%async_computation | async-start | bytes 32768 | tf_op jit(solution)/shard_map/all_to_all | solution.py:151
  13.7 22.9 %while.50 = (s32[]{:T(128)}, f32[8,64,128]{2,1,0:T(8,128)S(1)}, s32[8,64,128]{2,1,0:T(8,128)S(1)}, f32[8,64,128]{2,1,0:T(8,128)S(1)}, s32[]{:T(128)}) while((s32[]{:T(128)}, f32[8,64,128]{2,1,0:T(8,128)S(1)}, s32[8,64,128]{2,1,0:T(8,128)S(1)}, f32[8,64,128]{2,1,0:T(8,128)S(1)}, s32[]{:T(128)}) %tuple.124), condition=%wide.region_6.7_spmd, body=%wide.region_4.6_spmd.sunk | while | flops 3137538 | bytes 294985 | solution.py:91
  13.8 2.8 select_reduce_fusion.11
  16.6 2.8 select_reduce_fusion.11
  19.5 2.8 select_reduce_fusion.11
  22.3 2.8 select_reduce_fusion.11
  25.2 2.8 select_reduce_fusion.11
  28.1 2.8 select_reduce_fusion.11
  30.9 2.8 select_reduce_fusion.11
  33.8 2.8 select_reduce_fusion.11
  38.5 5.8 %all-to-all-start.1 = ((f32[32,32,128]{2,1,0:T(8,128)}), f32[32,32,128]{2,1,0:T(8,128)S(1)}, u32[]{:S(2)}, u32[]{:S(2)}) async-start(f32[32,32,128]{2,1,0:T(8,128)} %fusion.4), calls=%async_computation.1 | async-start | bytes 1048576 | tf_op jit(solution)/shard_map/all_to_all | solution.py:168
  44.4 3.7 collective-permute-start.4
  50.7 3.1 collective-permute-done.4
  56.8 3.1 all-to-all-done.1
  60.8 5.1 collective-permute-start
  67.5 4.0 collective-permute-done.1
  83.8 4.2 collective-permute-done.9
  90.8 4.4 collective-permute-done.10
  100.8 4.2 collective-permute-done.13
  105.2 2.8 collective-permute-start.15
  108.0 3.2 collective-permute-done.14
  116.9 4.2 collective-permute-done.17
  129.6 3.7 fusion.18
  133.3 2.9 all-to-all-start.2
  136.6 15.2 %all-to-all-done.2 = f32[32,32,128]{2,1,0:T(8,128)S(1)} async-done(((f32[32,32,128]{2,1,0:T(8,128)}), f32[32,32,128]{2,1,0:T(8,128)S(1)}, u32[]{:S(2)}, u32[]{:S(2)}) %all-to-all-start.2) | async-done | bytes 524320 | tf_op jit(solution)/shard_map/all_to_all | solution.py:180
  153.6 27.1 %while.51 = (s32[]{:T(128)}, f32[8,64,128]{2,1,0:T(8,128)S(1)}, s32[8,64,128]{2,1,0:T(8,128)S(1)}, f32[8,64,128]{2,1,0:T(8,128)}, s32[]{:T(128)}) while((s32[]{:T(128)}, f32[8,64,128]{2,1,0:T(8,128)S(1)}, s32[8,64,128]{2,1,0:T(8,128)S(1)}, f32[8,64,128]{2,1,0:T(8,128)}, s32[]{:T(128)}) %tuple.119), condition=%wide.region_11.12_spmd, body=%wide.region_9.11_spmd.sunk | while | flops 3137538 | bytes 294985 | solution.py:91
  181.4 27.3 %while.52 = (s32[]{:T(128)}, f32[8,64,128]{2,1,0:T(8,128)}, s32[8,64,128]{2,1,0:T(8,128)S(1)}, f32[8,64,128]{2,1,0:T(8,128)S(1)}, s32[]{:T(128)}) while((s32[]{:T(128)}, f32[8,64,128]{2,1,0:T(8,128)}, s32[8,64,128]{2,1,0:T(8,128)S(1)}, f32[8,64,128]{2,1,0:T(8,128)S(1)}, s32[]{:T(128)}) %tuple.125), condition=%wide.region_14.15_spmd, body=%wide.region_12.14_spmd.sunk | while | flops 3137538 | bytes 295493 | solution.py:91
  181.4 2.8 select_reduce_fusion.13
  195.1 2.8 select_reduce_fusion.13
  210.7 18.4 %all_to_all.54 = f32[32,32,128]{2,1,0:T(8,128)S(1)} all-to-all(f32[32,32,128]{2,1,0:T(8,128)S(1)} %fusion.2), channel_id=1, replica_groups=mesh['lat'=4,'lon'=8] {'lat','lon'}, dimensions={0} | all-to-all | bytes 1048576 | tf_op jit(solution)/shard_map/all_to_all | solution.py:168
  230.0 3.1 collective-permute-start.20
  234.5 4.2 collective-permute-done.21
  238.8 2.8 collective-permute-start.23
  241.7 3.9 collective-permute-done.22
  250.9 4.2 collective-permute-done.25
  257.9 4.0 collective-permute-done.26
  264.9 38.1 %all-reduce = (f32[]{:T(128)}, f32[]{:T(128)}) all-reduce(f32[]{:T(128)} %get-tuple-element.118, f32[]{:T(128)} %get-tuple-element.117), channel_id=1, replica_groups=mesh['lat'=4,'lon'=8] {'lat','lon'}, use_global_device_ids=true, to_apply=%region_8.9 | all-reduce | flops 2 | bytes 16 | tf_op jit(solution)/shard_map/psum | solution.py:70
  305.1 40.7 %psum.30 = f32[]{:T(128)} all-reduce(f32[]{:T(128)} %multiply_reduce_fusion), channel_id=1, replica_groups=mesh['lat'=4,'lon'=8] {'lat','lon'}, use_global_device_ids=true, to_apply=%region_18.19 | all-reduce | flops 1 | bytes 8 | tf_op jit(solution)/shard_map/psum | solution.py:70
  347.3 3.5 collective-permute-start.28
  352.1 4.2 collective-permute-done.29
  359.1 2.9 collective-permute-done.30
  368.8 4.2 collective-permute-done.33
  376.0 3.8 collective-permute-done.34
  382.2 3.7 fusion.16
  385.9 3.7 all-to-all-start.4
  389.6 15.6 %all-to-all-done.4 = f32[32,32,128]{2,1,0:T(8,128)} async-done(((f32[32,32,128]{2,1,0:T(8,128)}), f32[32,32,128]{2,1,0:T(8,128)}, u32[]{:S(2)}, u32[]{:S(2)}) %all-to-all-start.4) | async-done | bytes 524320 | tf_op jit(solution)/shard_map/all_to_all | solution.py:180
  408.0 27.1 %while.53 = (s32[]{:T(128)}, f32[8,64,128]{2,1,0:T(8,128)S(1)}, s32[8,64,128]{2,1,0:T(8,128)S(1)}, f32[8,64,128]{2,1,0:T(8,128)}, s32[]{:T(128)}) while((s32[]{:T(128)}, f32[8,64,128]{2,1,0:T(8,128)S(1)}, s32[8,64,128]{2,1,0:T(8,128)S(1)}, f32[8,64,128]{2,1,0:T(8,128)}, s32[]{:T(128)}) %tuple.121), condition=%wide.region_21.22_spmd, body=%wide.region_19.21_spmd.sunk | while | flops 3137538 | bytes 294985 | solution.py:91
  435.1 22.9 %while.54 = (s32[]{:T(128)}, f32[8,64,128]{2,1,0:T(8,128)S(1)}, s32[8,64,128]{2,1,0:T(8,128)S(1)}, f32[8,64,128]{2,1,0:T(8,128)S(1)}, s32[]{:T(128)}) while((s32[]{:T(128)}, f32[8,64,128]{2,1,0:T(8,128)S(1)}, s32[8,64,128]{2,1,0:T(8,128)S(1)}, f32[8,64,128]{2,1,0:T(8,128)S(1)}, s32[]{:T(128)}) %tuple.123), condition=%wide.region_24.25_spmd, body=%wide.region_22.24_spmd.sunk | while | flops 3137538 | bytes 294985 | solution.py:91
  435.2 2.8 select_reduce_fusion.15
  438.0 2.8 select_reduce_fusion.15
  440.9 2.8 select_reduce_fusion.15
  443.7 2.8 select_reduce_fusion.15
  446.6 2.8 select_reduce_fusion.15
  449.5 2.8 select_reduce_fusion.15
  452.3 2.8 select_reduce_fusion.15
  455.2 2.8 select_reduce_fusion.15
  459.0 18.4 %all_to_all.55 = f32[32,32,128]{2,1,0:T(8,128)S(1)} all-to-all(f32[32,32,128]{2,1,0:T(8,128)S(1)} %fusion), channel_id=1, replica_groups=mesh['lat'=4,'lon'=8] {'lat','lon'}, dimensions={0} | all-to-all | bytes 1048576 | tf_op jit(solution)/shard_map/all_to_all | solution.py:168
  478.3 3.1 collective-permute-start.36
  482.8 4.2 collective-permute-done.37
  489.8 4.3 collective-permute-done.38
  499.4 4.2 collective-permute-done.41
  503.8 2.9 collective-permute-start.43
  506.7 3.8 collective-permute-done.42
  513.5 38.2 %psum.31 = f32[]{:T(128)} all-reduce(f32[]{:T(128)} %fusion.267), channel_id=1, replica_groups=mesh['lat'=4,'lon'=8] {'lat','lon'}, use_global_device_ids=true, to_apply=%region_26.27 | all-reduce | flops 1 | bytes 8 | tf_op jit(solution)/shard_map/psum | solution.py:70
  (351 shorter events, 180.1 us)
Async XLA Ops:
  0.6 12.1 %copy-start.3 = (f32[512,128]{1,0:T(8,128)S(1)}, f32[512,128]{1,0:T(8,128)}, u32[]{:S(2)}) copy-start(f32[512,128]{1,0:T(8,128)} %param.26) | copy-start | bytes 786436
  3.6 10.1 %copy-start.2 = (s32[512,128]{1,0:T(8,128)S(1)}, s32[512,128]{1,0:T(8,128)}, u32[]{:S(2)}) copy-start(s32[512,128]{1,0:T(8,128)} %param.29) | copy-start | bytes 786436
  5.3 33.1 %all-to-all-start = ((s32[32,32,1]{1,2,0:T(1,128)}), s32[32,32,1]{1,2,0:T(1,128)S(1)}, u32[]{:S(2)}, u32[]{:S(2)}) async-start(s32[32,32,1]{1,2,0:T(1,128)} %sub.738), calls=%async_computation | async-start | bytes 32768 | tf_op jit(solution)/shard_map/all_to_all | solution.py:151
  38.4 5.9 %copy-start.7 = (f32[4,64,128]{2,1,0:T(8,128)S(1)}, f32[4,64,128]{2,1,0:T(8,128)}, u32[]{:S(2)}) copy-start(f32[4,64,128]{2,1,0:T(8,128)} %param.20) | copy-start | bytes 393220
  38.4 6.0 %copy-start = (f32[4,64,128]{2,1,0:T(8,128)S(1)}, f32[4,64,128]{2,1,0:T(8,128)}, u32[]{:S(2)}) copy-start(f32[4,64,128]{2,1,0:T(8,128)} %param.21) | copy-start | bytes 393220
  38.4 11.0 %copy-start.8 = (s32[64,128]{1,0:T(8,128)S(1)}, s32[64,128]{1,0:T(8,128)}, u32[]{:S(2)}) copy-start(s32[64,128]{1,0:T(8,128)} %param.23) | copy-start | bytes 98308
  38.5 21.5 %all-to-all-start.1 = ((f32[32,32,128]{2,1,0:T(8,128)}), f32[32,32,128]{2,1,0:T(8,128)S(1)}, u32[]{:S(2)}, u32[]{:S(2)}) async-start(f32[32,32,128]{2,1,0:T(8,128)} %fusion.4), calls=%async_computation.1 | async-start | bytes 1048576 | tf_op jit(solution)/shard_map/all_to_all | solution.py:168
  44.4 9.4 %collective-permute-start.4 = (f32[8,4,128]{2,1,0:T(4,128)S(1)}, f32[8,4,128]{2,1,0:T(4,128)S(1)}, u32[]{:S(2)}, u32[]{:S(2)}) collective-permute-start(f32[8,4,128]{2,1,0:T(4,128)S(1)} %get-tuple-element.166), channel_id=1, source_target_pairs={{0,8},{8,16},{16,24},{1,9},{9,17},{17,25},{2,10},{10,18},{18,26},{... | collective-permute-start | bytes 49160 | tf_op jit(solution)/shard_map/ppermute | solution.py:19
  48.1 5.8 %collective-permute-start.5 = (f32[8,4,128]{2,1,0:T(4,128)S(1)}, f32[8,4,128]{2,1,0:T(4,128)S(1)}, u32[]{:S(2)}, u32[]{:S(2)}) collective-permute-start(f32[8,4,128]{2,1,0:T(4,128)S(1)} %get-tuple-element.167), channel_id=1, source_target_pairs={{8,0},{16,8},{24,16},{9,1},{17,9},{25,17},{10,2},{18,10},{26,18},{... | collective-permute-start | bytes 49160 | tf_op jit(solution)/shard_map/ppermute | solution.py:22
  53.9 6.8 %copy-start.1 = (f32[4,64,128]{2,1,0:T(8,128)S(1)}, f32[4,64,128]{2,1,0:T(8,128)}, u32[]{:S(2)}) copy-start(f32[4,64,128]{2,1,0:T(8,128)} %param.22) | copy-start | bytes 393220
  53.9 6.8 %copy-start.9 = (f32[4]{0:T(128)S(1)}, f32[4]{0:T(128)}, u32[]{:S(2)}) copy-start(f32[4]{0:T(128)} %param.24) | copy-start | bytes 52
  54.1 13.1 %collective-permute-start.6 = (f32[8,72,4]{2,1,0:T(8,128)S(1)}, f32[8,72,4]{2,1,0:T(8,128)S(1)}, u32[]{:S(2)}, u32[]{:S(2)}) collective-permute-start(f32[8,72,4]{2,1,0:T(8,128)S(1)} %get-tuple-element.164), channel_id=1, source_target_pairs={{0,1},{1,2},{2,3},{3,4},{4,5},{5,6},{6,7},{7,0},{8,9},{9,10},{10,1... | collective-permute-start | bytes 27656 | tf_op jit(solution)/shard_map/ppermute | solution.py:19
  54.2 20.1 %collective-permute-start.7 = (f32[8,72,4]{2,1,0:T(8,128)S(1)}, f32[8,72,4]{2,1,0:T(8,128)}, u32[]{:S(2)}, u32[]{:S(2)}) collective-permute-start(f32[8,72,4]{2,1,0:T(8,128)S(1)} %get-tuple-element.165), channel_id=1, source_target_pairs={{1,0},{2,1},{3,2},{4,3},{5,4},{6,5},{7,6},{0,7},{9,8},{10,9},{11,1... | collective-permute-start | bytes 27656 | tf_op jit(solution)/shard_map/ppermute | solution.py:22
  60.8 6.7 %collective-permute-start = (f32[4,4,128]{2,1,0:T(4,128)S(1)}, f32[4,4,128]{2,1,0:T(4,128)S(1)}, u32[]{:S(2)}, u32[]{:S(2)}) collective-permute-start(f32[4,4,128]{2,1,0:T(4,128)S(1)} %get-tuple-element.206), channel_id=1, source_target_pairs={{0,8},{8,16},{16,24},{1,9},{9,17},{17,25},{2,10},{10,18},{18,26},{... | collective-permute-start | bytes 24584 | tf_op jit(solution)/shard_map/ppermute | solution.py:19
  65.9 5.5 collective-permute-start.1
  71.5 6.2 %collective-permute-start.2 = (f32[4,72,4]{2,1,0:T(8,128)S(1)}, f32[4,72,4]{2,1,0:T(8,128)S(1)}, u32[]{:S(2)}, u32[]{:S(2)}) collective-permute-start(f32[4,72,4]{2,1,0:T(8,128)S(1)} %get-tuple-element.186), channel_id=1, source_target_pairs={{0,1},{1,2},{2,3},{3,4},{4,5},{5,6},{6,7},{7,0},{8,9},{9,10},{10,1... | collective-permute-start | bytes 13832 | tf_op jit(solution)/shard_map/ppermute | solution.py:19
  71.6 6.1 %collective-permute-start.3 = (f32[4,72,4]{2,1,0:T(8,128)S(1)}, f32[4,72,4]{2,1,0:T(8,128)S(1)}, u32[]{:S(2)}, u32[]{:S(2)}) collective-permute-start(f32[4,72,4]{2,1,0:T(8,128)S(1)} %get-tuple-element.187), channel_id=1, source_target_pairs={{1,0},{2,1},{3,2},{4,3},{5,4},{6,5},{7,6},{0,7},{9,8},{10,9},{11,1... | collective-permute-start | bytes 13832 | tf_op jit(solution)/shard_map/ppermute | solution.py:22
  80.2 3.5 collective-permute-start.8
  82.4 5.5 collective-permute-start.9
  88.1 7.1 %collective-permute-start.10 = (f32[4,72,4]{2,1,0:T(8,128)S(1)}, f32[4,72,4]{2,1,0:T(8,128)S(1)}, u32[]{:S(2)}, u32[]{:S(2)}) collective-permute-start(f32[4,72,4]{2,1,0:T(8,128)S(1)} %get-tuple-element.184), channel_id=1, source_target_pairs={{0,1},{1,2},{2,3},{3,4},{4,5},{5,6},{6,7},{7,0},{8,9},{9,10},{10,1... | collective-permute-start | bytes 13832 | tf_op jit(solution)/shard_map/ppermute | solution.py:19
  88.1 7.0 %collective-permute-start.11 = (f32[4,72,4]{2,1,0:T(8,128)S(1)}, f32[4,72,4]{2,1,0:T(8,128)S(1)}, u32[]{:S(2)}, u32[]{:S(2)}) collective-permute-start(f32[4,72,4]{2,1,0:T(8,128)S(1)} %get-tuple-element.185), channel_id=1, source_target_pairs={{1,0},{2,1},{3,2},{4,3},{5,4},{6,5},{7,6},{0,7},{9,8},{10,9},{11,1... | collective-permute-start | bytes 13832 | tf_op jit(solution)/shard_map/ppermute | solution.py:22
  97.6 3.3 collective-permute-start.12
  99.5 5.5 collective-permute-start.13
  105.2 6.1 %collective-permute-start.14 = (f32[4,72,4]{2,1,0:T(8,128)S(1)}, f32[4,72,4]{2,1,0:T(8,128)S(1)}, u32[]{:S(2)}, u32[]{:S(2)}) collective-permute-start(f32[4,72,4]{2,1,0:T(8,128)S(1)} %get-tuple-element.182), channel_id=1, source_target_pairs={{0,1},{1,2},{2,3},{3,4},{4,5},{5,6},{6,7},{7,0},{8,9},{9,10},{10,1... | collective-permute-start | bytes 13832 | tf_op jit(solution)/shard_map/ppermute | solution.py:19
  105.2 6.0 %collective-permute-start.15 = (f32[4,72,4]{2,1,0:T(8,128)S(1)}, f32[4,72,4]{2,1,0:T(8,128)S(1)}, u32[]{:S(2)}, u32[]{:S(2)}) collective-permute-start(f32[4,72,4]{2,1,0:T(8,128)S(1)} %get-tuple-element.183), channel_id=1, source_target_pairs={{1,0},{2,1},{3,2},{4,3},{5,4},{6,5},{7,6},{0,7},{9,8},{10,9},{11,1... | collective-permute-start | bytes 13832 | tf_op jit(solution)/shard_map/ppermute | solution.py:22
  113.7 3.3 collective-permute-start.16
  115.6 5.5 collective-permute-start.17
  121.3 5.9 %collective-permute-start.18 = (f32[4,72,4]{2,1,0:T(8,128)S(1)}, f32[4,72,4]{2,1,0:T(8,128)S(1)}, u32[]{:S(2)}, u32[]{:S(2)}) collective-permute-start(f32[4,72,4]{2,1,0:T(8,128)S(1)} %get-tuple-element.180), channel_id=1, source_target_pairs={{0,1},{1,2},{2,3},{3,4},{4,5},{5,6},{6,7},{7,0},{8,9},{9,10},{10,1... | collective-permute-start | bytes 13832 | tf_op jit(solution)/shard_map/ppermute | solution.py:19
  121.3 5.9 %collective-permute-start.19 = (f32[4,72,4]{2,1,0:T(8,128)S(1)}, f32[4,72,4]{2,1,0:T(8,128)S(1)}, u32[]{:S(2)}, u32[]{:S(2)}) collective-permute-start(f32[4,72,4]{2,1,0:T(8,128)S(1)} %get-tuple-element.181), channel_id=1, source_target_pairs={{1,0},{2,1},{3,2},{4,3},{5,4},{6,5},{7,6},{0,7},{9,8},{10,9},{11,1... | collective-permute-start | bytes 13832 | tf_op jit(solution)/shard_map/ppermute | solution.py:22
  129.6 3.7 copy-start.5
  133.3 18.5 %all-to-all-start.2 = ((f32[32,32,128]{2,1,0:T(8,128)}), f32[32,32,128]{2,1,0:T(8,128)S(1)}, u32[]{:S(2)}, u32[]{:S(2)}) async-start(f32[32,32,128]{2,1,0:T(8,128)} %fusion.18), calls=%async_computation.2 | async-start | bytes 1048576 | tf_op jit(solution)/shard_map/all_to_all | solution.py:180
  230.0 4.5 collective-permute-start.20
  233.1 5.5 collective-permute-start.21
  238.8 6.8 %collective-permute-start.22 = (f32[4,72,4]{2,1,0:T(8,128)S(1)}, f32[4,72,4]{2,1,0:T(8,128)S(1)}, u32[]{:S(2)}, u32[]{:S(2)}) collective-permute-start(f32[4,72,4]{2,1,0:T(8,128)S(1)} %get-tuple-element.178), channel_id=1, source_target_pairs={{0,1},{1,2},{2,3},{3,4},{4,5},{5,6},{6,7},{7,0},{8,9},{9,10},{10,1... | collective-permute-start | bytes 13832 | tf_op jit(solution)/shard_map/ppermute | solution.py:19
  238.8 6.7 %collective-permute-start.23 = (f32[4,72,4]{2,1,0:T(8,128)S(1)}, f32[4,72,4]{2,1,0:T(8,128)S(1)}, u32[]{:S(2)}, u32[]{:S(2)}) collective-permute-start(f32[4,72,4]{2,1,0:T(8,128)S(1)} %get-tuple-element.179), channel_id=1, source_target_pairs={{1,0},{2,1},{3,2},{4,3},{5,4},{6,5},{7,6},{0,7},{9,8},{10,9},{11,1... | collective-permute-start | bytes 13832 | tf_op jit(solution)/shard_map/ppermute | solution.py:22
  248.0 2.9 collective-permute-start.24
  249.6 5.5 collective-permute-start.25
  255.2 6.7 %collective-permute-start.26 = (f32[4,72,4]{2,1,0:T(8,128)S(1)}, f32[4,72,4]{2,1,0:T(8,128)S(1)}, u32[]{:S(2)}, u32[]{:S(2)}) collective-permute-start(f32[4,72,4]{2,1,0:T(8,128)S(1)} %get-tuple-element.176), channel_id=1, source_target_pairs={{0,1},{1,2},{2,3},{3,4},{4,5},{5,6},{6,7},{7,0},{8,9},{9,10},{10,1... | collective-permute-start | bytes 13832 | tf_op jit(solution)/shard_map/ppermute | solution.py:19
  255.3 6.6 %collective-permute-start.27 = (f32[4,72,4]{2,1,0:T(8,128)S(1)}, f32[4,72,4]{2,1,0:T(8,128)S(1)}, u32[]{:S(2)}, u32[]{:S(2)}) collective-permute-start(f32[4,72,4]{2,1,0:T(8,128)S(1)} %get-tuple-element.177), channel_id=1, source_target_pairs={{1,0},{2,1},{3,2},{4,3},{5,4},{6,5},{7,6},{0,7},{9,8},{10,9},{11,1... | collective-permute-start | bytes 13832 | tf_op jit(solution)/shard_map/ppermute | solution.py:22
  347.3 4.9 collective-permute-start.28
  350.8 5.5 collective-permute-start.29
  356.4 5.6 %collective-permute-start.30 = (f32[4,72,4]{2,1,0:T(8,128)S(1)}, f32[4,72,4]{2,1,0:T(8,128)S(1)}, u32[]{:S(2)}, u32[]{:S(2)}) collective-permute-start(f32[4,72,4]{2,1,0:T(8,128)S(1)} %get-tuple-element.174), channel_id=1, source_target_pairs={{0,1},{1,2},{2,3},{3,4},{4,5},{5,6},{6,7},{7,0},{8,9},{9,10},{10,1... | collective-permute-start | bytes 13832 | tf_op jit(solution)/shard_map/ppermute | solution.py:19
  356.5 5.9 %collective-permute-start.31 = (f32[4,72,4]{2,1,0:T(8,128)S(1)}, f32[4,72,4]{2,1,0:T(8,128)S(1)}, u32[]{:S(2)}, u32[]{:S(2)}) collective-permute-start(f32[4,72,4]{2,1,0:T(8,128)S(1)} %get-tuple-element.175), channel_id=1, source_target_pairs={{1,0},{2,1},{3,2},{4,3},{5,4},{6,5},{7,6},{0,7},{9,8},{10,9},{11,1... | collective-permute-start | bytes 13832 | tf_op jit(solution)/shard_map/ppermute | solution.py:22
  364.9 3.9 collective-permute-start.32
  367.4 5.5 collective-permute-start.33
  373.1 6.7 %collective-permute-start.34 = (f32[4,72,4]{2,1,0:T(8,128)S(1)}, f32[4,72,4]{2,1,0:T(8,128)S(1)}, u32[]{:S(2)}, u32[]{:S(2)}) collective-permute-start(f32[4,72,4]{2,1,0:T(8,128)S(1)} %get-tuple-element.172), channel_id=1, source_target_pairs={{0,1},{1,2},{2,3},{3,4},{4,5},{5,6},{6,7},{7,0},{8,9},{9,10},{10,1... | collective-permute-start | bytes 13832 | tf_op jit(solution)/shard_map/ppermute | solution.py:19
  373.7 6.1 %collective-permute-start.35 = (f32[4,72,4]{2,1,0:T(8,128)S(1)}, f32[4,72,4]{2,1,0:T(8,128)S(1)}, u32[]{:S(2)}, u32[]{:S(2)}) collective-permute-start(f32[4,72,4]{2,1,0:T(8,128)S(1)} %get-tuple-element.173), channel_id=1, source_target_pairs={{1,0},{2,1},{3,2},{4,3},{5,4},{6,5},{7,6},{0,7},{9,8},{10,9},{11,1... | collective-permute-start | bytes 13832 | tf_op jit(solution)/shard_map/ppermute | solution.py:22
  385.9 19.3 %all-to-all-start.4 = ((f32[32,32,128]{2,1,0:T(8,128)}), f32[32,32,128]{2,1,0:T(8,128)}, u32[]{:S(2)}, u32[]{:S(2)}) async-start(f32[32,32,128]{2,1,0:T(8,128)} %fusion.16), calls=%async_computation.4 | async-start | bytes 1048576 | tf_op jit(solution)/shard_map/all_to_all | solution.py:180
  478.3 4.5 collective-permute-start.36
  481.4 5.5 collective-permute-start.37
  487.1 7.0 %collective-permute-start.38 = (f32[4,72,4]{2,1,0:T(8,128)S(1)}, f32[4,72,4]{2,1,0:T(8,128)S(1)}, u32[]{:S(2)}, u32[]{:S(2)}) collective-permute-start(f32[4,72,4]{2,1,0:T(8,128)S(1)} %get-tuple-element.170), channel_id=1, source_target_pairs={{0,1},{1,2},{2,3},{3,4},{4,5},{5,6},{6,7},{7,0},{8,9},{9,10},{10,1... | collective-permute-start | bytes 13832 | tf_op jit(solution)/shard_map/ppermute | solution.py:19
  487.2 6.9 %collective-permute-start.39 = (f32[4,72,4]{2,1,0:T(8,128)S(1)}, f32[4,72,4]{2,1,0:T(8,128)S(1)}, u32[]{:S(2)}, u32[]{:S(2)}) collective-permute-start(f32[4,72,4]{2,1,0:T(8,128)S(1)} %get-tuple-element.171), channel_id=1, source_target_pairs={{1,0},{2,1},{3,2},{4,3},{5,4},{6,5},{7,6},{0,7},{9,8},{10,9},{11,1... | collective-permute-start | bytes 13832 | tf_op jit(solution)/shard_map/ppermute | solution.py:22
  496.5 2.9 collective-permute-start.40
  498.1 5.5 collective-permute-start.41
  503.8 6.8 %collective-permute-start.42 = (f32[4,72,4]{2,1,0:T(8,128)S(1)}, f32[4,72,4]{2,1,0:T(8,128)S(1)}, u32[]{:S(2)}, u32[]{:S(2)}) collective-permute-start(f32[4,72,4]{2,1,0:T(8,128)S(1)} %get-tuple-element.168), channel_id=1, source_target_pairs={{0,1},{1,2},{2,3},{3,4},{4,5},{5,6},{6,7},{7,0},{8,9},{9,10},{10,1... | collective-permute-start | bytes 13832 | tf_op jit(solution)/shard_map/ppermute | solution.py:19
  503.8 6.7 %collective-permute-start.43 = (f32[4,72,4]{2,1,0:T(8,128)S(1)}, f32[4,72,4]{2,1,0:T(8,128)S(1)}, u32[]{:S(2)}, u32[]{:S(2)}) collective-permute-start(f32[4,72,4]{2,1,0:T(8,128)S(1)} %get-tuple-element.169), channel_id=1, source_target_pairs={{1,0},{2,1},{3,2},{4,3},{5,4},{6,5},{7,6},{0,7},{9,8},{10,9},{11,1... | collective-permute-start | bytes 13832 | tf_op jit(solution)/shard_map/ppermute | solution.py:22
  512.7 40.4 %copy-start.4 = (f32[512,128]{1,0:T(8,128)S(1)}, f32[512,128]{1,0:T(8,128)}, u32[]{:S(2)}) copy-start(f32[512,128]{1,0:T(8,128)} %param.25) | copy-start | bytes 786436
  513.5 40.3 %copy-start.6 = (f32[4,64,128]{2,1,0:T(8,128)S(1)}, f32[4,64,128]{2,1,0:T(8,128)}, u32[]{:S(2)}) copy-start(f32[4,64,128]{2,1,0:T(8,128)} %copy-done.5) | copy-start | bytes 393220
where the time goes:
time: 565 us; the launch traced here: 555 us
  blocking collectives  154 us (27%)
  other arithmetic  143 us (25%)
  waiting for transfers between devices  115 us (20%)
  starting transfers between devices  94.7 us (17%)
  local copies, waits for them, and re-layouts  22.1 us (4%)
  matrix products  18.9 us (3%)
  between operations  6.39 us (1%)
    psum x3, blocking collectives, total_sum(): return lax.psum(value, ('lat', 'lon'))  117 us
    reduce_sum x24, other arithmetic, cells_to_rows(): jnp.sum(jnp.where(offsets[:, :, None] == columns, values[:, :, None], 0.0...  66.8 us
    ppermute x22, starting transfers between devices, with_halo(): lax.ppermute(lax.slice_in_dim(block, 0, width, axis=dim), axis, backward)  43.4 us
    ppermute x22, waiting for transfers between devices, with_halo(): lax.ppermute(lax.slice_in_dim(block, 0, width, axis=dim), axis, backward)  42.2 us
    reduce_sum x16, other arithmetic, rows_to_cells(): jnp.sum(jnp.where(offsets[:, :, None] == columns, rows[:, None, :], 0.0),...  41.2 us
    ppermute x22, waiting for transfers between devices, with_halo(): lax.ppermute(lax.slice_in_dim(block, block.shape[dim] - width, None, axis...  38.6 us
    all_to_all x2, blocking collectives, send_back(): lax.all_to_all(pack(to_rows(values)), ('lat', 'lon'), split_axis=0, conca...  36.8 us
    ppermute x22, starting transfers between devices, with_halo(): lax.ppermute(lax.slice_in_dim(block, block.shape[dim] - width, None, axis...  31.4 us
  transfers between devices with their start and end apart: 48, of which 26 were waited for; matrix products, arithmetic and copies ran while one was open for 5% of the time, Pallas kernels for 0%

commit v1 on v0

v1 whole, which is shorter than its diff:
```python
import functools

import jax
import jax.numpy as jnp
from jax import lax
from jax.experimental import pallas as pl
from jax.experimental.pallas import tpu as pltpu
from jax.sharding import PartitionSpec as P

PASSES = 8
RIM = 4 * PASSES
LANES = 128
SUB = 8
GROUP = 8
LOW = 32
AXES = ("lat", "lon")
F32 = jnp.float32
BF16 = jnp.bfloat16


def iota(shape, dim):
    return lax.broadcasted_iota(jnp.int32, shape, dim)


def call(kernel, outs, args, scratch=(), smem=(), flops=1000, nbytes=100000):
    vmem = pl.BlockSpec(memory_space=pltpu.VMEM)
    smem_spec = pl.BlockSpec(memory_space=pltpu.SMEM)
    return pl.pallas_call(
        kernel,
        out_shape=[jax.ShapeDtypeStruct(shape, dtype) for shape, dtype in outs],
        in_specs=[smem_spec if index in smem else vmem for index in range(len(args))],
        out_specs=[vmem] * len(outs),
        scratch_shapes=list(scratch),
        cost_estimate=pl.CostEstimate(flops=flops, bytes_accessed=nbytes, transcendentals=0),
    )(*args)


def split(value):
    high = value.astype(BF16)
    low = (value - high.astype(F32)).astype(BF16)
    return high, low


def contract(left, right, dims):
    return lax.dot_general(left, right, (dims, ((), ())), preferred_element_type=F32)


def swap_blocks(x, sub, lane):
    block = lane // LOW
    own = sub % 4
    up = pltpu.roll(pltpu.roll(x, SUB - 1, 0), LOW, 1)
    down = pltpu.roll(pltpu.roll(x, 1, 0), LANES - LOW, 1)
    odd_row, odd_block = own % 2, block % 2
    x = jnp.where(odd_row == odd_block, x, jnp.where(odd_row == 0, up, down))
    turned = pltpu.roll(x, 2 * LOW, 1)
    up = pltpu.roll(turned, SUB - 2, 0)
    down = pltpu.roll(turned, 2, 0)
    high_row, high_block = own // 2, block // 2
    return jnp.where(high_row == high_block, x, jnp.where(high_row == 0, up, down))


def route_kernel(devices, capacity, owner_ref, rid_ref, me_ref, inn_ref, var_ref, off_ref, send_ref, slot_ref, rows_ref):
    tiles = off_ref.shape[0]
    per_row = LANES // capacity
    hits = (owner_ref[...] == iota((tiles, LANES), 1)).astype(F32)
    earlier = (iota((tiles, tiles), 1) < iota((tiles, tiles), 0)).astype(BF16)
    before = jnp.dot(earlier, hits.astype(BF16), preferred_element_type=F32)
    rank = jnp.sum(hits * before, axis=1, keepdims=True)
    slot = owner_ref[...].astype(F32) * capacity + rank
    slot_wide = jnp.broadcast_to(slot, (tiles, LANES))
    slot_ref[...] = slot_wide
    slot_row = jnp.transpose(slot_wide)[0:1, :].astype(jnp.int32)
    shift = (me_ref[0] % per_row) * capacity
    rank_hot = (rank.astype(jnp.int32) + shift == iota((tiles, LANES), 1)).astype(BF16)
    marked = jnp.transpose(hits) * (rid_ref[...].astype(F32) + 1.0)
    ids = jnp.dot(marked.astype(BF16), rank_hot, preferred_element_type=F32)
    spare = send_ref.shape[1] - 2 * capacity
    pad_row = iota((devices, spare, LANES), 1)
    send_ref[:, 2 * capacity :, :] = jnp.where(
        pad_row == 0, jnp.broadcast_to(ids[0:devices][:, None, :], (devices, spare, LANES)), 0.0
    )

    sub = iota((SUB, LANES), 0)
    lane = iota((SUB, LANES), 1)
    tall = iota((LOW, LANES), 0)

    def expand(index, carry):
        start = pl.multiple_of(index * GROUP, GROUP)
        window = pl.ds(start, GROUP)
        offsets = off_ref[window, :]
        weight = var_ref[window, :]
        value = weight * inn_ref[window, :]
        low = offsets % LOW
        high = offsets // LOW
        hot, parts = [], []
        for tile in range(GROUP):
            pick = slice(tile, tile + 1)
            hot.append((low[pick, :] == tall).astype(F32).astype(BF16))
            both = jnp.where(sub < 4, value[pick, :], weight[pick, :])
            parts.append(jnp.where(high[pick, :] == sub % 4, both, 0.0))
        upper, lower = split(jnp.concatenate(parts, 0))
        product = contract(jnp.concatenate([upper, lower], 0), jnp.concatenate(hot, 0), ((1,), (1,)))
        half = GROUP * SUB
        total = product[:half] + product[half:]
        quads = []
        for side in range(2):
            lanes = slice(side * LANES, (side + 1) * LANES)
            merged = total[side * 4 * SUB : (side * 4 + 1) * SUB, lanes]
            for tile in range(1, 4):
                base = (side * 4 + tile) * SUB
                merged = jnp.where(lane // LOW == tile, total[base : base + SUB, lanes], merged)
            quads.append(swap_blocks(merged, sub, lane))
        first, second = quads
        rows_ref[window, 0:LANES] = jnp.where(sub < 4, first, pltpu.roll(second, 4, 0))
        rows_ref[window, LANES : 2 * LANES] = jnp.where(sub < 4, pltpu.roll(first, 4, 0), second)
        return carry

    lax.fori_loop(0, tiles // GROUP, expand, 0, unroll=2)
    upper, lower = split(rows_ref[...])
    for block in range(devices * capacity // LANES):
        place = (iota((LANES, tiles), 0) + block * LANES == slot_row).astype(F32).astype(BF16)
        packed = jnp.dot(place, upper, preferred_element_type=F32) + jnp.dot(
            place, lower, preferred_element_type=F32
        )
        owners = slice(block * per_row, (block + 1) * per_row)
        send_ref[owners, 0:capacity, :] = packed[:, 0:LANES].reshape(per_row, capacity, LANES)
        send_ref[owners, capacity : 2 * capacity, :] = packed[:, LANES:].reshape(per_row, capacity, LANES)


def collect_kernel(capacity, got_ref, low_ref, high_ref, ids_ref):
    devices = got_ref.shape[0]
    per_row = LANES // capacity
    rows = 2 * low_ref.shape[1]
    total = jnp.zeros((rows, 2 * LANES), F32)
    tall = iota((rows, LANES), 0) + 1
    for block in range(devices // per_row):
        owners = slice(block * per_row, (block + 1) * per_row)
        ids = jnp.sum(got_ref[owners, 2 * capacity : 2 * capacity + SUB, :], axis=0)[0:1, :]
        ids_ref[block : block + 1, :] = ids
        hot = (ids.astype(jnp.int32) == tall).astype(F32).astype(BF16)
        values = jnp.concatenate(
            [
                got_ref[owners, 0:capacity, :].reshape(LANES, LANES),
                got_ref[owners, capacity : 2 * capacity, :].reshape(LANES, LANES),
            ],
            1,
        )
        upper, lower = split(values)
        total = total + contract(
            jnp.concatenate([hot, hot], 1), jnp.concatenate([upper, lower], 0), ((1,), (0,))
        )
    half = rows // 2
    for plane in range(2):
        lanes = slice(plane * LANES, (plane + 1) * LANES)
        low_ref[plane] = total[0:half, lanes]
        high_ref[plane] = total[half:, lanes]


def faces_kernel(last_ref, lat_ref, lon_ref, std_ref, mask_ref, low_ref, high_ref):
    fields, rows, cols = lat_ref.shape
    half = rows // 2
    mask = mask_ref[...].astype(F32)
    edge = (iota((rows, cols), 0) == rows - 1) & (last_ref[0] == 1)
    for field in range(fields):
        planes = (jnp.where(edge, 0.0, lat_ref[field]), lon_ref[field], mask * std_ref[field])
        for kind, plane in enumerate(planes):
            low_ref[kind * fields + field] = plane[0:half]
            high_ref[kind * fields + field] = plane[half:]


def turn_kernel(low_ref, high_ref, south_ref, north_ref, mid_ref, first_ref, last_ref):
    for plane in range(low_ref.shape[0]):
        tall = jnp.concatenate([south_ref[plane], low_ref[plane], high_ref[plane], north_ref[plane]], 0)
        turned = jnp.transpose(tall)
        mid_ref[plane] = turned
        first_ref[plane] = turned[0:RIM]
        last_ref[plane] = turned[turned.shape[0] - RIM :]


def weave_kernel(fields, mid_ref, west_ref, east_ref, north_ref, east_face_ref, scale_ref):
    cols = mid_ref.shape[1]
    span = cols // 2 + RIM
    for kind, target in enumerate((north_ref, east_face_ref, scale_ref)):
        for field in range(fields):
            plane = kind * fields + field
            target[pl.ds(field, RIM, stride=SUB), :] = west_ref[plane]
            target[pl.ds(RIM * SUB + field, span, stride=SUB), :] = mid_ref[plane, 0:span, :]
            target[pl.ds(fields + field, span, stride=SUB), :] = mid_ref[plane, cols - span : cols, :]
            target[pl.ds(span * SUB + fields + field, RIM, stride=SUB), :] = east_ref[plane]


def solve_kernel(
    fields,
    north_ref,
    east_ref,
    scale_ref,
    mid_ref,
    west_ref,
    far_ref,
    lam_ref,
    image_ref,
    image_next_ref,
    seen_ref,
    seen_next_ref,
    parts_ref,
    u_ref,
    grid_ref,
    rhs_ref,
    turn_ref,
    t_ref,
):
    cols = mid_ref.shape[1]
    half = cols // 2
    length = half + 2 * RIM
    lam = lam_ref[...]
    sub = iota((SUB, LANES), 0)
    lane = iota((SUB, LANES), 1)
    inner = ((lane >= RIM) & (lane < LANES - RIM)).astype(F32)
    for plane in range(2):
        grid_ref[plane, 0:RIM, :] = west_ref[plane]
        grid_ref[plane, RIM : RIM + cols, :] = mid_ref[plane]
        grid_ref[plane, RIM + cols :, :] = far_ref[plane]

    def at(j):
        return slice(j * SUB, (j + 1) * SUB)

    def grid(plane, j):
        return jnp.where(
            sub < fields, grid_ref[plane, j : j + 1, :], grid_ref[plane, half + j : half + j + 1, :]
        )

    def group_sum(x):
        odd = sub % 2
        x = x + jnp.where(odd == 0, pltpu.roll(x, SUB - 1, 0), pltpu.roll(x, 1, 0))
        top = (sub // 2) % 2
        return x + jnp.where(top == 0, pltpu.roll(x, SUB - 2, 0), pltpu.roll(x, 2, 0))

    def diffuse(edge):
        def one_pass(index, carry):
            low, high = edge + 1, length - edge - 1
            here = u_ref[at(low), :]
            flux = east_ref[at(low - 1), :] * (here - u_ref[at(low - 1), :])
            for j in range(low, high):
                ahead = u_ref[at(j + 1), :]
                flux_next = east_ref[at(j), :] * (ahead - here)
                rise = north_ref[at(j), :] * (pltpu.roll(here, LANES - 1, 1) - here)
                u_ref[at(j), :] = here + ((flux_next - flux) + (rise - pltpu.roll(rise, 1, 1)))
                flux, here = flux_next, ahead
            return carry

        lax.fori_loop(0, PASSES, one_pass, 0)

    first, last = RIM, length - RIM
    for j in range(length):
        u_ref[at(j), :] = lam * scale_ref[at(j), :] * grid(0, j)
    diffuse(0)
    for j in range(first, last):
        rhs_ref[at(j - first), :] = u_ref[at(j), :]
    diffuse(PASSES)
    for j in range(2 * PASSES, length - 2 * PASSES):
        image = scale_ref[at(j), :] * u_ref[at(j), :]
        seen = group_sum(lam * image)
        if first <= j < last:
            image_ref[at(j - first), :] = image
            t_ref[0, at(j - first), :] = seen
        u_ref[at(j), :] = lam * scale_ref[at(j), :] * (grid(1, j) * seen)
    diffuse(2 * PASSES)
    zero = jnp.zeros((SUB, LANES), F32)
    sum_bb, sum_bw = zero, zero
    for j in range(first, last):
        rhs = rhs_ref[at(j - first), :]
        turn = u_ref[at(j), :]
        turn_ref[at(j - first), :] = turn
        sum_bb = sum_bb + rhs * rhs
        sum_bw = sum_bw + rhs * turn
    diffuse(3 * PASSES)
    sum_00, sum_01 = zero, zero
    for j in range(first, last):
        image = scale_ref[at(j), :] * u_ref[at(j), :]
        image_next_ref[at(j - first), :] = image
        seen_next = group_sum(lam * image)
        t_ref[1, at(j - first), :] = seen_next
        seen = t_ref[0, at(j - first), :]
        weighted = grid(1, j) * seen
        sum_00 = sum_00 + weighted * seen
        sum_01 = sum_01 + weighted * seen_next

    def whole(x):
        return jnp.sum(jnp.sum(x * inner, axis=1, keepdims=True), axis=0, keepdims=True)

    def ratio(top, bottom):
        return jnp.where(bottom > 0, top / jnp.where(bottom > 0, bottom, 1.0), 0.0)

    one_of = (sub % fields == 0).astype(F32)
    bb, bw = whole(sum_bb), whole(sum_bw)
    s00, s01 = whole(sum_00 * one_of), whole(sum_01 * one_of)
    fit, seen_fit = ratio(bw, bb), ratio(s01, s00)
    rest, seen_rest = zero, zero
    for j in range(first, last):
        left = turn_ref[at(j - first), :] - fit * rhs_ref[at(j - first), :]
        rest = rest + left * left
        left = t_ref[1, at(j - first), :] - seen_fit * t_ref[0, at(j - first), :]
        seen_rest = seen_rest + grid(1, j) * (left * left)
    rest, seen_rest = whole(rest), whole(seen_rest * one_of)
    wide = iota(parts_ref.shape, 1)
    parts = jnp.zeros(parts_ref.shape, F32)
    for position, number in enumerate((bb, bw, fit, rest, s00, seen_fit, seen_rest)):
        parts = jnp.where(wide == position, number, parts)
    parts_ref[...] = parts
    for plane, target in enumerate((seen_ref, seen_next_ref)):
        flat = jnp.concatenate(
            [
                t_ref[plane, pl.ds(0, half, stride=SUB), :],
                t_ref[plane, pl.ds(fields, half, stride=SUB), :],
            ],
            0,
        )
        target[...] = jnp.transpose(flat)[RIM : LANES - RIM, :]


def answer_kernel(parts_ref, seen_ref, seen_next_ref, ids_ref, back_ref, coef_ref):
    rows = seen_ref.shape[0]

    def column(index):
        return parts_ref[:, index : index + 1]

    def add(x):
        return jnp.sum(x, axis=0, keepdims=True)

    bb_each, fit_each, s00_each, seen_fit_each = column(0), column(2), column(4), column(5)
    bb, bw = add(bb_each), add(column(1))
    fit = bw / bb
    step = bb / (bb + bw)
    gap = fit_each - fit
    rest = add(column(3) + gap * (gap * bb_each))
    tilt = step * rest / bb
    full = fit + tilt
    gap = seen_fit_each - full
    energy = rest + tilt * tilt * bb + add(column(6) + gap * (gap * s00_each))
    step_next = jnp.where(rest > 0, rest / jnp.where(rest > 0, energy, 1.0), 0.0)
    coef = step * (1.0 + step_next * full)
    coef_next = -step * step_next
    final = coef * seen_ref[...] + coef_next * seen_next_ref[...]
    line = iota(coef_ref.shape, 0)
    coef_ref[...] = jnp.where(line == 0, coef, coef_next)
    upper, lower = split(final)
    both = jnp.concatenate([upper, lower], 0)
    blocks = ids_ref.shape[0]
    ids = jnp.transpose(jnp.concatenate([ids_ref[...]] * (LANES // blocks), 0)).astype(jnp.int32)
    wide = iota((LANES, 2 * rows), 1) % rows + 1
    for block in range(blocks):
        hot = (ids[:, block : block + 1] == wide).astype(F32).astype(BF16)
        back_ref[block * LANES : (block + 1) * LANES, :] = jnp.dot(
            hot, both, preferred_element_type=F32
        )


def increment_kernel(fields, image_ref, image_next_ref, coef_ref, out_ref):
    half = image_ref.shape[0] // SUB
    coef, coef_next = coef_ref[0:1, :], coef_ref[1:2, :]
    for field in range(fields):
        parts = []
        for side in range(2):
            pick = pl.ds(side * fields + field, half, stride=SUB)
            parts.append(coef * image_ref[pick, :] + coef_next * image_next_ref[pick, :])
        out_ref[field] = jnp.transpose(jnp.concatenate(parts, 0))[RIM : LANES - RIM, :]


def depart_kernel(back_ref, slot_ref, off_ref, inn_ref, out_ref):
    slots = back_ref.shape[0]
    upper, lower = split(back_ref[...])
    for block in range(off_ref.shape[0] // LANES):
        window = slice(block * LANES, (block + 1) * LANES)
        slot = slot_ref[window, :].astype(jnp.int32)
        place = jnp.concatenate(
            [
                (slot == iota((LANES, LANES), 1) + part * LANES).astype(F32).astype(BF16)
                for part in range(slots // LANES)
            ],
            1,
        )
        rows = jnp.dot(place, upper, preferred_element_type=F32) + jnp.dot(
            place, lower, preferred_element_type=F32
        )
        seen = jnp.take_along_axis(rows, off_ref[window, :], axis=1)
        out_ref[window, :] = inn_ref[window, :] - seen


def neighbours(low, high, axis, periodic):
    count = lax.axis_size(axis)
    forward = [(i, i + 1) for i in range(count - 1)]
    if periodic:
        forward.append((count - 1, 0))
    backward = [(target, source) for source, target in forward]
    return lax.ppermute(high, axis, forward), lax.ppermute(low, axis, backward)


def exchange(low, high):
    planes = low.shape[0]
    south, north = neighbours(low, high, "lat", False)
    mid, first, last = call(
        turn_kernel,
        [((planes, LANES, LANES), F32), ((planes, RIM, LANES), F32), ((planes, RIM, LANES), F32)],
        (low, high, south, north),
        nbytes=4 * planes * 300 * LANES,
    )
    west, east = neighbours(first, last, "lon", True)
    return mid, west, east


def on_device(
    lat_coef, lon_coef, std_scale, land_mask, lst_weights, innovation, inv_var, owner, row_ids, offsets
):
    fields, tile_rows, tile_cols = lat_coef.shape
    tiles, width = innovation.shape
    lat_count, lon_count = lax.axis_size("lat"), lax.axis_size("lon")
    devices = lat_count * lon_count
    capacity = max(2, 2 * tiles // devices)
    if (2 * fields, tile_cols, width, tile_rows + 2 * RIM) != (SUB, LANES, LANES, LANES):
        raise ValueError("tile shape")
    if RIM > tile_rows // 2 or capacity % SUB or LANES % capacity or tiles % LANES:
        raise ValueError("slot shape")
    half = tile_rows // 2
    slots = devices * capacity
    last = (lax.axis_index("lat") == lat_count - 1).astype(jnp.int32).reshape(1)
    me = (lax.axis_index("lat") * lon_count + lax.axis_index("lon")).astype(jnp.int32).reshape(1)

    face_low, face_high = call(
        faces_kernel,
        [((3 * fields, half, LANES), F32)] * 2,
        (last, lat_coef, lon_coef, std_scale, land_mask),
        smem=(0,),
    )
    block = 2 * capacity + SUB
    send, slot = call(
        functools.partial(route_kernel, devices, capacity),
        [((devices, block, LANES), F32), ((tiles, LANES), F32)],
        (owner, row_ids.reshape(1, tiles), me, innovation, inv_var, offsets),
        scratch=(pltpu.VMEM((tiles, 2 * LANES), F32),),
        smem=(2,),
        flops=10**9,
        nbytes=10**7,
    )
    face_mid, face_west, face_east = exchange(face_low, face_high)
    got = lax.all_to_all(send, AXES, split_axis=0, concat_axis=0, tiled=True)
    span = tile_cols // 2 + 2 * RIM
    north8, east8, scale8 = call(
        functools.partial(weave_kernel, fields),
        [((span * SUB, LANES), F32)] * 3,
        (face_mid, face_west, face_east),
        nbytes=3 * 10**6,
    )
    low, high, ids = call(
        functools.partial(collect_kernel, capacity),
        [((2, half, LANES), F32)] * 2 + [((slots // LANES, LANES), F32)],
        (got,),
    )
    mid, west, east = exchange(low, high)
    lam = jnp.broadcast_to(jnp.concatenate([lst_weights, lst_weights])[:, None], (SUB, LANES))
    inner = (tile_cols // 2 * SUB, LANES)
    image, image_next, seen, seen_next, parts = call(
        functools.partial(solve_kernel, fields),
        [(inner, F32)] * 2 + [((tile_rows, LANES), F32)] * 2 + [((devices, LANES), F32)],
        (north8, east8, scale8, mid, west, east, lam),
        scratch=(
            pltpu.VMEM((span * SUB, LANES), F32),
            pltpu.VMEM((2, tile_cols + 2 * RIM, LANES), F32),
            pltpu.VMEM(inner, F32),
            pltpu.VMEM(inner, F32),
            pltpu.VMEM((2,) + inner, F32),
        ),
        flops=10**9,
        nbytes=10**7,
    )
    parts = lax.all_to_all(parts, AXES, split_axis=0, concat_axis=0, tiled=True)
    back, coef = call(
        answer_kernel,
        [((slots, LANES), F32), ((SUB, LANES), F32)],
        (parts, seen, seen_next, ids),
    )
    back = lax.all_to_all(
        back.reshape(devices, capacity, LANES), AXES, split_axis=0, concat_axis=0, tiled=True
    ).reshape(slots, LANES)
    (increment,) = call(
        functools.partial(increment_kernel, fields),
        [((fields, tile_rows, tile_cols), F32)],
        (image, image_next, coef),
        nbytes=10**6,
    )
    (departure,) = call(depart_kernel, [((tiles, width), F32)], (back, slot, offsets, innovation))
    return increment, departure


def solution(mesh):
    grid = P(None, "lat", "lon")
    tile = P(AXES, None)
    in_specs = (grid, grid, grid, P("lat", "lon"), P(), tile, tile, tile, P(AXES), tile)
    return jax.shard_map(on_device, mesh=mesh, in_specs=in_specs, out_specs=(grid, tile), check_vma=False)
```

time: 565 us -> 135 us (0.24); the launches traced: 555 us -> 134 us
  blocking collectives: 154 us -> 10.3 us
  other arithmetic: 143 us -> 0.07 us
  waiting for transfers between devices: 115 us -> 35.8 us
  starting transfers between devices: 94.7 us -> 32.4 us
  Pallas kernels: 0 us -> 48.1 us
  matrix products: 18.9 us -> 0 us
  local copies, waits for them, and re-layouts: 22.1 us -> 6.71 us
    psum x3 -> x0, blocking collectives: 117 us -> none  [total_sum(): return lax.psum(value, ('lat', 'lon'))]
    reduce_sum x45 -> x0, other arithmetic: 111 us -> none  [the longest x24 66.8 us: cells_to_rows(): jnp.sum(jnp.where(offsets[:, :, None] == columns, values[:, :, None], 0.0...]
    ppermute x44 -> x8, waiting for transfers between devices: 80.9 us -> 22 us  [the longest x4 17.9 us: neighbours(): lax.ppermute(high, axis, forward)]
    ppermute x44 -> x8, starting transfers between devices: 74.9 us -> 22.5 us  [the longest x4 14.6 us: neighbours(): lax.ppermute(high, axis, forward)]
    pallas_call x0 -> x10, Pallas kernels: none -> 48.1 us  [call(): pl.pallas_call(kernel, out_shape=[jax.ShapeDtypeStruct(shape, dtype) for...]
    all_to_all x2 -> x1, blocking collectives: 36.8 us -> 10.3 us  [on_device(): parts = lax.all_to_all(parts, AXES, split_axis=0, concat_axis=0, tiled=True)]
    sub x38 -> x0, other arithmetic: 21.7 us -> none  [the longest x36 21 us: pass_step(): centre + face_north * (north - centre) - face_south * (centre - south)]
    all_to_all x4 -> x2, waiting for transfers between devices: 34 us -> 13.8 us  [the longest x1 13.8 us: on_device(): lax.all_to_all(back.reshape(devices, capacity, LANES), AXES, split_axis=0...]
  transfers between devices with their start and end apart: 48 -> 10, of which waited for: 26 -> 4; matrix products, arithmetic and copies ran while one was open for 5% -> 0% of each run, Pallas kernels for 0% -> 9%
where the time goes in v1:
time: 135 us; the launch traced here: 134 us
  Pallas kernels  48.1 us (36%)
  waiting for transfers between devices  35.8 us (27%)
  starting transfers between devices  32.4 us (24%)
  blocking collectives  10.3 us (8%)
  local copies, waits for them, and re-layouts  6.71 us (5%)
    pallas_call x10, Pallas kernels, call(): pl.pallas_call(kernel, out_shape=[jax.ShapeDtypeStruct(shape, dtype) for...  48.1 us
    ppermute x4, waiting for transfers between devices, neighbours(): lax.ppermute(high, axis, forward)  17.9 us
    ppermute x4, starting transfers between devices, neighbours(): lax.ppermute(high, axis, forward)  14.6 us
    all_to_all x1, waiting for transfers between devices, on_device(): lax.all_to_all(back.reshape(devices, capacity, LANES), AXES, split_axis=0...  13.8 us
    all_to_all x1, blocking collectives, on_device(): parts = lax.all_to_all(parts, AXES, split_axis=0, concat_axis=0, tiled=True)  10.3 us
    ppermute x4, starting transfers between devices, neighbours(): lax.ppermute(low, axis, backward)  7.87 us
    all_to_all x1, starting transfers between devices, on_device(): got = lax.all_to_all(send, AXES, split_axis=0, concat_axis=0, tiled=True)  7.33 us
    unnamed x23, local copies, waits for them, and re-layouts  6.05 us
  transfers between devices with their start and end apart: 10, of which 4 were waited for; matrix products, arithmetic and copies ran while one was open for 0% of the time, Pallas kernels for 9%

profile of v1, /device:TPU:0, one launch (start us, length us, event | category | flops | bytes accessed | tf_op | source)
XLA Modules:
  0.0 134.1 jit_solution(8202422872631885162)
XLA Ops:
  0.6 1.5 %copy.13.owner_ref = s32[512,1]{1,0:T(8,128)} copy(s32[512,1]{0,1:T(1,128)} %param.17) | data formatting | bytes 4096 | tf_op args[7]
  2.2 15.0 %shard_map.116 = (f32[32,72,128]{2,1,0:T(8,128)}, f32[512,128]{1,0:T(8,128)}) custom-call(s32[512,1]{1,0:T(8,128)} %copy.13.owner_ref, s32[1,512]{1,0:T(1,128)} %bitcast.13, s32[1]{0:T(128)} %bitcast.2.me_ref, f32[512,128]{1,0:T(8,128)} %inn_ref.3, f32[512,128]{1,0:T(8,128)} %var_ref.1, s32[512,128]{1,0:T(8,128)} %off_ref.3), custom_call_target="tpu_custom_call" | custom-call | flops 1000000000 | bytes 10000000 | tf_op jit(solution)/shard_map/pallas_call | solution.py:28
  17.2 7.3 %all-to-all-start = ((f32[32,72,128]{2,1,0:T(8,128)}), f32[32,72,128]{2,1,0:T(8,128)S(1)}, u32[]{:S(2)}, u32[]{:S(2)}) async-start(f32[32,72,128]{2,1,0:T(8,128)} %get-tuple-element.33), calls=%async_computation | async-start | bytes 2359296 | tf_op jit(solution)/shard_map/all_to_all | solution.py:445
  24.5 0.0 copy-start.10
  24.6 1.8 %shard_map.113 = (f32[12,32,128]{2,1,0:T(8,128)}, f32[12,32,128]{2,1,0:T(8,128)}) custom-call(s32[1]{0:T(128)} %bitcast.last_ref, f32[4,64,128]{2,1,0:T(8,128)} %lat_ref.1, f32[4,64,128]{2,1,0:T(8,128)} %lon_ref.1, f32[4,64,128]{2,1,0:T(8,128)} %std_ref.1, s32[64,128]{1,0:T(8,128)} %mask_ref.1), custom_call_target="tpu_custom_call" | custom-call | flops 1000 | bytes 100000 | tf_op jit(solution)/shard_map/pallas_call | solution.py:28
  26.4 3.7 %collective-permute-start = (f32[12,32,128]{2,1,0:T(8,128)}, f32[12,32,128]{2,1,0:T(8,128)S(1)}, u32[]{:S(2)}, u32[]{:S(2)}) collective-permute-start(f32[12,32,128]{2,1,0:T(8,128)} %get-tuple-element.26.high_ref), channel_id=1, source_target_pairs={{0,8},{8,16},{16,24},{1,9},{9,17},{17,25},{2,10},{10,18},{18,26},{... | collective-permute-start | bytes 589832 | tf_op jit(solution)/shard_map/ppermute | solution.py:395
  30.1 1.3 collective-permute-start.1
  31.4 17.3 %collective-permute-done.south_ref = f32[12,32,128]{2,1,0:T(8,128)S(1)} collective-permute-done((f32[12,32,128]{2,1,0:T(8,128)}, f32[12,32,128]{2,1,0:T(8,128)S(1)}, u32[]{:S(2)}, u32[]{:S(2)}) %collective-permute-start) | collective-permute-done | bytes 196640 | tf_op jit(solution)/shard_map/ppermute | solution.py:395
  48.6 0.0 copy-start.4
  48.6 0.0 collective-permute-done.1.north_ref
  48.6 0.7 copy-done.4
  49.3 0.0 copy-start.5
  49.3 0.7 copy-done.5
  49.9 2.5 %shard_map.114 = (f32[12,128,128]{2,1,0:T(8,128)}, f32[12,32,128]{2,1,0:T(8,128)}, f32[12,32,128]{2,1,0:T(8,128)}) custom-call(f32[12,32,128]{2,1,0:T(8,128)} %get-tuple-element.25.low_ref, f32[12,32,128]{2,1,0:T(8,128)} %get-tuple-element.26.high_ref, f32[12,32,128]{2,1,0:T(8,128)} %copy-done.4, f32[12,32,128]{2,1,0:T(8,128)} %copy-done.5), custom_call_target="tpu_custom_call" | custom-call | flops 1000 | bytes 1843200 | tf_op jit(solution)/shard_map/pallas_call | solution.py:28
  52.4 0.0 collective-permute-start.2
  52.5 2.6 %collective-permute-start.3 = (f32[12,32,128]{2,1,0:T(8,128)}, f32[12,32,128]{2,1,0:T(8,128)S(1)}, u32[]{:S(2)}, u32[]{:S(2)}) collective-permute-start(f32[12,32,128]{2,1,0:T(8,128)} %get-tuple-element.29), channel_id=1, source_target_pairs={{1,0},{2,1},{3,2},{4,3},{5,4},{6,5},{7,6},{0,7},{9,8},{10,9},{11,1... | collective-permute-start | bytes 589832 | tf_op jit(solution)/shard_map/ppermute | solution.py:395
  55.1 0.0 all-to-all-done.got_ref
  55.1 0.0 copy-start
  55.1 1.0 copy-done
  56.1 2.2 %shard_map.117 = (f32[2,32,128]{2,1,0:T(8,128)}, f32[2,32,128]{2,1,0:T(8,128)}, f32[8,128]{1,0:T(8,128)}) custom-call(f32[32,72,128]{2,1,0:T(8,128)} %copy-done), custom_call_target="tpu_custom_call" | custom-call | flops 1000 | bytes 100000 | tf_op jit(solution)/shard_map/pallas_call | solution.py:28
  58.3 10.9 %collective-permute-start.4 = (f32[2,32,128]{2,1,0:T(8,128)}, f32[2,32,128]{2,1,0:T(8,128)S(1)}, u32[]{:S(2)}, u32[]{:S(2)}) collective-permute-start(f32[2,32,128]{2,1,0:T(8,128)} %get-tuple-element.35.high_ref), channel_id=1, source_target_pairs={{0,8},{8,16},{16,24},{1,9},{9,17},{17,25},{2,10},{10,18},{18,26},{... | collective-permute-start | bytes 98312 | tf_op jit(solution)/shard_map/ppermute | solution.py:395
  69.3 1.3 collective-permute-start.5
  70.6 0.6 collective-permute-done.4.south_ref
  71.2 0.0 copy-start.6
  71.2 4.1 %collective-permute-done.5.north_ref = f32[2,32,128]{2,1,0:T(8,128)S(1)} collective-permute-done((f32[2,32,128]{2,1,0:T(8,128)}, f32[2,32,128]{2,1,0:T(8,128)S(1)}, u32[]{:S(2)}, u32[]{:S(2)}) %collective-permute-start.5) | collective-permute-done | bytes 32800 | tf_op jit(solution)/shard_map/ppermute | solution.py:395
  75.3 0.0 copy-done.6
  75.3 0.0 copy-start.7
  75.3 0.6 copy-done.7
  75.9 1.6 %shard_map.118 = (f32[2,128,128]{2,1,0:T(8,128)}, f32[2,32,128]{2,1,0:T(8,128)}, f32[2,32,128]{2,1,0:T(8,128)}) custom-call(f32[2,32,128]{2,1,0:T(8,128)} %get-tuple-element.34.low_ref, f32[2,32,128]{2,1,0:T(8,128)} %get-tuple-element.35.high_ref, f32[2,32,128]{2,1,0:T(8,128)} %copy-done.6, f32[2,32,128]{2,1,0:T(8,128)} %copy-done.7), custom_call_target="tpu_custom_call" | custom-call | flops 1000 | bytes 307200 | tf_op jit(solution)/shard_map/pallas_call | solution.py:28
  77.5 0.0 collective-permute-start.6
  77.5 2.6 %collective-permute-start.7 = (f32[2,32,128]{2,1,0:T(8,128)}, f32[2,32,128]{2,1,0:T(8,128)S(1)}, u32[]{:S(2)}, u32[]{:S(2)}) collective-permute-start(f32[2,32,128]{2,1,0:T(8,128)} %get-tuple-element.38), channel_id=1, source_target_pairs={{1,0},{2,1},{3,2},{4,3},{5,4},{6,5},{7,6},{0,7},{9,8},{10,9},{11,1... | collective-permute-start | bytes 98312 | tf_op jit(solution)/shard_map/ppermute | solution.py:395
  80.1 0.0 copy-done.10
  80.1 0.1 pad_maximum_fusion
  80.2 0.0 collective-permute-done.2.west_ref
  80.2 0.0 copy-start.2
  80.2 0.0 collective-permute-done.3.east_ref
  80.2 0.0 copy-start.3
  80.2 0.7 copy-done.2
  80.9 0.1 copy-done.3
  80.9 2.6 %shard_map.115 = (f32[1024,128]{1,0:T(8,128)}, f32[1024,128]{1,0:T(8,128)}, f32[1024,128]{1,0:T(8,128)}) custom-call(f32[12,128,128]{2,1,0:T(8,128)} %get-tuple-element.27.mid_ref, f32[12,32,128]{2,1,0:T(8,128)} %copy-done.2, f32[12,32,128]{2,1,0:T(8,128)} %copy-done.3), custom_call_target="tpu_custom_call" | custom-call | flops 1000 | bytes 3000000 | tf_op jit(solution)/shard_map/pallas_call | solution.py:28
  83.5 0.0 collective-permute-done.6.west_ref
  83.5 0.0 copy-start.8
  83.5 0.0 collective-permute-done.7.far_ref
  83.5 0.0 copy-start.9
  83.5 0.7 broadcast_in_dim.2.lam_ref
  84.2 0.0 copy-done.8
  84.2 0.0 copy-done.9
  84.2 15.1 %shard_map.119 = (f32[512,128]{1,0:T(8,128)}, f32[512,128]{1,0:T(8,128)}, f32[64,128]{1,0:T(8,128)}, f32[64,128]{1,0:T(8,128)}, f32[32,128]{1,0:T(8,128)}) custom-call(f32[1024,128]{1,0:T(8,128)} %get-tuple-element.30.north_ref, f32[1024,128]{1,0:T(8,128)} %get-tuple-element.31.east_ref, f32[1024,128]{1,0:T(8,128)} %get-tuple-element.32.scale_ref, ...), custom_call_target="tpu_custom_call" | custom-call | flops 1000000000 | bytes 10000000 | tf_op jit(solution)/shard_map/pallas_call | solution.py:28
  99.4 10.3 %all_to_all.21 = f32[32,1,128]{2,1,0:T(1,128)} all-to-all(f32[32,1,128]{2,1,0:T(1,128)} %bitcast.12), channel_id=1, replica_groups=mesh['lat'=4,'lon'=8] {'lat','lon'}, dimensions={0} | all-to-all | bytes 32768 | tf_op jit(solution)/shard_map/all_to_all | solution.py:475
  109.7 2.6 %shard_map.120 = (f32[1024,128]{1,0:T(8,128)}, f32[8,128]{1,0:T(8,128)}) custom-call(f32[32,128]{1,0:T(8,128)} %bitcast.11, f32[64,128]{1,0:T(8,128)} %get-tuple-element.42.seen_ref, f32[64,128]{1,0:T(8,128)} %get-tuple-element.43.seen_next_ref, f32[8,128]{1,0:T(8,128)} %get-tuple-element.44.ids_ref), custom_call_target="tpu_custom_call" | custom-call | flops 1000 | bytes 100000 | tf_op jit(solution)/shard_map/pallas_call | solution.py:28
  112.3 2.6 %all-to-all-start.2 = ((f32[32,32,128]{2,1,0:T(8,128)}), f32[32,32,128]{2,1,0:T(8,128)S(1)}, u32[]{:S(2)}, u32[]{:S(2)}) async-start(f32[32,32,128]{2,1,0:T(8,128)} %bitcast.10), calls=%async_computation.2 | async-start | bytes 1048576 | tf_op jit(solution)/shard_map/all_to_all | solution.py:481
  114.9 1.8 %shard_map.121 = f32[4,64,128]{2,1,0:T(8,128)} custom-call(f32[512,128]{1,0:T(8,128)} %get-tuple-element.39.image_ref, f32[512,128]{1,0:T(8,128)} %get-tuple-element.40.image_next_ref, f32[8,128]{1,0:T(8,128)} %get-tuple-element.45.coef_ref), custom_call_target="tpu_custom_call" | custom-call | flops 1000 | bytes 1000000 | tf_op jit(solution)/shard_map/pallas_call | solution.py:28
  116.7 13.8 %all-to-all-done.2 = f32[32,32,128]{2,1,0:T(8,128)S(1)} async-done(((f32[32,32,128]{2,1,0:T(8,128)}), f32[32,32,128]{2,1,0:T(8,128)S(1)}, u32[]{:S(2)}, u32[]{:S(2)}) %all-to-all-start.2) | async-done | bytes 524320 | tf_op jit(solution)/shard_map/all_to_all | solution.py:481
  130.5 0.0 copy-start.1
  130.5 0.8 copy-done.1
  131.3 2.8 %shard_map.122 = f32[512,128]{1,0:T(8,128)} custom-call(f32[1024,128]{1,0:T(8,128)} %bitcast.9, f32[512,128]{1,0:T(8,128)} %get-tuple-element.47.slot_ref, s32[512,128]{1,0:T(8,128)} %off_ref.3, f32[512,128]{1,0:T(8,128)} %inn_ref.3), custom_call_target="tpu_custom_call" | custom-call | flops 1000 | bytes 100000 | tf_op jit(solution)/shard_map/pallas_call | solution.py:28
Async XLA Ops:
  17.2 37.9 %all-to-all-start = ((f32[32,72,128]{2,1,0:T(8,128)}), f32[32,72,128]{2,1,0:T(8,128)S(1)}, u32[]{:S(2)}, u32[]{:S(2)}) async-start(f32[32,72,128]{2,1,0:T(8,128)} %get-tuple-element.33), calls=%async_computation | async-start | bytes 2359296 | tf_op jit(solution)/shard_map/all_to_all | solution.py:445
  24.5 55.6 %copy-start.10 = (f32[4]{0:T(128)S(1)}, f32[4]{0:T(128)}, u32[]{:S(2)}) copy-start(f32[4]{0:T(128)} %param.14) | copy-start | bytes 52
  26.4 22.2 %collective-permute-start = (f32[12,32,128]{2,1,0:T(8,128)}, f32[12,32,128]{2,1,0:T(8,128)S(1)}, u32[]{:S(2)}, u32[]{:S(2)}) collective-permute-start(f32[12,32,128]{2,1,0:T(8,128)} %get-tuple-element.26.high_ref), channel_id=1, source_target_pairs={{0,8},{8,16},{16,24},{1,9},{9,17},{17,25},{2,10},{10,18},{18,26},{... | collective-permute-start | bytes 589832 | tf_op jit(solution)/shard_map/ppermute | solution.py:395
  30.1 18.6 %collective-permute-start.1 = (f32[12,32,128]{2,1,0:T(8,128)}, f32[12,32,128]{2,1,0:T(8,128)S(1)}, u32[]{:S(2)}, u32[]{:S(2)}) collective-permute-start(f32[12,32,128]{2,1,0:T(8,128)} %get-tuple-element.25.low_ref), channel_id=1, source_target_pairs={{8,0},{16,8},{24,16},{9,1},{17,9},{25,17},{10,2},{18,10},{26,18},{... | collective-permute-start | bytes 589832 | tf_op jit(solution)/shard_map/ppermute | solution.py:395
  48.6 0.7 copy-start.4
  49.3 0.7 copy-start.5
  52.4 27.7 %collective-permute-start.2 = (f32[12,32,128]{2,1,0:T(8,128)}, f32[12,32,128]{2,1,0:T(8,128)S(1)}, u32[]{:S(2)}, u32[]{:S(2)}) collective-permute-start(f32[12,32,128]{2,1,0:T(8,128)} %get-tuple-element.28), channel_id=1, source_target_pairs={{0,1},{1,2},{2,3},{3,4},{4,5},{5,6},{6,7},{7,0},{8,9},{9,10},{10,1... | collective-permute-start | bytes 589832 | tf_op jit(solution)/shard_map/ppermute | solution.py:395
  52.5 27.7 %collective-permute-start.3 = (f32[12,32,128]{2,1,0:T(8,128)}, f32[12,32,128]{2,1,0:T(8,128)S(1)}, u32[]{:S(2)}, u32[]{:S(2)}) collective-permute-start(f32[12,32,128]{2,1,0:T(8,128)} %get-tuple-element.29), channel_id=1, source_target_pairs={{1,0},{2,1},{3,2},{4,3},{5,4},{6,5},{7,6},{0,7},{9,8},{10,9},{11,1... | collective-permute-start | bytes 589832 | tf_op jit(solution)/shard_map/ppermute | solution.py:395
  55.1 1.0 copy-start
  58.3 12.8 %collective-permute-start.4 = (f32[2,32,128]{2,1,0:T(8,128)}, f32[2,32,128]{2,1,0:T(8,128)S(1)}, u32[]{:S(2)}, u32[]{:S(2)}) collective-permute-start(f32[2,32,128]{2,1,0:T(8,128)} %get-tuple-element.35.high_ref), channel_id=1, source_target_pairs={{0,8},{8,16},{16,24},{1,9},{9,17},{17,25},{2,10},{10,18},{18,26},{... | collective-permute-start | bytes 98312 | tf_op jit(solution)/shard_map/ppermute | solution.py:395
  69.3 6.0 %collective-permute-start.5 = (f32[2,32,128]{2,1,0:T(8,128)}, f32[2,32,128]{2,1,0:T(8,128)S(1)}, u32[]{:S(2)}, u32[]{:S(2)}) collective-permute-start(f32[2,32,128]{2,1,0:T(8,128)} %get-tuple-element.34.low_ref), channel_id=1, source_target_pairs={{8,0},{16,8},{24,16},{9,1},{17,9},{25,17},{10,2},{18,10},{26,18},{... | collective-permute-start | bytes 98312 | tf_op jit(solution)/shard_map/ppermute | solution.py:395
  71.2 4.1 %copy-start.6 = (f32[2,32,128]{2,1,0:T(8,128)}, f32[2,32,128]{2,1,0:T(8,128)S(1)}, u32[]{:S(2)}) copy-start(f32[2,32,128]{2,1,0:T(8,128)S(1)} %collective-permute-done.4.south_ref) | copy-start | bytes 98308
  75.3 0.6 copy-start.7
  77.5 6.1 %collective-permute-start.6 = (f32[2,32,128]{2,1,0:T(8,128)}, f32[2,32,128]{2,1,0:T(8,128)S(1)}, u32[]{:S(2)}, u32[]{:S(2)}) collective-permute-start(f32[2,32,128]{2,1,0:T(8,128)} %get-tuple-element.37), channel_id=1, source_target_pairs={{0,1},{1,2},{2,3},{3,4},{4,5},{5,6},{6,7},{7,0},{8,9},{9,10},{10,1... | collective-permute-start | bytes 98312 | tf_op jit(solution)/shard_map/ppermute | solution.py:395
  77.5 6.1 %collective-permute-start.7 = (f32[2,32,128]{2,1,0:T(8,128)}, f32[2,32,128]{2,1,0:T(8,128)S(1)}, u32[]{:S(2)}, u32[]{:S(2)}) collective-permute-start(f32[2,32,128]{2,1,0:T(8,128)} %get-tuple-element.38), channel_id=1, source_target_pairs={{1,0},{2,1},{3,2},{4,3},{5,4},{6,5},{7,6},{0,7},{9,8},{10,9},{11,1... | collective-permute-start | bytes 98312 | tf_op jit(solution)/shard_map/ppermute | solution.py:395
  80.2 0.7 copy-start.2
  80.2 0.7 copy-start.3
  83.5 0.7 copy-start.8
  83.5 0.7 copy-start.9
  112.3 18.2 %all-to-all-start.2 = ((f32[32,32,128]{2,1,0:T(8,128)}), f32[32,32,128]{2,1,0:T(8,128)S(1)}, u32[]{:S(2)}, u32[]{:S(2)}) async-start(f32[32,32,128]{2,1,0:T(8,128)} %bitcast.10), calls=%async_computation.2 | async-start | bytes 1048576 | tf_op jit(solution)/shard_map/all_to_all | solution.py:481
  130.5 0.8 copy-start.1

commit v2 on v1

v2 whole, which is shorter than its diff:
```python
import functools

import jax
import jax.numpy as jnp
from jax import lax
from jax.experimental import pallas as pl
from jax.experimental.pallas import tpu as pltpu
from jax.sharding import PartitionSpec as P

PASSES = 8
RIM = 4 * PASSES
LANES = 128
SUB = 8
GROUP = 8
STEP = 4
REACH = LANES // STEP
LOW_BITS = 5
LOW = 2**LOW_BITS
AXES = ("lat", "lon")
F32 = jnp.float32
BF16 = jnp.bfloat16


def iota(shape, dim):
    return lax.broadcasted_iota(jnp.int32, shape, dim)


def call(kernel, outs, args, scratch=(), smem=(), hbm=(), flops=1000, nbytes=100000):
    spaces = [pltpu.VMEM] * len(args)
    for index in smem:
        spaces[index] = pltpu.SMEM
    for index in hbm:
        spaces[index] = pltpu.HBM
    args = [
        pltpu.with_memory_space_constraint(arg, pltpu.HBM) if space == pltpu.HBM else arg
        for arg, space in zip(args, spaces)
    ]
    return pl.pallas_call(
        kernel,
        out_shape=[jax.ShapeDtypeStruct(shape, dtype) for shape, dtype in outs],
        in_specs=[pl.BlockSpec(memory_space=space) for space in spaces],
        out_specs=[pl.BlockSpec(memory_space=pltpu.VMEM)] * len(outs),
        scratch_shapes=list(scratch),
        compiler_params=pltpu.CompilerParams(vmem_limit_bytes=20 * 2**20),
        cost_estimate=pl.CostEstimate(flops=flops, bytes_accessed=nbytes, transcendentals=0),
    )(*args)


def fetch(sources, targets, sems):
    copies = [
        pltpu.make_async_copy(source, target, sems.at[index])
        for index, (source, target) in enumerate(zip(sources, targets))
    ]
    for copy in copies:
        copy.start()
    return copies


def split(value):
    high = value.astype(BF16)
    low = (value - high.astype(F32)).astype(BF16)
    return high, low


def contract(left, right, dims):
    return lax.dot_general(left, right, (dims, ((), ())), preferred_element_type=F32)


def swap_blocks(x, sub, lane):
    block = lane // LOW
    own = sub % 4
    up = pltpu.roll(pltpu.roll(x, SUB - 1, 0), LOW, 1)
    down = pltpu.roll(pltpu.roll(x, 1, 0), LANES - LOW, 1)
    odd_row, odd_block = own % 2, block % 2
    x = jnp.where(odd_row == odd_block, x, jnp.where(odd_row == 0, up, down))
    turned = pltpu.roll(x, 2 * LOW, 1)
    up = pltpu.roll(turned, SUB - 2, 0)
    down = pltpu.roll(turned, 2, 0)
    high_row, high_block = own // 2, block // 2
    return jnp.where(high_row == high_block, x, jnp.where(high_row == 0, up, down))


def route_kernel(devices, capacity, *refs):
    me_ref, sources = refs[0], refs[1:6]
    send_ref, slot_ref, rows_ref, packed_ref = refs[6:10]
    owner_ref, rid_ref, inn_ref, var_ref, off_ref = local = refs[10:15]
    copies = fetch(sources, local, refs[15])
    copies[0].wait()
    copies[1].wait()
    tiles = off_ref.shape[0]
    per_row = LANES // capacity
    hits = (owner_ref[...] == iota((devices, tiles), 0)).astype(F32)
    earlier = (iota((tiles, tiles), 0) < iota((tiles, tiles), 1)).astype(F32).astype(BF16)
    before = jnp.dot(hits.astype(BF16), earlier, preferred_element_type=F32)
    rank = jnp.sum(hits * before, axis=0, keepdims=True)
    slot_row = owner_ref[...] * capacity + rank.astype(jnp.int32)
    slot_ref[...] = jnp.transpose(jnp.broadcast_to(slot_row.astype(F32), (LANES, tiles)))
    shift = (me_ref[0] % per_row) * capacity
    rank_hot = (rank.astype(jnp.int32) + shift == iota((LANES, tiles), 0)).astype(F32).astype(BF16)
    marked = hits * (rid_ref[...].astype(F32) + 1.0)
    ids = contract(marked.astype(BF16), rank_hot, ((1,), (1,)))
    spare = send_ref.shape[1] - 2 * capacity
    pad_row = iota((devices, spare, LANES), 1)
    send_ref[:, 2 * capacity :, :] = jnp.where(
        pad_row == 0, jnp.broadcast_to(ids[:, None, :], (devices, spare, LANES)), 0.0
    )

    for copy in copies[2:]:
        copy.wait()
    sub = iota((SUB, LANES), 0)
    lane = iota((SUB, LANES), 1)
    tall = iota((LOW, LANES), 0)

    def expand(index, carry):
        start = pl.multiple_of(index * GROUP, GROUP)
        window = pl.ds(start, GROUP)
        offsets = off_ref[window, :]
        weight = var_ref[window, :]
        value = weight * inn_ref[window, :]
        low = offsets & (LOW - 1)
        high = offsets >> LOW_BITS
        hot, parts = [], []
        for tile in range(GROUP):
            pick = slice(tile, tile + 1)
            hot.append((low[pick, :] == tall).astype(F32).astype(BF16))
            both = jnp.where(sub < 4, value[pick, :], weight[pick, :])
            parts.append(jnp.where(high[pick, :] == sub % 4, both, 0.0))
        upper, lower = split(jnp.concatenate(parts, 0))
        product = contract(jnp.concatenate([upper, lower], 0), jnp.concatenate(hot, 0), ((1,), (1,)))
        half = GROUP * SUB
        total = product[:half] + product[half:]
        quads = []
        for side in range(2):
            lanes = slice(side * LANES, (side + 1) * LANES)
            merged = total[side * 4 * SUB : (side * 4 + 1) * SUB, lanes]
            for tile in range(1, 4):
                base = (side * 4 + tile) * SUB
                merged = jnp.where(lane // LOW == tile, total[base : base + SUB, lanes], merged)
            quads.append(swap_blocks(merged, sub, lane))
        first, second = quads
        rows_ref[window, 0:LANES] = jnp.where(sub < 4, first, pltpu.roll(second, 4, 0))
        rows_ref[window, LANES : 2 * LANES] = jnp.where(sub < 4, pltpu.roll(first, 4, 0), second)
        return carry

    lax.fori_loop(0, tiles // GROUP, expand, 0, unroll=32)
    upper, lower = split(rows_ref[...])
    slots = devices * capacity
    place = (iota((slots, tiles), 0) == slot_row).astype(F32).astype(BF16)
    packed_ref[...] = jnp.dot(place, upper, preferred_element_type=F32)
    packed_ref[...] += jnp.dot(place, lower, preferred_element_type=F32)
    for side in range(2):
        lanes = slice(side * LANES, (side + 1) * LANES)
        send_ref[:, side * capacity : (side + 1) * capacity, :] = packed_ref[:, lanes].reshape(
            devices, capacity, LANES
        )


def collect_kernel(capacity, got_ref, low_ref, high_ref, ids_ref):
    devices = got_ref.shape[0]
    per_row = LANES // capacity
    rows = 2 * low_ref.shape[1]
    total = jnp.zeros((rows, 2 * LANES), F32)
    line = iota((rows, LANES), 0)
    tall = line // RIM * RIM + STEP * (line % SUB) + line % RIM // SUB + 1
    for block in range(devices // per_row):
        owners = slice(block * per_row, (block + 1) * per_row)
        ids = jnp.sum(got_ref[owners, 2 * capacity : 2 * capacity + SUB, :], axis=0)[0:1, :]
        ids_ref[block : block + 1, :] = ids
        hot = (ids.astype(jnp.int32) == tall).astype(F32).astype(BF16)
        values = jnp.concatenate(
            [
                got_ref[owners, 0:capacity, :].reshape(LANES, LANES),
                got_ref[owners, capacity : 2 * capacity, :].reshape(LANES, LANES),
            ],
            1,
        )
        upper, lower = split(values)
        total = total + contract(
            jnp.concatenate([hot, hot], 1), jnp.concatenate([upper, lower], 0), ((1,), (0,))
        )
    half = rows // 2
    for plane in range(2):
        lanes = slice(plane * LANES, (plane + 1) * LANES)
        low_ref[plane] = total[0:half, lanes]
        high_ref[plane] = total[half:, lanes]


def faces_kernel(fields, last_ref, *refs):
    sources, low_ref, high_ref = refs[0:4], refs[4], refs[5]
    lat_ref, lon_ref, std_ref, mask_ref = local = refs[6:10]
    copies = fetch(sources, local, refs[10])
    for copy in copies:
        copy.wait()
    final = (iota((SUB, LANES), 0) == SUB - 1) & (last_ref[0] == 1)
    for part, target in enumerate((low_ref, high_ref)):
        for step in range(STEP):
            rows = pl.ds(part * RIM + step, SUB, stride=STEP)
            place = slice(step * SUB, (step + 1) * SUB)
            mask = mask_ref[rows, :].astype(F32)
            for field in range(fields):
                face = lat_ref[field, rows, :]
                if part == 1 and step == STEP - 1:
                    face = jnp.where(final, 0.0, face)
                target[field, place, :] = face
                target[fields + field, place, :] = lon_ref[field, rows, :]
                target[2 * fields + field, place, :] = mask * std_ref[field, rows, :]


def turn_kernel(order, low_ref, high_ref, south_ref, north_ref, mid_ref, first_ref, last_ref):
    for plane, pieces in enumerate(order):
        tall = jnp.concatenate(
            [
                ref[source, step * SUB : (step + 1) * SUB, :]
                for source, step in pieces
                for ref in (south_ref, low_ref, high_ref, north_ref)
            ],
            0,
        )
        turned = jnp.transpose(tall)
        mid_ref[plane] = turned
        first_ref[plane] = turned[0:RIM]
        last_ref[plane] = turned[turned.shape[0] - RIM :]


def at(index):
    return slice(index * SUB, (index + 1) * SUB)


def weave_kernel(mid_ref, west_ref, east_ref, north_ref, east_face_ref, scale_ref, wide_ref):
    cols = mid_ref.shape[1]
    length = cols + 2 * RIM
    count = length // SUB
    for plane in range(mid_ref.shape[0]):
        wide_ref[plane, 0:RIM, :] = west_ref[plane]
        wide_ref[plane, RIM : RIM + cols, :] = mid_ref[plane]
        wide_ref[plane, RIM + cols :, :] = east_ref[plane]
    for kind, target in enumerate((north_ref, east_face_ref, scale_ref)):
        for step in range(STEP):
            for j in range(count):
                target[at(j * STEP + step), :] = wide_ref[
                    kind * STEP + step, pl.ds(j, SUB, stride=count), :
                ]


def solve_kernel(
    north_ref,
    east_ref,
    scale_ref,
    mid_ref,
    west_ref,
    far_ref,
    lam_ref,
    image_ref,
    image_next_ref,
    seen_ref,
    seen_next_ref,
    parts_ref,
    u_ref,
    wide_ref,
    grid_ref,
    rhs_ref,
    turn_ref,
    t_ref,
    line_ref,
):
    cols = mid_ref.shape[1]
    length = cols + 2 * RIM
    count = length // SUB
    total = count * STEP
    lam = lam_ref[...]
    sub = iota((SUB, LANES), 0)
    lane = iota((SUB, LANES), 1)
    group = lane // REACH
    inner = (lane % REACH >= RIM // STEP) & (lane % REACH < REACH - RIM // STEP)
    for plane in range(2):
        wide_ref[plane, 0:RIM, :] = west_ref[plane]
        wide_ref[plane, RIM : RIM + cols, :] = mid_ref[plane]
        wide_ref[plane, RIM + cols :, :] = far_ref[plane]
        for j in range(count):
            x = wide_ref[plane, pl.ds(j, SUB, stride=count), :]
            even = jnp.where(group % 2 == 0, x, pltpu.roll(x, REACH, 1))
            odd = jnp.where(group % 2 == 1, x, pltpu.roll(x, LANES - REACH, 1))
            for parity, y in enumerate((even, odd)):
                turned = pltpu.roll(y, 2 * REACH, 1)
                grid_ref[plane, at(j * STEP + parity), :] = jnp.where(group < 2, y, turned)
                grid_ref[plane, at(j * STEP + 2 + parity), :] = jnp.where(group < 2, turned, y)

    def group_sum(x):
        x = x + pltpu.roll(x, 2 * REACH, 1)
        return x + pltpu.roll(x, REACH, 1)

    def diffuse():
        def one_pass(index, carry):
            here = [u_ref[at(step), :] for step in range(STEP)]
            seam = []
            for step in range(STEP):
                final = (count - 1) * STEP + step
                ahead = pltpu.roll(here[step], SUB - 1, 0)
                seam.append(east_ref[at(final), :] * (ahead - u_ref[at(final), :]))
            west = [pltpu.roll(flux, 1, 0) for flux in seam]
            for j in range(count):
                base = j * STEP
                if j + 1 < count:
                    ahead = [u_ref[at(base + STEP + step), :] for step in range(STEP)]
                    flux = [
                        east_ref[at(base + step), :] * (ahead[step] - here[step]) for step in range(STEP)
                    ]
                else:
                    ahead, flux = here, seam
                above = here[1:] + [pltpu.roll(here[0], LANES - 1, 1)]
                rise = [north_ref[at(base + step), :] * (above[step] - here[step]) for step in range(STEP)]
                below = [pltpu.roll(rise[STEP - 1], 1, 1)] + rise[:-1]
                for step in range(STEP):
                    u_ref[at(base + step), :] = here[step] + (
                        (flux[step] - west[step]) + (rise[step] - below[step])
                    )
                west, here = flux, ahead
            return carry

        lax.fori_loop(0, PASSES, one_pass, 0)

    zero = jnp.zeros((SUB, LANES), F32)
    own = [
        inner & (count * sub + j >= RIM) & (count * sub + j < RIM + cols) for j in range(count)
    ]
    spans = {}
    for j in range(count):
        edges = tuple(RIM <= count * row + j < RIM + cols for row in range(SUB))
        spans.setdefault(edges, []).append(j)

    def whole(terms, extra=None):
        out = zero
        for members in spans.values():
            keep = own[members[0]] if extra is None else own[members[0]] & extra
            out = out + jnp.where(keep, sum((terms(j) for j in members), zero), 0.0)
        return jnp.sum(jnp.sum(out, axis=1, keepdims=True), axis=0, keepdims=True)

    def ratio(top, bottom):
        return jnp.where(bottom > 0, top / jnp.where(bottom > 0, bottom, 1.0), 0.0)

    def over_steps(term):
        return lambda j: sum((term(j * STEP + step) for step in range(STEP)), zero)

    for index in range(total):
        u_ref[at(index), :] = lam * scale_ref[at(index), :] * grid_ref[0, at(index), :]
    diffuse()
    for index in range(total):
        rhs_ref[at(index), :] = u_ref[at(index), :]
    diffuse()
    for index in range(total):
        scale = scale_ref[at(index), :]
        image = scale * u_ref[at(index), :]
        seen = group_sum(lam * image)
        image_ref[at(index), :] = image
        t_ref[0, at(index), :] = seen
        u_ref[at(index), :] = lam * scale * (grid_ref[1, at(index), :] * seen)
    diffuse()
    for index in range(total):
        turn_ref[at(index), :] = u_ref[at(index), :]
    diffuse()
    for index in range(total):
        image = scale_ref[at(index), :] * u_ref[at(index), :]
        image_next_ref[at(index), :] = image
        t_ref[1, at(index), :] = group_sum(lam * image)

    once = group == 0
    bb = whole(over_steps(lambda n: rhs_ref[at(n), :] * rhs_ref[at(n), :]))
    bw = whole(over_steps(lambda n: rhs_ref[at(n), :] * turn_ref[at(n), :]))
    weighted = lambda n: grid_ref[1, at(n), :] * t_ref[0, at(n), :]
    s00 = whole(over_steps(lambda n: weighted(n) * t_ref[0, at(n), :]), once)
    s01 = whole(over_steps(lambda n: weighted(n) * t_ref[1, at(n), :]), once)
    fit, seen_fit = ratio(bw, bb), ratio(s01, s00)

    def left(n):
        gap = turn_ref[at(n), :] - fit * rhs_ref[at(n), :]
        return gap * gap

    def seen_left(n):
        gap = t_ref[1, at(n), :] - seen_fit * t_ref[0, at(n), :]
        return grid_ref[1, at(n), :] * (gap * gap)

    rest, seen_rest = whole(over_steps(left)), whole(over_steps(seen_left), once)
    wide = iota(parts_ref.shape, 1)
    parts = jnp.zeros(parts_ref.shape, F32)
    for position, number in enumerate((bb, bw, fit, rest, s00, seen_fit, seen_rest)):
        parts = jnp.where(wide == position, number, parts)
    parts_ref[...] = parts
    edge = RIM // STEP
    for plane, target in enumerate((seen_ref, seen_next_ref)):
        for j in range(count):
            x = t_ref[plane, at(j * STEP), :]
            for step in range(1, STEP):
                x = jnp.where(group == step, t_ref[plane, at(j * STEP + step), :], x)
            line_ref[pl.ds(j, SUB, stride=count), :] = x
        flat = jnp.transpose(line_ref[RIM : RIM + cols, :])
        depth = REACH - 2 * edge
        for step in range(STEP):
            start = step * REACH + edge
            target[step * depth : (step + 1) * depth, :] = flat[start : start + depth]


def pack_kernel(seen_ref, seen_next_ref, ids_ref, both_ref):
    rows = seen_ref.shape[0]
    blocks = ids_ref.shape[0]
    upper, lower = split(jnp.concatenate([seen_ref[...], seen_next_ref[...]], 1))
    both = jnp.concatenate([upper, lower], 0)
    ids = jnp.transpose(jnp.concatenate([ids_ref[...]] * (LANES // blocks), 0)).astype(jnp.int32)
    line = iota((LANES, 2 * rows), 1) % rows
    depth = rows // STEP
    wide = STEP * (line % depth) + line // depth + 1
    hot = jnp.concatenate(
        [(ids[:, block : block + 1] == wide).astype(F32).astype(BF16) for block in range(blocks)], 0
    )
    both_ref[...] = jnp.dot(hot, both, preferred_element_type=F32)


def answer_kernel(parts_ref, both_ref, back_ref, coef_ref):

    def column(index):
        return parts_ref[:, index : index + 1]

    def add(x):
        return jnp.sum(x, axis=0, keepdims=True)

    bb_each, fit_each, s00_each, seen_fit_each = column(0), column(2), column(4), column(5)
    bb, bw = add(bb_each), add(column(1))
    fit = bw / bb
    step = bb / (bb + bw)
    gap = fit_each - fit
    rest = add(column(3) + gap * (gap * bb_each))
    tilt = step * rest / bb
    full = fit + tilt
    gap = seen_fit_each - full
    energy = rest + tilt * tilt * bb + add(column(6) + gap * (gap * s00_each))
    step_next = jnp.where(rest > 0, rest / jnp.where(rest > 0, energy, 1.0), 0.0)
    coef = step * (1.0 + step_next * full)
    coef_next = -step * step_next
    line = iota(coef_ref.shape, 0)
    coef_ref[...] = jnp.where(line == 0, coef, coef_next)
    back_ref[...] = coef * both_ref[:, 0:LANES] + coef_next * both_ref[:, LANES:]


def increment_kernel(image_ref, image_next_ref, coef_ref, out_ref, line_ref):
    fields, _, cols = out_ref.shape
    count = image_ref.shape[0] // (SUB * STEP)
    coef, coef_next = coef_ref[0:1, :], coef_ref[1:2, :]
    edge = RIM // STEP
    depth = REACH - 2 * edge
    for step in range(STEP):
        for j in range(count):
            index = at(j * STEP + step)
            line_ref[step, pl.ds(j, SUB, stride=count), :] = (
                coef * image_ref[index, :] + coef_next * image_next_ref[index, :]
            )
        flat = jnp.transpose(line_ref[step, RIM : RIM + cols, :])
        for field in range(fields):
            start = field * REACH + edge
            out_ref[field, pl.ds(step, depth, stride=STEP), :] = flat[start : start + depth]


def depart_kernel(back_ref, slot_ref, off_ref, inn_ref, out_ref):
    slots = back_ref.shape[0]
    upper, lower = split(back_ref[...])
    slot = slot_ref[...].astype(jnp.int32)
    line = iota((LANES, LANES), 1)
    place = jnp.concatenate(
        [
            jnp.concatenate(
                [
                    (slot[block * LANES : (block + 1) * LANES] == line + part * LANES).astype(F32).astype(BF16)
                    for part in range(slots // LANES)
                ],
                1,
            )
            for block in range(slot.shape[0] // LANES)
        ],
        0,
    )
    rows = jnp.dot(place, jnp.concatenate([upper, lower], 1), preferred_element_type=F32)
    seen = jnp.take_along_axis(rows[:, 0:LANES] + rows[:, LANES:], off_ref[...], axis=1)
    out_ref[...] = inn_ref[...] - seen


def neighbours(low, high, axis, periodic):
    count = lax.axis_size(axis)
    forward = [(i, i + 1) for i in range(count - 1)]
    if periodic:
        forward.append((count - 1, 0))
    backward = [(target, source) for source, target in forward]
    return lax.ppermute(high, axis, forward), lax.ppermute(low, axis, backward)


def exchange(low, high, order):
    planes = len(order)
    south, north = neighbours(low, high, "lat", False)
    mid, first, last = call(
        functools.partial(turn_kernel, order),
        [((planes, LANES, LANES), F32), ((planes, RIM, LANES), F32), ((planes, RIM, LANES), F32)],
        (low, high, south, north),
        nbytes=4 * planes * 300 * LANES,
    )
    west, east = neighbours(first, last, "lon", True)
    return mid, west, east


def analyse(
    lat_coef, lon_coef, std_scale, land_mask, lst_weights, innovation, inv_var, owner, row_ids, offsets
):
    fields, tile_rows, tile_cols = lat_coef.shape
    tiles, width = innovation.shape
    lat_count, lon_count = lax.axis_size("lat"), lax.axis_size("lon")
    devices = lat_count * lon_count
    capacity = max(2, 2 * tiles // devices)
    if (fields * REACH, tile_cols, width, tile_rows + 2 * RIM) != (LANES,) * 4:
        raise ValueError("tile shape")
    if RIM > tile_rows // 2 or capacity % SUB or LANES % capacity or tiles % LANES:
        raise ValueError("slot shape")
    half = tile_rows // 2
    slots = devices * capacity
    last = (lax.axis_index("lat") == lat_count - 1).astype(jnp.int32).reshape(1)
    me = (lax.axis_index("lat") * lon_count + lax.axis_index("lon")).astype(jnp.int32).reshape(1)

    face_low, face_high = call(
        functools.partial(faces_kernel, fields),
        [((3 * fields, half, LANES), F32)] * 2,
        (last, lat_coef, lon_coef, std_scale, land_mask),
        scratch=[pltpu.VMEM(x.shape, x.dtype) for x in (lat_coef, lon_coef, std_scale, land_mask)]
        + [pltpu.SemaphoreType.DMA((4,))],
        smem=(0,),
        hbm=(1, 2, 3, 4),
    )
    face_low, face_high, owner = lax.optimization_barrier((face_low, face_high, owner))
    block = 2 * capacity + SUB
    tables = (owner.reshape(1, tiles), row_ids.reshape(1, tiles), innovation, inv_var, offsets)
    send, slot = call(
        functools.partial(route_kernel, devices, capacity),
        [((devices, block, LANES), F32), ((tiles, LANES), F32)],
        (me,) + tables,
        scratch=[pltpu.VMEM((tiles, 2 * LANES), F32), pltpu.VMEM((slots, 2 * LANES), F32)]
        + [pltpu.VMEM(x.shape, x.dtype) for x in tables]
        + [pltpu.SemaphoreType.DMA((len(tables),))],
        smem=(0,),
        hbm=range(1, 1 + len(tables)),
        flops=10**9,
        nbytes=10**7,
    )
    face_mid, face_west, face_east = exchange(
        face_low,
        face_high,
        [[(kind * fields + field, step) for field in range(fields)] for kind in range(3) for step in range(STEP)],
    )
    got = lax.all_to_all(send, AXES, split_axis=0, concat_axis=0, tiled=True)
    span = tile_cols + 2 * RIM
    woven = (span * STEP, LANES)
    north8, east8, scale8 = call(
        weave_kernel,
        [(woven, F32)] * 3,
        (face_mid, face_west, face_east),
        scratch=(pltpu.VMEM((3 * STEP, span, LANES), F32),),
        nbytes=3 * 10**6,
    )
    low, high, ids = call(
        functools.partial(collect_kernel, capacity),
        [((2, half, LANES), F32)] * 2 + [((slots // LANES, LANES), F32)],
        (got,),
    )
    mid, west, east = exchange(low, high, [[(plane, step) for step in range(STEP)] for plane in range(2)])
    lam = jnp.broadcast_to(jnp.repeat(lst_weights, REACH)[None, :], (SUB, LANES))
    image, image_next, seen, seen_next, parts = call(
        solve_kernel,
        [(woven, F32)] * 2 + [((tile_rows, LANES), F32)] * 2 + [((devices, LANES), F32)],
        (north8, east8, scale8, mid, west, east, lam),
        scratch=(
            pltpu.VMEM(woven, F32),
            pltpu.VMEM((2, span, LANES), F32),
            pltpu.VMEM((2,) + woven, F32),
            pltpu.VMEM(woven, F32),
            pltpu.VMEM(woven, F32),
            pltpu.VMEM((2,) + woven, F32),
            pltpu.VMEM((span, LANES), F32),
        ),
        flops=10**9,
        nbytes=10**7,
    )
    (both,) = call(pack_kernel, [((slots, 2 * LANES), F32)], (seen, seen_next, ids), nbytes=10**6)
    parts = lax.all_to_all(parts, AXES, split_axis=0, concat_axis=0, tiled=True)
    back, coef = call(
        answer_kernel, [((slots, LANES), F32), ((SUB, LANES), F32)], (parts, both), nbytes=10**6
    )
    back = lax.all_to_all(
        back.reshape(devices, capacity, LANES), AXES, split_axis=0, concat_axis=0, tiled=True
    ).reshape(slots, LANES)
    (increment,) = call(
        increment_kernel,
        [((fields, tile_rows, tile_cols), F32)],
        (image, image_next, coef),
        scratch=(pltpu.VMEM((STEP, span, LANES), F32),),
        nbytes=10**6,
    )
    (departure,) = call(depart_kernel, [((tiles, width), F32)], (back, slot, offsets, innovation))
    return increment, departure


def solution(mesh):
    grid = P(None, "lat", "lon")
    tile = P(AXES, None)
    in_specs = (grid, grid, grid, P("lat", "lon"), P(), tile, tile, tile, P(AXES), tile)
    return jax.shard_map(analyse, mesh=mesh, in_specs=in_specs, out_specs=(grid, tile), check_vma=False)
```

time: 135 us -> 104 us (0.77)
  Pallas kernels: 48.1 us -> 20 us
  waiting for transfers between devices: 35.8 us -> 48.6 us
  blocking collectives: 10.3 us -> 0 us
  local copies, waits for them, and re-layouts: 6.71 us -> 0.17 us
  starting transfers between devices: 32.4 us -> 33.9 us
    pallas_call x10 -> x11, Pallas kernels: 48.1 us -> 20 us  [call(): pl.pallas_call(kernel, out_shape=[jax.ShapeDtypeStruct(shape, dtype) for...]
    all_to_all x1 -> x0, blocking collectives: 10.3 us -> none  [on_device(): parts = lax.all_to_all(parts, AXES, split_axis=0, concat_axis=0, tiled=True)]
    all_to_all x2 -> x3, waiting for transfers between devices: 13.8 us -> 24 us  [the longest x1 14.8 us: analyse(): lax.all_to_all(back.reshape(devices, capacity, LANES), AXES, split_axis=0...]
    unnamed x23 -> x6, local copies, waits for them, and re-layouts: 6.05 us -> 0.01 us
    all_to_all x2 -> x3, starting transfers between devices: 9.93 us -> 13.1 us  [the longest x1 7.34 us: analyse(): got = lax.all_to_all(send, AXES, split_axis=0, concat_axis=0, tiled=True)]
    ppermute x4, waiting for transfers between devices: 17.9 us -> 20.4 us  [neighbours(): lax.ppermute(high, axis, forward)]
    ppermute x4, starting transfers between devices: 14.6 us -> 12.9 us  [neighbours(): lax.ppermute(high, axis, forward)]
  transfers between devices with their start and end apart: 10 -> 11, of which waited for: 4 -> 7; matrix products, arithmetic and copies ran while one was open for 0% -> 0% of each run, Pallas kernels for 9% -> 2%
where the time goes in v2:
time: 104 us; the launch traced here: 103 us
  waiting for transfers between devices  48.6 us (47%)
  starting transfers between devices  33.9 us (33%)
  Pallas kernels  20 us (19%)
    ppermute x4, waiting for transfers between devices, neighbours(): lax.ppermute(high, axis, forward)  20.4 us
    pallas_call x11, Pallas kernels, call(): pl.pallas_call(kernel, out_shape=[jax.ShapeDtypeStruct(shape, dtype) for...  20 us
    all_to_all x1, waiting for transfers between devices, analyse(): lax.all_to_all(back.reshape(devices, capacity, LANES), AXES, split_axis=0...  14.8 us
    ppermute x4, starting transfers between devices, neighbours(): lax.ppermute(high, axis, forward)  12.9 us
    ppermute x4, starting transfers between devices, neighbours(): lax.ppermute(low, axis, backward)  7.85 us
    all_to_all x1, starting transfers between devices, analyse(): got = lax.all_to_all(send, AXES, split_axis=0, concat_axis=0, tiled=True)  7.34 us
    all_to_all x1, waiting for transfers between devices, analyse(): parts = lax.all_to_all(parts, AXES, split_axis=0, concat_axis=0, tiled=True)  6.6 us
    ppermute x4, waiting for transfers between devices, neighbours(): lax.ppermute(low, axis, backward)  4.24 us
  transfers between devices with their start and end apart: 11, of which 7 were waited for; matrix products, arithmetic and copies ran while one was open for 0% of the time, Pallas kernels for 2%

profile of v2, /device:TPU:0, one launch (start us, length us, event | category | flops | bytes accessed | tf_op | source)
XLA Modules:
  0.0 103.4 jit_solution(12073733981690741790)
XLA Ops:
  0.6 1.1 %shard_map.113 = (f32[12,32,128]{2,1,0:T(8,128)S(1)}, f32[12,32,128]{2,1,0:T(8,128)S(1)}) custom-call(s32[1]{0:T(128)} %bitcast.last_ref, f32[4,64,128]{2,1,0:T(8,128)} %refs_0_.1, f32[4,64,128]{2,1,0:T(8,128)} %refs_1_.1, f32[4,64,128]{2,1,0:T(8,128)} %refs_2_.1, s32[64,128]{1,0:T(8,128)} %refs_3_.2), custom_call_target="tpu_custom_call" | custom-call | flops 1000 | bytes 100000 | tf_op jit(solution)/shard_map/pallas_call | solution.py:38
  1.8 5.4 %shard_map.116 = (f32[32,72,128]{2,1,0:T(8,128)}, f32[512,128]{1,0:T(8,128)S(1)}) custom-call(s32[1]{0:T(128)} %bitcast.1.refs_0_, s32[1,512]{1,0:T(1,128)} %bitcast.12, s32[1,512]{1,0:T(1,128)} %bitcast.13, f32[512,128]{1,0:T(8,128)} %inn_ref.1, f32[512,128]{1,0:T(8,128)} %refs_4_.1, s32[512,128]{1,0:T(8,128)} %off_ref.1), custom_call_target="tpu_custom_call" | custom-call | flops 1000000000 | bytes 10000000 | tf_op jit(solution)/shard_map/pallas_call | solution.py:38
  7.1 7.3 %all-to-all-start = ((f32[32,72,128]{2,1,0:T(8,128)}), f32[32,72,128]{2,1,0:T(8,128)S(1)}, u32[]{:S(2)}, u32[]{:S(2)}) async-start(f32[32,72,128]{2,1,0:T(8,128)} %get-tuple-element.39), calls=%async_computation | async-start | bytes 2359296 | tf_op jit(solution)/shard_map/all_to_all | solution.py:552
  14.5 0.0 copy-start.2
  14.5 3.7 %collective-permute-start = (f32[12,32,128]{2,1,0:T(8,128)S(1)}, f32[12,32,128]{2,1,0:T(8,128)S(1)}, u32[]{:S(2)}, u32[]{:S(2)}) collective-permute-start(f32[12,32,128]{2,1,0:T(8,128)S(1)} %get-tuple-element.31.high_ref), channel_id=1, source_target_pairs={{0,8},{8,16},{16,24},{1,9},{9,17},{17,25},{2,10},{10,18},{18,26},{... | collective-permute-start | bytes 589832 | tf_op jit(solution)/shard_map/ppermute | solution.py:490
  18.2 1.3 %collective-permute-start.1 = (f32[12,32,128]{2,1,0:T(8,128)S(1)}, f32[12,32,128]{2,1,0:T(8,128)S(1)}, u32[]{:S(2)}, u32[]{:S(2)}) collective-permute-start(f32[12,32,128]{2,1,0:T(8,128)S(1)} %get-tuple-element.30.low_ref), channel_id=1, source_target_pairs={{8,0},{16,8},{24,16},{9,1},{17,9},{25,17},{10,2},{18,10},{26,18},{... | collective-permute-start | bytes 589832 | tf_op jit(solution)/shard_map/ppermute | solution.py:490
  19.5 19.0 %collective-permute-done.south_ref = f32[12,32,128]{2,1,0:T(8,128)S(1)} collective-permute-done((f32[12,32,128]{2,1,0:T(8,128)S(1)}, f32[12,32,128]{2,1,0:T(8,128)S(1)}, u32[]{:S(2)}, u32[]{:S(2)}) %collective-permute-start) | collective-permute-done | bytes 196640 | tf_op jit(solution)/shard_map/ppermute | solution.py:490
  38.5 0.0 collective-permute-done.1.north_ref
  38.5 0.3 shard_map.114
  38.7 0.1 collective-permute-start.2
  38.8 2.6 %collective-permute-start.3 = (f32[12,32,128]{2,1,0:T(8,128)S(1)}, f32[12,32,128]{2,1,0:T(8,128)S(1)}, u32[]{:S(2)}, u32[]{:S(2)}) collective-permute-start(f32[12,32,128]{2,1,0:T(8,128)S(1)} %get-tuple-element.34), channel_id=1, source_target_pairs={{1,0},{2,1},{3,2},{4,3},{5,4},{6,5},{7,6},{0,7},{9,8},{10,9},{11,1... | collective-permute-start | bytes 589832 | tf_op jit(solution)/shard_map/ppermute | solution.py:490
  41.4 2.7 %all-to-all-done.got_ref = f32[32,72,128]{2,1,0:T(8,128)S(1)} async-done(((f32[32,72,128]{2,1,0:T(8,128)}), f32[32,72,128]{2,1,0:T(8,128)S(1)}, u32[]{:S(2)}, u32[]{:S(2)}) %all-to-all-start) | async-done | bytes 1179680 | tf_op jit(solution)/shard_map/all_to_all | solution.py:552
  44.1 0.3 shard_map.117
  44.4 9.1 %collective-permute-start.4 = (f32[2,32,128]{2,1,0:T(8,128)S(1)}, f32[2,32,128]{2,1,0:T(8,128)S(1)}, u32[]{:S(2)}, u32[]{:S(2)}) collective-permute-start(f32[2,32,128]{2,1,0:T(8,128)S(1)} %get-tuple-element.41.high_ref), channel_id=1, source_target_pairs={{0,8},{8,16},{16,24},{1,9},{9,17},{17,25},{2,10},{10,18},{18,26},{... | collective-permute-start | bytes 98312 | tf_op jit(solution)/shard_map/ppermute | solution.py:490
  53.5 1.3 %collective-permute-start.5 = (f32[2,32,128]{2,1,0:T(8,128)S(1)}, f32[2,32,128]{2,1,0:T(8,128)S(1)}, u32[]{:S(2)}, u32[]{:S(2)}) collective-permute-start(f32[2,32,128]{2,1,0:T(8,128)S(1)} %get-tuple-element.40.low_ref), channel_id=1, source_target_pairs={{8,0},{16,8},{24,16},{9,1},{17,9},{25,17},{10,2},{18,10},{26,18},{... | collective-permute-start | bytes 98312 | tf_op jit(solution)/shard_map/ppermute | solution.py:490
  54.8 0.3 collective-permute-done.4.south_ref
  55.1 4.2 %collective-permute-done.5.north_ref = f32[2,32,128]{2,1,0:T(8,128)S(1)} collective-permute-done((f32[2,32,128]{2,1,0:T(8,128)S(1)}, f32[2,32,128]{2,1,0:T(8,128)S(1)}, u32[]{:S(2)}, u32[]{:S(2)}) %collective-permute-start.5) | collective-permute-done | bytes 32800 | tf_op jit(solution)/shard_map/ppermute | solution.py:490
  59.3 0.1 shard_map.118
  59.4 0.1 collective-permute-start.6
  59.4 2.6 %collective-permute-start.7 = (f32[2,32,128]{2,1,0:T(8,128)S(1)}, f32[2,32,128]{2,1,0:T(8,128)S(1)}, u32[]{:S(2)}, u32[]{:S(2)}) collective-permute-start(f32[2,32,128]{2,1,0:T(8,128)S(1)} %get-tuple-element.44), channel_id=1, source_target_pairs={{1,0},{2,1},{3,2},{4,3},{5,4},{6,5},{7,6},{0,7},{9,8},{10,9},{11,1... | collective-permute-start | bytes 98312 | tf_op jit(solution)/shard_map/ppermute | solution.py:490
  62.1 0.0 copy-done.2
  62.1 0.1 broadcast_in_dim.10
  62.2 0.1 broadcast_in_dim.11
  62.2 0.0 collective-permute-done.2.west_ref
  62.2 0.0 collective-permute-done.3.east_ref
  62.2 0.3 shard_map.115
  62.6 1.1 %collective-permute-done.6.west_ref = f32[2,32,128]{2,1,0:T(8,128)S(1)} collective-permute-done((f32[2,32,128]{2,1,0:T(8,128)S(1)}, f32[2,32,128]{2,1,0:T(8,128)S(1)}, u32[]{:S(2)}, u32[]{:S(2)}) %collective-permute-start.6) | collective-permute-done | bytes 32800 | tf_op jit(solution)/shard_map/ppermute | solution.py:490
  63.7 0.0 collective-permute-done.7.far_ref
  63.7 8.3 %shard_map.119 = (f32[768,128]{1,0:T(8,128)S(1)}, f32[768,128]{1,0:T(8,128)S(1)}, f32[64,128]{1,0:T(8,128)S(1)}, f32[64,128]{1,0:T(8,128)S(1)}, f32[32,128]{1,0:T(8,128)}) custom-call(f32[768,128]{1,0:T(8,128)S(1)} %get-tuple-element.35.north_ref, f32[768,128]{1,0:T(8,128)S(1)} %get-tuple-element.36.east_ref, f32[768,128]{1,0:T(8,128)S(1)} %get-tuple-element.37.scale_ref, ...), custom_call_target="tpu_custom_call" | custom-call | flops 1000000000 | bytes 10000000 | tf_op jit(solution)/shard_map/pallas_call | solution.py:38
  72.0 3.1 %all-to-all-start.1 = ((f32[32,1,128]{2,1,0:T(1,128)}), f32[32,1,128]{2,1,0:T(1,128)S(1)}, u32[]{:S(2)}, u32[]{:S(2)}) async-start(f32[32,1,128]{2,1,0:T(1,128)} %bitcast.5), calls=%async_computation.1 | async-start | bytes 32768 | tf_op jit(solution)/shard_map/all_to_all | solution.py:586
  75.0 0.5 shard_map.120.both_ref
  75.6 6.6 %all-to-all-done.1 = f32[32,1,128]{2,1,0:T(1,128)S(1)} async-done(((f32[32,1,128]{2,1,0:T(1,128)}), f32[32,1,128]{2,1,0:T(1,128)S(1)}, u32[]{:S(2)}, u32[]{:S(2)}) %all-to-all-start.1) | async-done | bytes 16416 | tf_op jit(solution)/shard_map/all_to_all | solution.py:586
  82.2 1.6 %shard_map.121 = (f32[1024,128]{1,0:T(8,128)}, f32[8,128]{1,0:T(8,128)S(1)}) custom-call(f32[32,128]{1,0:T(8,128)S(1)} %bitcast.11, f32[1024,256]{1,0:T(8,128)S(1)} %shard_map.120.both_ref), custom_call_target="tpu_custom_call" | custom-call | flops 1000 | bytes 1000000 | tf_op jit(solution)/shard_map/pallas_call | solution.py:38
  83.8 0.0 copy-start
  83.8 0.0 copy-start.1
  83.8 2.7 %all-to-all-start.2 = ((f32[32,32,128]{2,1,0:T(8,128)}), f32[32,32,128]{2,1,0:T(8,128)S(1)}, u32[]{:S(2)}, u32[]{:S(2)}) async-start(f32[32,32,128]{2,1,0:T(8,128)} %bitcast.7), calls=%async_computation.2 | async-start | bytes 1048576 | tf_op jit(solution)/shard_map/all_to_all | solution.py:590
  86.5 0.8 shard_map.122
  87.4 14.8 %all-to-all-done.2 = f32[32,32,128]{2,1,0:T(8,128)S(1)} async-done(((f32[32,32,128]{2,1,0:T(8,128)}), f32[32,32,128]{2,1,0:T(8,128)S(1)}, u32[]{:S(2)}, u32[]{:S(2)}) %all-to-all-start.2) | async-done | bytes 524320 | tf_op jit(solution)/shard_map/all_to_all | solution.py:590
  102.1 0.0 copy-done
  102.1 0.0 copy-done.1
  102.1 1.3 %shard_map.123 = f32[512,128]{1,0:T(8,128)} custom-call(f32[1024,128]{1,0:T(8,128)S(1)} %bitcast.10, f32[512,128]{1,0:T(8,128)S(1)} %get-tuple-element.53.slot_ref, s32[512,128]{1,0:T(8,128)S(1)} %copy-done.1, f32[512,128]{1,0:T(8,128)S(1)} %copy-done), custom_call_target="tpu_custom_call" | custom-call | flops 1000 | bytes 100000 | tf_op jit(solution)/shard_map/pallas_call | solution.py:38
  (1 shorter events, 0.0 us)
Async XLA Ops:
  7.1 36.9 %all-to-all-start = ((f32[32,72,128]{2,1,0:T(8,128)}), f32[32,72,128]{2,1,0:T(8,128)S(1)}, u32[]{:S(2)}, u32[]{:S(2)}) async-start(f32[32,72,128]{2,1,0:T(8,128)} %get-tuple-element.39), calls=%async_computation | async-start | bytes 2359296 | tf_op jit(solution)/shard_map/all_to_all | solution.py:552
  14.5 47.6 %copy-start.2 = (f32[4]{0:T(128)S(1)}, f32[4]{0:T(128)}, u32[]{:S(2)}) copy-start(f32[4]{0:T(128)} %param.14) | copy-start | bytes 52
  14.5 23.9 %collective-permute-start = (f32[12,32,128]{2,1,0:T(8,128)S(1)}, f32[12,32,128]{2,1,0:T(8,128)S(1)}, u32[]{:S(2)}, u32[]{:S(2)}) collective-permute-start(f32[12,32,128]{2,1,0:T(8,128)S(1)} %get-tuple-element.31.high_ref), channel_id=1, source_target_pairs={{0,8},{8,16},{16,24},{1,9},{9,17},{17,25},{2,10},{10,18},{18,26},{... | collective-permute-start | bytes 589832 | tf_op jit(solution)/shard_map/ppermute | solution.py:490
  18.2 20.3 %collective-permute-start.1 = (f32[12,32,128]{2,1,0:T(8,128)S(1)}, f32[12,32,128]{2,1,0:T(8,128)S(1)}, u32[]{:S(2)}, u32[]{:S(2)}) collective-permute-start(f32[12,32,128]{2,1,0:T(8,128)S(1)} %get-tuple-element.30.low_ref), channel_id=1, source_target_pairs={{8,0},{16,8},{24,16},{9,1},{17,9},{25,17},{10,2},{18,10},{26,18},{... | collective-permute-start | bytes 589832 | tf_op jit(solution)/shard_map/ppermute | solution.py:490
  38.7 23.5 %collective-permute-start.2 = (f32[12,32,128]{2,1,0:T(8,128)S(1)}, f32[12,32,128]{2,1,0:T(8,128)S(1)}, u32[]{:S(2)}, u32[]{:S(2)}) collective-permute-start(f32[12,32,128]{2,1,0:T(8,128)S(1)} %get-tuple-element.33), channel_id=1, source_target_pairs={{0,1},{1,2},{2,3},{3,4},{4,5},{5,6},{6,7},{7,0},{8,9},{9,10},{10,1... | collective-permute-start | bytes 589832 | tf_op jit(solution)/shard_map/ppermute | solution.py:490
  38.8 23.5 %collective-permute-start.3 = (f32[12,32,128]{2,1,0:T(8,128)S(1)}, f32[12,32,128]{2,1,0:T(8,128)S(1)}, u32[]{:S(2)}, u32[]{:S(2)}) collective-permute-start(f32[12,32,128]{2,1,0:T(8,128)S(1)} %get-tuple-element.34), channel_id=1, source_target_pairs={{1,0},{2,1},{3,2},{4,3},{5,4},{6,5},{7,6},{0,7},{9,8},{10,9},{11,1... | collective-permute-start | bytes 589832 | tf_op jit(solution)/shard_map/ppermute | solution.py:490
  44.4 10.7 %collective-permute-start.4 = (f32[2,32,128]{2,1,0:T(8,128)S(1)}, f32[2,32,128]{2,1,0:T(8,128)S(1)}, u32[]{:S(2)}, u32[]{:S(2)}) collective-permute-start(f32[2,32,128]{2,1,0:T(8,128)S(1)} %get-tuple-element.41.high_ref), channel_id=1, source_target_pairs={{0,8},{8,16},{16,24},{1,9},{9,17},{17,25},{2,10},{10,18},{18,26},{... | collective-permute-start | bytes 98312 | tf_op jit(solution)/shard_map/ppermute | solution.py:490
  53.5 5.8 %collective-permute-start.5 = (f32[2,32,128]{2,1,0:T(8,128)S(1)}, f32[2,32,128]{2,1,0:T(8,128)S(1)}, u32[]{:S(2)}, u32[]{:S(2)}) collective-permute-start(f32[2,32,128]{2,1,0:T(8,128)S(1)} %get-tuple-element.40.low_ref), channel_id=1, source_target_pairs={{8,0},{16,8},{24,16},{9,1},{17,9},{25,17},{10,2},{18,10},{26,18},{... | collective-permute-start | bytes 98312 | tf_op jit(solution)/shard_map/ppermute | solution.py:490
  59.4 4.3 %collective-permute-start.6 = (f32[2,32,128]{2,1,0:T(8,128)S(1)}, f32[2,32,128]{2,1,0:T(8,128)S(1)}, u32[]{:S(2)}, u32[]{:S(2)}) collective-permute-start(f32[2,32,128]{2,1,0:T(8,128)S(1)} %get-tuple-element.43), channel_id=1, source_target_pairs={{0,1},{1,2},{2,3},{3,4},{4,5},{5,6},{6,7},{7,0},{8,9},{9,10},{10,1... | collective-permute-start | bytes 98312 | tf_op jit(solution)/shard_map/ppermute | solution.py:490
  59.4 4.2 %collective-permute-start.7 = (f32[2,32,128]{2,1,0:T(8,128)S(1)}, f32[2,32,128]{2,1,0:T(8,128)S(1)}, u32[]{:S(2)}, u32[]{:S(2)}) collective-permute-start(f32[2,32,128]{2,1,0:T(8,128)S(1)} %get-tuple-element.44), channel_id=1, source_target_pairs={{1,0},{2,1},{3,2},{4,3},{5,4},{6,5},{7,6},{0,7},{9,8},{10,9},{11,1... | collective-permute-start | bytes 98312 | tf_op jit(solution)/shard_map/ppermute | solution.py:490
  72.0 10.2 %all-to-all-start.1 = ((f32[32,1,128]{2,1,0:T(1,128)}), f32[32,1,128]{2,1,0:T(1,128)S(1)}, u32[]{:S(2)}, u32[]{:S(2)}) async-start(f32[32,1,128]{2,1,0:T(1,128)} %bitcast.5), calls=%async_computation.1 | async-start | bytes 32768 | tf_op jit(solution)/shard_map/all_to_all | solution.py:586
  83.8 18.4 %copy-start = (f32[512,128]{1,0:T(8,128)S(1)}, f32[512,128]{1,0:T(8,128)}, u32[]{:S(2)}) copy-start(f32[512,128]{1,0:T(8,128)} %inn_ref.1) | copy-start | bytes 786436
  83.8 18.4 %copy-start.1 = (s32[512,128]{1,0:T(8,128)S(1)}, s32[512,128]{1,0:T(8,128)}, u32[]{:S(2)}) copy-start(s32[512,128]{1,0:T(8,128)} %off_ref.1) | copy-start | bytes 786436
  83.8 18.4 %all-to-all-start.2 = ((f32[32,32,128]{2,1,0:T(8,128)}), f32[32,32,128]{2,1,0:T(8,128)S(1)}, u32[]{:S(2)}, u32[]{:S(2)}) async-start(f32[32,32,128]{2,1,0:T(8,128)} %bitcast.7), calls=%async_computation.2 | async-start | bytes 1048576 | tf_op jit(solution)/shard_map/all_to_all | solution.py:590

commit v3 on v2

--- a/solution.py
+++ b/solution.py
@@ -25,10 +25,8 @@
     return lax.broadcasted_iota(jnp.int32, shape, dim)
 
 
-def call(kernel, outs, args, scratch=(), smem=(), hbm=(), flops=1000, nbytes=100000):
+def call(kernel, outs, args, scratch=(), hbm=(), flops=1000, nbytes=100000):
     spaces = [pltpu.VMEM] * len(args)
-    for index in smem:
-        spaces[index] = pltpu.SMEM
     for index in hbm:
         spaces[index] = pltpu.HBM
     args = [
@@ -81,7 +79,7 @@
 
 
 def route_kernel(devices, capacity, *refs):
-    me_ref, sources = refs[0], refs[1:6]
+    flags_ref, sources = refs[0], refs[1:6]
     send_ref, slot_ref, rows_ref, packed_ref = refs[6:10]
     owner_ref, rid_ref, inn_ref, var_ref, off_ref = local = refs[10:15]
     copies = fetch(sources, local, refs[15])
@@ -95,16 +93,14 @@
     rank = jnp.sum(hits * before, axis=0, keepdims=True)
     slot_row = owner_ref[...] * capacity + rank.astype(jnp.int32)
     slot_ref[...] = jnp.transpose(jnp.broadcast_to(slot_row.astype(F32), (LANES, tiles)))
-    shift = (me_ref[0] % per_row) * capacity
+    shift = (flags_ref[1:2, 0:1] % per_row) * capacity
     rank_hot = (rank.astype(jnp.int32) + shift == iota((LANES, tiles), 0)).astype(F32).astype(BF16)
     marked = hits * (rid_ref[...].astype(F32) + 1.0)
     ids = contract(marked.astype(BF16), rank_hot, ((1,), (1,)))
-    spare = send_ref.shape[1] - 2 * capacity
-    pad_row = iota((devices, spare, LANES), 1)
-    send_ref[:, 2 * capacity :, :] = jnp.where(
-        pad_row == 0, jnp.broadcast_to(ids[:, None, :], (devices, spare, LANES)), 0.0
-    )
-
+    block = 2 * capacity + 1
+    for device in range(devices):
+        place = device * block + 2 * capacity
+        send_ref[place : place + 1, :] = ids[device : device + 1, :]
     for copy in copies[2:]:
         copy.wait()
     sub = iota((SUB, LANES), 0)
@@ -148,29 +144,38 @@
     place = (iota((slots, tiles), 0) == slot_row).astype(F32).astype(BF16)
     packed_ref[...] = jnp.dot(place, upper, preferred_element_type=F32)
     packed_ref[...] += jnp.dot(place, lower, preferred_element_type=F32)
-    for side in range(2):
-        lanes = slice(side * LANES, (side + 1) * LANES)
-        send_ref[:, side * capacity : (side + 1) * capacity, :] = packed_ref[:, lanes].reshape(
-            devices, capacity, LANES
-        )
-
-
-def collect_kernel(capacity, got_ref, low_ref, high_ref, ids_ref):
-    devices = got_ref.shape[0]
+    for device in range(devices):
+        for side in range(2):
+            start = device * block + side * capacity
+            send_ref[start : start + capacity, :] = packed_ref[
+                device * capacity : (device + 1) * capacity, side * LANES : (side + 1) * LANES
+            ]
+
+
+def by_parity(odd, low, high):
+    return jnp.where(odd, low, high), jnp.where(odd, high, low)
+
+
+def collect_kernel(devices, capacity, flags_ref, got_ref, low_ref, high_ref, ids_ref, first_ref, second_ref):
+    block = 2 * capacity + 1
     per_row = LANES // capacity
     rows = 2 * low_ref.shape[1]
     total = jnp.zeros((rows, 2 * LANES), F32)
     line = iota((rows, LANES), 0)
     tall = line // RIM * RIM + STEP * (line % SUB) + line % RIM // SUB + 1
-    for block in range(devices // per_row):
-        owners = slice(block * per_row, (block + 1) * per_row)
-        ids = jnp.sum(got_ref[owners, 2 * capacity : 2 * capacity + SUB, :], axis=0)[0:1, :]
-        ids_ref[block : block + 1, :] = ids
+
+    def piece(device, start, size):
+        return got_ref[device * block + start : device * block + start + size, :]
+
+    for group in range(devices // per_row):
+        members = range(group * per_row, (group + 1) * per_row)
+        ids = sum(piece(device, 2 * capacity, 1) for device in members)
+        ids_ref[group : group + 1, :] = ids
         hot = (ids.astype(jnp.int32) == tall).astype(F32).astype(BF16)
         values = jnp.concatenate(
             [
-                got_ref[owners, 0:capacity, :].reshape(LANES, LANES),
-                got_ref[owners, capacity : 2 * capacity, :].reshape(LANES, LANES),
+                jnp.concatenate([piece(device, side * capacity, capacity) for device in members], 0)
+                for side in range(2)
             ],
             1,
         )
@@ -179,19 +184,22 @@
             jnp.concatenate([hot, hot], 1), jnp.concatenate([upper, lower], 0), ((1,), (0,))
         )
     half = rows // 2
+    odd = flags_ref[2:3, :] == 1
     for plane in range(2):
         lanes = slice(plane * LANES, (plane + 1) * LANES)
-        low_ref[plane] = total[0:half, lanes]
-        high_ref[plane] = total[half:, lanes]
-
-
-def faces_kernel(fields, last_ref, *refs):
-    sources, low_ref, high_ref = refs[0:4], refs[4], refs[5]
-    lat_ref, lon_ref, std_ref, mask_ref = local = refs[6:10]
-    copies = fetch(sources, local, refs[10])
+        low, high = total[0:half, lanes], total[half:, lanes]
+        low_ref[plane] = low
+        high_ref[plane] = high
+        first_ref[plane], second_ref[plane] = by_parity(odd, low, high)
+
+
+def faces_kernel(fields, flags_ref, *refs):
+    sources, low_ref, high_ref, first_ref, second_ref = refs[0:4], *refs[4:8]
+    lat_ref, lon_ref, std_ref, mask_ref = local = refs[8:12]
+    copies = fetch(sources, local, refs[12])
     for copy in copies:
         copy.wait()
-    final = (iota((SUB, LANES), 0) == SUB - 1) & (last_ref[0] == 1)
+    final = (iota((SUB, LANES), 0) == SUB - 1) & (flags_ref[0:1, :] == 1)
     for part, target in enumerate((low_ref, high_ref)):
         for step in range(STEP):
             rows = pl.ds(part * RIM + step, SUB, stride=STEP)
@@ -204,36 +212,40 @@
                 target[field, place, :] = face
                 target[fields + field, place, :] = lon_ref[field, rows, :]
                 target[2 * fields + field, place, :] = mask * std_ref[field, rows, :]
-
-
-def turn_kernel(order, low_ref, high_ref, south_ref, north_ref, mid_ref, first_ref, last_ref):
+    odd = flags_ref[2:3, :] == 1
+    for plane in range(3 * fields):
+        first_ref[plane], second_ref[plane] = by_parity(odd, low_ref[plane], high_ref[plane])
+
+
+def turn_kernel(order, flags_ref, low_ref, high_ref, got_ref, other_ref, mid_ref, first_ref, second_ref):
+    odd = flags_ref[2:3, :] == 1
+    odd_lon = flags_ref[3:4, :] == 1
     for plane, pieces in enumerate(order):
-        tall = jnp.concatenate(
-            [
-                ref[source, step * SUB : (step + 1) * SUB, :]
-                for source, step in pieces
-                for ref in (south_ref, low_ref, high_ref, north_ref)
-            ],
-            0,
+        rows = []
+        for source, step in pieces:
+            place = slice(step * SUB, (step + 1) * SUB)
+            south, north = by_parity(odd, got_ref[source, place, :], other_ref[source, place, :])
+            rows.extend([south, low_ref[source, place, :], high_ref[source, place, :], north])
+        turned = jnp.transpose(jnp.concatenate(rows, 0))
+        mid_ref[plane] = turned
+        first_ref[plane], second_ref[plane] = by_parity(
+            odd_lon, turned[0:RIM], turned[turned.shape[0] - RIM :]
         )
-        turned = jnp.transpose(tall)
-        mid_ref[plane] = turned
-        first_ref[plane] = turned[0:RIM]
-        last_ref[plane] = turned[turned.shape[0] - RIM :]
 
 
 def at(index):
     return slice(index * SUB, (index + 1) * SUB)
 
 
-def weave_kernel(mid_ref, west_ref, east_ref, north_ref, east_face_ref, scale_ref, wide_ref):
+def weave_kernel(flags_ref, mid_ref, got_ref, other_ref, north_ref, east_face_ref, scale_ref, wide_ref):
     cols = mid_ref.shape[1]
     length = cols + 2 * RIM
     count = length // SUB
     for plane in range(mid_ref.shape[0]):
-        wide_ref[plane, 0:RIM, :] = west_ref[plane]
+        west, east = by_parity(flags_ref[3:4, :] == 1, got_ref[plane], other_ref[plane])
+        wide_ref[plane, 0:RIM, :] = west
         wide_ref[plane, RIM : RIM + cols, :] = mid_ref[plane]
-        wide_ref[plane, RIM + cols :, :] = east_ref[plane]
+        wide_ref[plane, RIM + cols :, :] = east
     for kind, target in enumerate((north_ref, east_face_ref, scale_ref)):
         for step in range(STEP):
             for j in range(count):
@@ -243,12 +255,13 @@
 
 
 def solve_kernel(
+    flags_ref,
     north_ref,
     east_ref,
     scale_ref,
     mid_ref,
-    west_ref,
-    far_ref,
+    got_ref,
+    other_ref,
     lam_ref,
     image_ref,
     image_next_ref,
@@ -273,9 +286,10 @@
     group = lane // REACH
     inner = (lane % REACH >= RIM // STEP) & (lane % REACH < REACH - RIM // STEP)
     for plane in range(2):
-        wide_ref[plane, 0:RIM, :] = west_ref[plane]
+        west, east = by_parity(flags_ref[3:4, :] == 1, got_ref[plane], other_ref[plane])
+        wide_ref[plane, 0:RIM, :] = west
         wide_ref[plane, RIM : RIM + cols, :] = mid_ref[plane]
-        wide_ref[plane, RIM + cols :, :] = far_ref[plane]
+        wide_ref[plane, RIM + cols :, :] = east
         for j in range(count):
             x = wide_ref[plane, pl.ds(j, SUB, stride=count), :]
             even = jnp.where(group % 2 == 0, x, pltpu.roll(x, REACH, 1))
@@ -328,61 +342,65 @@
         edges = tuple(RIM <= count * row + j < RIM + cols for row in range(SUB))
         spans.setdefault(edges, []).append(j)
 
-    def whole(terms, extra=None):
+    kind_of = {j: edges for edges, members in spans.items() for j in members}
+
+    def tally():
+        return {edges: zero for edges in spans}
+
+    def whole(sums, extra=None):
         out = zero
-        for members in spans.values():
+        for edges, members in spans.items():
             keep = own[members[0]] if extra is None else own[members[0]] & extra
-            out = out + jnp.where(keep, sum((terms(j) for j in members), zero), 0.0)
+            out = out + jnp.where(keep, sums[edges], 0.0)
         return jnp.sum(jnp.sum(out, axis=1, keepdims=True), axis=0, keepdims=True)
 
     def ratio(top, bottom):
         return jnp.where(bottom > 0, top / jnp.where(bottom > 0, bottom, 1.0), 0.0)
 
-    def over_steps(term):
-        return lambda j: sum((term(j * STEP + step) for step in range(STEP)), zero)
-
+    once = group == 0
+    sum_bb, sum_bw, sum_00, sum_01 = tally(), tally(), tally(), tally()
     for index in range(total):
         u_ref[at(index), :] = lam * scale_ref[at(index), :] * grid_ref[0, at(index), :]
     diffuse()
     for index in range(total):
-        rhs_ref[at(index), :] = u_ref[at(index), :]
+        rhs = u_ref[at(index), :]
+        rhs_ref[at(index), :] = rhs
+        sum_bb[kind_of[index // STEP]] += rhs * rhs
     diffuse()
     for index in range(total):
         scale = scale_ref[at(index), :]
         image = scale * u_ref[at(index), :]
         seen = group_sum(lam * image)
+        weighted = grid_ref[1, at(index), :] * seen
         image_ref[at(index), :] = image
         t_ref[0, at(index), :] = seen
-        u_ref[at(index), :] = lam * scale * (grid_ref[1, at(index), :] * seen)
+        u_ref[at(index), :] = lam * scale * weighted
+        sum_00[kind_of[index // STEP]] += weighted * seen
     diffuse()
     for index in range(total):
-        turn_ref[at(index), :] = u_ref[at(index), :]
+        turn = u_ref[at(index), :]
+        turn_ref[at(index), :] = turn
+        sum_bw[kind_of[index // STEP]] += turn * rhs_ref[at(index), :]
     diffuse()
     for index in range(total):
         image = scale_ref[at(index), :] * u_ref[at(index), :]
         image_next_ref[at(index), :] = image
-        t_ref[1, at(index), :] = group_sum(lam * image)
-
-    once = group == 0
-    bb = whole(over_steps(lambda n: rhs_ref[at(n), :] * rhs_ref[at(n), :]))
-    bw = whole(over_steps(lambda n: rhs_ref[at(n), :] * turn_ref[at(n), :]))
-    weighted = lambda n: grid_ref[1, at(n), :] * t_ref[0, at(n), :]
-    s00 = whole(over_steps(lambda n: weighted(n) * t_ref[0, at(n), :]), once)
-    s01 = whole(over_steps(lambda n: weighted(n) * t_ref[1, at(n), :]), once)
+        seen = group_sum(lam * image)
+        t_ref[1, at(index), :] = seen
+        sum_01[kind_of[index // STEP]] += grid_ref[1, at(index), :] * t_ref[0, at(index), :] * seen
+    bb, bw, s00, s01 = whole(sum_bb), whole(sum_bw), whole(sum_00, once), whole(sum_01, once)
     fit, seen_fit = ratio(bw, bb), ratio(s01, s00)
-
-    def left(n):
-        gap = turn_ref[at(n), :] - fit * rhs_ref[at(n), :]
-        return gap * gap
-
-    def seen_left(n):
-        gap = t_ref[1, at(n), :] - seen_fit * t_ref[0, at(n), :]
-        return grid_ref[1, at(n), :] * (gap * gap)
-
-    rest, seen_rest = whole(over_steps(left)), whole(over_steps(seen_left), once)
+    left, seen_left = tally(), tally()
+    for index in range(total):
+        kind = kind_of[index // STEP]
+        gap = turn_ref[at(index), :] - fit * rhs_ref[at(index), :]
+        left[kind] += gap * gap
+        gap = t_ref[1, at(index), :] - seen_fit * t_ref[0, at(index), :]
+        seen_left[kind] += grid_ref[1, at(index), :] * (gap * gap)
+    rest, seen_rest = whole(left), whole(seen_left, once)
     wide = iota(parts_ref.shape, 1)
     parts = jnp.zeros(parts_ref.shape, F32)
-    for position, number in enumerate((bb, bw, fit, rest, s00, seen_fit, seen_rest)):
+    for position, number in enumerate((bb, s00, bw, s01, fit, seen_fit, rest, seen_rest)):
         parts = jnp.where(wide == position, number, parts)
     parts_ref[...] = parts
     edge = RIM // STEP
@@ -415,23 +433,30 @@
 
 
 def answer_kernel(parts_ref, both_ref, back_ref, coef_ref):
-
-    def column(index):
-        return parts_ref[:, index : index + 1]
+    parts = parts_ref[...]
+
+    def ahead(x, count):
+        return pltpu.roll(x, LANES - count, 1)
 
     def add(x):
-        return jnp.sum(x, axis=0, keepdims=True)
-
-    bb_each, fit_each, s00_each, seen_fit_each = column(0), column(2), column(4), column(5)
-    bb, bw = add(bb_each), add(column(1))
-    fit = bw / bb
+        return jnp.broadcast_to(jnp.sum(x, axis=0, keepdims=True), (SUB, LANES))
+
+    sums = add(parts)
+    fits = jnp.where(sums > 0, ahead(sums, 2) / sums, 0.0)
+    gap = ahead(parts, 4) - fits[0:1, :]
+    rests = add(ahead(parts, 6) + gap * (gap * parts))
+
+    def pick(x, lane):
+        return x[0:1, lane : lane + 1]
+
+    bb, s00, bw = pick(sums, 0), pick(sums, 1), pick(sums, 2)
+    fit, seen_fit = pick(fits, 0), pick(fits, 1)
+    rest, seen_rest = pick(rests, 0), pick(rests, 1)
     step = bb / (bb + bw)
-    gap = fit_each - fit
-    rest = add(column(3) + gap * (gap * bb_each))
-    tilt = step * rest / bb
+    tilt = rest / (bb + bw)
     full = fit + tilt
-    gap = seen_fit_each - full
-    energy = rest + tilt * tilt * bb + add(column(6) + gap * (gap * s00_each))
+    gap = seen_fit - full
+    energy = rest + tilt * tilt * bb + seen_rest + gap * (gap * s00)
     step_next = jnp.where(rest > 0, rest / jnp.where(rest > 0, energy, 1.0), 0.0)
     coef = step * (1.0 + step_next * full)
     coef_next = -step * step_next
@@ -481,26 +506,26 @@
     out_ref[...] = inn_ref[...] - seen
 
 
-def neighbours(low, high, axis, periodic):
+def swap(first, second, axis, periodic):
     count = lax.axis_size(axis)
-    forward = [(i, i + 1) for i in range(count - 1)]
+    pairs = [[(i, i + 1) for i in range(start, count - 1, 2)] for start in (0, 1)]
     if periodic:
-        forward.append((count - 1, 0))
-    backward = [(target, source) for source, target in forward]
-    return lax.ppermute(high, axis, forward), lax.ppermute(low, axis, backward)
-
-
-def exchange(low, high, order):
+        pairs[1].append((count - 1, 0))
+    both = [edges + [(target, source) for source, target in edges] for edges in pairs]
+    return lax.ppermute(first, axis, both[0]), lax.ppermute(second, axis, both[1])
+
+
+def exchange(flags, low, high, first, second, order):
     planes = len(order)
-    south, north = neighbours(low, high, "lat", False)
-    mid, first, last = call(
+    got, other = swap(first, second, "lat", False)
+    mid, first, second = call(
         functools.partial(turn_kernel, order),
         [((planes, LANES, LANES), F32), ((planes, RIM, LANES), F32), ((planes, RIM, LANES), F32)],
-        (low, high, south, north),
+        (flags, low, high, got, other),
         nbytes=4 * planes * 300 * LANES,
     )
-    west, east = neighbours(first, last, "lon", True)
-    return mid, west, east
+    got, other = swap(first, second, "lon", True)
+    return mid, got, other
 
 
 def analyse(
@@ -513,63 +538,67 @@
     capacity = max(2, 2 * tiles // devices)
     if (fields * REACH, tile_cols, width, tile_rows + 2 * RIM) != (LANES,) * 4:
         raise ValueError("tile shape")
-    if RIM > tile_rows // 2 or capacity % SUB or LANES % capacity or tiles % LANES:
+    if RIM > tile_rows // 2 or lat_count % 2 or lon_count % 2 or capacity % SUB or LANES % capacity or tiles % LANES:
         raise ValueError("slot shape")
     half = tile_rows // 2
     slots = devices * capacity
-    last = (lax.axis_index("lat") == lat_count - 1).astype(jnp.int32).reshape(1)
-    me = (lax.axis_index("lat") * lon_count + lax.axis_index("lon")).astype(jnp.int32).reshape(1)
-
-    face_low, face_high = call(
+    lat_index, lon_index = lax.axis_index("lat"), lax.axis_index("lon")
+    last = (lat_index == lat_count - 1).astype(jnp.int32)
+    flags = jnp.zeros((SUB, LANES), jnp.int32)
+    for line, flag in enumerate((last, lat_index * lon_count + lon_index, lat_index % 2, lon_index % 2)):
+        flags = jnp.where(iota(flags.shape, 0) == line, flag.astype(jnp.int32), flags)
+
+    face_low, face_high, *face_ends = call(
         functools.partial(faces_kernel, fields),
-        [((3 * fields, half, LANES), F32)] * 2,
-        (last, lat_coef, lon_coef, std_scale, land_mask),
+        [((3 * fields, half, LANES), F32)] * 4,
+        (flags, lat_coef, lon_coef, std_scale, land_mask),
         scratch=[pltpu.VMEM(x.shape, x.dtype) for x in (lat_coef, lon_coef, std_scale, land_mask)]
         + [pltpu.SemaphoreType.DMA((4,))],
-        smem=(0,),
         hbm=(1, 2, 3, 4),
     )
-    face_low, face_high, owner = lax.optimization_barrier((face_low, face_high, owner))
-    block = 2 * capacity + SUB
+    block = 2 * capacity + 1
     tables = (owner.reshape(1, tiles), row_ids.reshape(1, tiles), innovation, inv_var, offsets)
     send, slot = call(
         functools.partial(route_kernel, devices, capacity),
-        [((devices, block, LANES), F32), ((tiles, LANES), F32)],
-        (me,) + tables,
+        [((devices * block, LANES), F32), ((tiles, LANES), F32)],
+        (flags,) + tables,
         scratch=[pltpu.VMEM((tiles, 2 * LANES), F32), pltpu.VMEM((slots, 2 * LANES), F32)]
         + [pltpu.VMEM(x.shape, x.dtype) for x in tables]
         + [pltpu.SemaphoreType.DMA((len(tables),))],
-        smem=(0,),
-        hbm=range(1, 1 + len(tables)),
+            hbm=range(1, 1 + len(tables)),
         flops=10**9,
         nbytes=10**7,
     )
-    face_mid, face_west, face_east = exchange(
+    face_all = exchange(
+        flags,
         face_low,
         face_high,
+        *face_ends,
         [[(kind * fields + field, step) for field in range(fields)] for kind in range(3) for step in range(STEP)],
     )
-    got = lax.all_to_all(send, AXES, split_axis=0, concat_axis=0, tiled=True)
+    got = lax.all_to_all(
+        send.reshape(devices, 1, block * LANES), AXES, split_axis=0, concat_axis=0, tiled=True
+    ).reshape(devices * block, LANES)
     span = tile_cols + 2 * RIM
     woven = (span * STEP, LANES)
     north8, east8, scale8 = call(
         weave_kernel,
         [(woven, F32)] * 3,
-        (face_mid, face_west, face_east),
+        (flags, *face_all),
         scratch=(pltpu.VMEM((3 * STEP, span, LANES), F32),),
         nbytes=3 * 10**6,
     )
-    low, high, ids = call(
-        functools.partial(collect_kernel, capacity),
-        [((2, half, LANES), F32)] * 2 + [((slots // LANES, LANES), F32)],
-        (got,),
-    )
-    mid, west, east = exchange(low, high, [[(plane, step) for step in range(STEP)] for plane in range(2)])
+    low, high, ids, *ends = call(
+        functools.partial(collect_kernel, devices, capacity),
+        [((2, half, LANES), F32)] * 2 + [((slots // LANES, LANES), F32)] + [((2, half, LANES), F32)] * 2,
+        (flags, got),
+    )
+    grid = exchange(flags, low, high, *ends, [[(plane, step) for step in range(STEP)] for plane in range(2)])
     lam = jnp.broadcast_to(jnp.repeat(lst_weights, REACH)[None, :], (SUB, LANES))
     image, image_next, seen, seen_next, parts = call(
         solve_kernel,
         [(woven, F32)] * 2 + [((tile_rows, LANES), F32)] * 2 + [((devices, LANES), F32)],
-        (north8, east8, scale8, mid, west, east, lam),
+        (flags, north8, east8, scale8, *grid, lam),
         scratch=(
             pltpu.VMEM(woven, F32),
             pltpu.VMEM((2, span, LANES), F32),

time: 104 us -> 95.9 us (0.922)
  starting transfers between devices: 33.9 us -> 28 us
  waiting for transfers between devices: 48.6 us -> 46.3 us
    ppermute x8, starting transfers between devices: 20.7 us -> 13.7 us  [the longest x4 9.11 us: swap(): lax.ppermute(first, axis, both[0])]
    ppermute x8, waiting for transfers between devices: 24.6 us -> 22.9 us  [the longest x4 19.8 us: swap(): lax.ppermute(first, axis, both[0])]
    all_to_all x1, starting transfers between devices: 3.05 us -> 4.3 us  [analyse(): parts = lax.all_to_all(parts, AXES, split_axis=0, concat_axis=0, tiled=True)]
  transfers between devices with their start and end apart: 11 -> 11, of which waited for: 7 -> 7; matrix products, arithmetic and copies ran while one was open for 0% -> 0% of each run, Pallas kernels for 2% -> 4%
where the time goes in v3:
time: 95.9 us; the launch traced here: 95.5 us
  waiting for transfers between devices  46.3 us (48%)
  starting transfers between devices  28 us (29%)
  Pallas kernels  20.1 us (21%)
    pallas_call x11, Pallas kernels, call(): pl.pallas_call(kernel, out_shape=[jax.ShapeDtypeStruct(shape, dtype) for...  20.1 us
    ppermute x4, waiting for transfers between devices, swap(): lax.ppermute(first, axis, both[0])  19.8 us
    all_to_all x1, waiting for transfers between devices, analyse(): lax.all_to_all(back.reshape(devices, capacity, LANES), AXES, split_axis=0...  14.8 us
    ppermute x4, starting transfers between devices, swap(): lax.ppermute(first, axis, both[0])  9.11 us
    all_to_all x1, starting transfers between devices, analyse(): lax.all_to_all(send.reshape(devices, 1, block * LANES), AXES, split_axis=...  7.34 us
    all_to_all x1, waiting for transfers between devices, analyse(): parts = lax.all_to_all(parts, AXES, split_axis=0, concat_axis=0, tiled=True)  6.6 us
    ppermute x4, starting transfers between devices, swap(): lax.ppermute(second, axis, both[1])  4.55 us
    all_to_all x1, starting transfers between devices, analyse(): parts = lax.all_to_all(parts, AXES, split_axis=0, concat_axis=0, tiled=True)  4.3 us
  transfers between devices with their start and end apart: 11, of which 7 were waited for; matrix products, arithmetic and copies ran while one was open for 0% of the time, Pallas kernels for 4%

profile of v3, /device:TPU:0, one launch (start us, length us, event | category | flops | bytes accessed | tf_op | source)
XLA Modules:
  0.0 95.5 jit_solution(3553053665073445489)
XLA Ops:
  0.7 0.1 select_select_fusion.flags_ref.refs_0_
  0.8 5.3 %shard_map.116 = (f32[2080,128]{1,0:T(8,128)}, f32[512,128]{1,0:T(8,128)S(1)}) custom-call(s32[8,128]{1,0:T(8,128)S(1)} %select_select_fusion.flags_ref.refs_0_, s32[1,512]{1,0:T(1,128)} %bitcast.13, s32[1,512]{1,0:T(1,128)} %bitcast.14, f32[512,128]{1,0:T(8,128)} %inn_ref.1, f32[512,128]{1,0:T(8,128)} %refs_4_.1, s32[512,128]{1,0:T(8,128)} %off_ref.1), custom_call_target="tpu_custom_call" | custom-call | flops 1000000000 | bytes 10000000 | tf_op jit(solution)/shard_map/pallas_call | solution.py:36
  6.1 7.3 %all-to-all-start = ((f32[32,1,8320]{2,1,0:T(1,128)}), f32[32,1,8320]{2,1,0:T(1,128)S(1)}, u32[]{:S(2)}, u32[]{:S(2)}) async-start(f32[32,1,8320]{2,1,0:T(1,128)} %bitcast.2), calls=%async_computation | async-start | bytes 2129920 | tf_op jit(solution)/shard_map/all_to_all | solution.py:579
  13.5 1.1 %shard_map.113 = (f32[12,32,128]{2,1,0:T(8,128)S(1)}, f32[12,32,128]{2,1,0:T(8,128)S(1)}, f32[12,32,128]{2,1,0:T(8,128)S(1)}, f32[12,32,128]{2,1,0:T(8,128)S(1)}) custom-call(s32[8,128]{1,0:T(8,128)S(1)} %select_select_fusion.flags_ref.refs_0_, f32[4,64,128]{2,1,0:T(8,128)} %refs_0_.1, f32[4,64,128]{2,1,0:T(8,128)} %refs_1_.1, f32[4,64,128]{2,1,0:T(8,128)} %refs_2_.1, ...), custom_call_target="tpu_custom_call" | custom-call | flops 1000 | bytes 100000 | tf_op jit(solution)/shard_map/pallas_call | solution.py:36
  14.6 0.0 copy-start.2
  14.6 1.8 %collective-permute-start = (f32[12,32,128]{2,1,0:T(8,128)S(1)}, f32[12,32,128]{2,1,0:T(8,128)S(1)}, u32[]{:S(2)}, u32[]{:S(2)}) collective-permute-start(f32[12,32,128]{2,1,0:T(8,128)S(1)} %get-tuple-element.31), channel_id=1, source_target_pairs={{0,8},{16,24},{8,0},{24,16},{1,9},{17,25},{9,1},{25,17},{2,10},{18... | collective-permute-start | bytes 589832 | tf_op jit(solution)/shard_map/ppermute | solution.py:515
  16.5 0.7 collective-permute-start.1
  17.1 18.4 %collective-permute-done.got_ref = f32[12,32,128]{2,1,0:T(8,128)S(1)} collective-permute-done((f32[12,32,128]{2,1,0:T(8,128)S(1)}, f32[12,32,128]{2,1,0:T(8,128)S(1)}, u32[]{:S(2)}, u32[]{:S(2)}) %collective-permute-start) | collective-permute-done | bytes 196640 | tf_op jit(solution)/shard_map/ppermute | solution.py:515
  35.6 0.0 collective-permute-done.1.other_ref
  35.6 0.3 shard_map.114
  35.9 0.1 collective-permute-start.2
  36.0 2.6 %collective-permute-start.3 = (f32[12,32,128]{2,1,0:T(8,128)S(1)}, f32[12,32,128]{2,1,0:T(8,128)S(1)}, u32[]{:S(2)}, u32[]{:S(2)}) collective-permute-start(f32[12,32,128]{2,1,0:T(8,128)S(1)} %get-tuple-element.35), channel_id=1, source_target_pairs={{1,2},{3,4},{5,6},{7,0},{2,1},{4,3},{6,5},{0,7},{9,10},{11,12},{13... | collective-permute-start | bytes 589832 | tf_op jit(solution)/shard_map/ppermute | solution.py:515
  38.5 2.1 %all-to-all-done = f32[32,1,8320]{2,1,0:T(1,128)S(1)} async-done(((f32[32,1,8320]{2,1,0:T(1,128)}), f32[32,1,8320]{2,1,0:T(1,128)S(1)}, u32[]{:S(2)}, u32[]{:S(2)}) %all-to-all-start) | async-done | bytes 1064992 | tf_op jit(solution)/shard_map/all_to_all | solution.py:579
  40.6 0.3 shard_map.117
  40.9 7.1 %collective-permute-start.4 = (f32[2,32,128]{2,1,0:T(8,128)S(1)}, f32[2,32,128]{2,1,0:T(8,128)S(1)}, u32[]{:S(2)}, u32[]{:S(2)}) collective-permute-start(f32[2,32,128]{2,1,0:T(8,128)S(1)} %get-tuple-element.42), channel_id=1, source_target_pairs={{0,8},{16,24},{8,0},{24,16},{1,9},{17,25},{9,1},{25,17},{2,10},{18... | collective-permute-start | bytes 98312 | tf_op jit(solution)/shard_map/ppermute | solution.py:515
  48.0 0.7 collective-permute-start.5
  48.7 1.2 %collective-permute-done.4.got_ref = f32[2,32,128]{2,1,0:T(8,128)S(1)} collective-permute-done((f32[2,32,128]{2,1,0:T(8,128)S(1)}, f32[2,32,128]{2,1,0:T(8,128)S(1)}, u32[]{:S(2)}, u32[]{:S(2)}) %collective-permute-start.4) | collective-permute-done | bytes 32800 | tf_op jit(solution)/shard_map/ppermute | solution.py:515
  49.9 0.0 collective-permute-done.5.other_ref
  49.9 0.1 shard_map.118
  50.1 0.1 collective-permute-start.6
  50.1 0.6 collective-permute-start.7
  50.8 0.0 copy-done.2
  50.8 0.1 broadcast_in_dim.27
  50.9 0.1 broadcast_in_dim.28
  50.9 0.0 collective-permute-done.2.got_ref
  50.9 0.0 collective-permute-done.3.other_ref
  50.9 0.3 shard_map.115
  51.2 0.1 collective-permute-done.6.got_ref
  51.3 3.1 %collective-permute-done.7.other_ref = f32[2,32,128]{2,1,0:T(8,128)S(1)} collective-permute-done((f32[2,32,128]{2,1,0:T(8,128)S(1)}, f32[2,32,128]{2,1,0:T(8,128)S(1)}, u32[]{:S(2)}, u32[]{:S(2)}) %collective-permute-start.7) | collective-permute-done | bytes 32800 | tf_op jit(solution)/shard_map/ppermute | solution.py:515
  54.5 8.8 %shard_map.119 = (f32[768,128]{1,0:T(8,128)S(1)}, f32[768,128]{1,0:T(8,128)S(1)}, f32[64,128]{1,0:T(8,128)S(1)}, f32[64,128]{1,0:T(8,128)S(1)}, f32[32,128]{1,0:T(8,128)}) custom-call(s32[8,128]{1,0:T(8,128)S(1)} %select_select_fusion.flags_ref.refs_0_, f32[768,128]{1,0:T(8,128)S(1)} %get-tuple-element.36.north_ref, ...), custom_call_target="tpu_custom_call" | custom-call | flops 1000000000 | bytes 10000000 | tf_op jit(solution)/shard_map/pallas_call | solution.py:36
  63.3 4.3 %all-to-all-start.1 = ((f32[32,1,128]{2,1,0:T(1,128)}), f32[32,1,128]{2,1,0:T(1,128)S(1)}, u32[]{:S(2)}, u32[]{:S(2)}) async-start(f32[32,1,128]{2,1,0:T(1,128)} %bitcast.5), calls=%async_computation.1 | async-start | bytes 32768 | tf_op jit(solution)/shard_map/all_to_all | solution.py:615
  67.6 0.5 shard_map.120.both_ref
  68.1 6.6 %all-to-all-done.1 = f32[32,1,128]{2,1,0:T(1,128)S(1)} async-done(((f32[32,1,128]{2,1,0:T(1,128)}), f32[32,1,128]{2,1,0:T(1,128)S(1)}, u32[]{:S(2)}, u32[]{:S(2)}) %all-to-all-start.1) | async-done | bytes 16416 | tf_op jit(solution)/shard_map/all_to_all | solution.py:615
  74.7 1.2 %shard_map.121 = (f32[1024,128]{1,0:T(8,128)}, f32[8,128]{1,0:T(8,128)S(1)}) custom-call(f32[32,128]{1,0:T(8,128)S(1)} %bitcast.12, f32[1024,256]{1,0:T(8,128)S(1)} %shard_map.120.both_ref), custom_call_target="tpu_custom_call" | custom-call | flops 1000 | bytes 1000000 | tf_op jit(solution)/shard_map/pallas_call | solution.py:36
  75.9 0.0 copy-start
  75.9 0.0 copy-start.1
  75.9 2.7 %all-to-all-start.2 = ((f32[32,32,128]{2,1,0:T(8,128)}), f32[32,32,128]{2,1,0:T(8,128)S(1)}, u32[]{:S(2)}, u32[]{:S(2)}) async-start(f32[32,32,128]{2,1,0:T(8,128)} %bitcast.7), calls=%async_computation.2 | async-start | bytes 1048576 | tf_op jit(solution)/shard_map/all_to_all | solution.py:619
  78.7 0.8 shard_map.122
  79.5 14.8 %all-to-all-done.2 = f32[32,32,128]{2,1,0:T(8,128)S(1)} async-done(((f32[32,32,128]{2,1,0:T(8,128)}), f32[32,32,128]{2,1,0:T(8,128)S(1)}, u32[]{:S(2)}, u32[]{:S(2)}) %all-to-all-start.2) | async-done | bytes 524320 | tf_op jit(solution)/shard_map/all_to_all | solution.py:619
  94.3 0.0 copy-done
  94.3 0.0 copy-done.1
  94.3 1.3 %shard_map.123 = f32[512,128]{1,0:T(8,128)} custom-call(f32[1024,128]{1,0:T(8,128)S(1)} %bitcast.11, f32[512,128]{1,0:T(8,128)S(1)} %get-tuple-element.55.slot_ref, s32[512,128]{1,0:T(8,128)S(1)} %copy-done.1, f32[512,128]{1,0:T(8,128)S(1)} %copy-done), custom_call_target="tpu_custom_call" | custom-call | flops 1000 | bytes 100000 | tf_op jit(solution)/shard_map/pallas_call | solution.py:36
  (4 shorter events, 0.0 us)
Async XLA Ops:
  6.1 34.5 %all-to-all-start = ((f32[32,1,8320]{2,1,0:T(1,128)}), f32[32,1,8320]{2,1,0:T(1,128)S(1)}, u32[]{:S(2)}, u32[]{:S(2)}) async-start(f32[32,1,8320]{2,1,0:T(1,128)} %bitcast.2), calls=%async_computation | async-start | bytes 2129920 | tf_op jit(solution)/shard_map/all_to_all | solution.py:579
  14.6 36.2 %copy-start.2 = (f32[4]{0:T(128)S(1)}, f32[4]{0:T(128)}, u32[]{:S(2)}) copy-start(f32[4]{0:T(128)} %param.14) | copy-start | bytes 52
  14.6 20.9 %collective-permute-start = (f32[12,32,128]{2,1,0:T(8,128)S(1)}, f32[12,32,128]{2,1,0:T(8,128)S(1)}, u32[]{:S(2)}, u32[]{:S(2)}) collective-permute-start(f32[12,32,128]{2,1,0:T(8,128)S(1)} %get-tuple-element.31), channel_id=1, source_target_pairs={{0,8},{16,24},{8,0},{24,16},{1,9},{17,25},{9,1},{25,17},{2,10},{18... | collective-permute-start | bytes 589832 | tf_op jit(solution)/shard_map/ppermute | solution.py:515
  16.5 19.1 %collective-permute-start.1 = (f32[12,32,128]{2,1,0:T(8,128)S(1)}, f32[12,32,128]{2,1,0:T(8,128)S(1)}, u32[]{:S(2)}, u32[]{:S(2)}) collective-permute-start(f32[12,32,128]{2,1,0:T(8,128)S(1)} %get-tuple-element.32), channel_id=1, source_target_pairs={{8,16},{16,8},{9,17},{17,9},{10,18},{18,10},{11,19},{19,11},{12,20... | collective-permute-start | bytes 589832 | tf_op jit(solution)/shard_map/ppermute | solution.py:515
  35.9 15.1 %collective-permute-start.2 = (f32[12,32,128]{2,1,0:T(8,128)S(1)}, f32[12,32,128]{2,1,0:T(8,128)S(1)}, u32[]{:S(2)}, u32[]{:S(2)}) collective-permute-start(f32[12,32,128]{2,1,0:T(8,128)S(1)} %get-tuple-element.34), channel_id=1, source_target_pairs={{0,1},{2,3},{4,5},{6,7},{1,0},{3,2},{5,4},{7,6},{8,9},{10,11},{12,... | collective-permute-start | bytes 589832 | tf_op jit(solution)/shard_map/ppermute | solution.py:515
  36.0 15.0 %collective-permute-start.3 = (f32[12,32,128]{2,1,0:T(8,128)S(1)}, f32[12,32,128]{2,1,0:T(8,128)S(1)}, u32[]{:S(2)}, u32[]{:S(2)}) collective-permute-start(f32[12,32,128]{2,1,0:T(8,128)S(1)} %get-tuple-element.35), channel_id=1, source_target_pairs={{1,2},{3,4},{5,6},{7,0},{2,1},{4,3},{6,5},{0,7},{9,10},{11,12},{13... | collective-permute-start | bytes 589832 | tf_op jit(solution)/shard_map/ppermute | solution.py:515
  40.9 9.0 %collective-permute-start.4 = (f32[2,32,128]{2,1,0:T(8,128)S(1)}, f32[2,32,128]{2,1,0:T(8,128)S(1)}, u32[]{:S(2)}, u32[]{:S(2)}) collective-permute-start(f32[2,32,128]{2,1,0:T(8,128)S(1)} %get-tuple-element.42), channel_id=1, source_target_pairs={{0,8},{16,24},{8,0},{24,16},{1,9},{17,25},{9,1},{25,17},{2,10},{18... | collective-permute-start | bytes 98312 | tf_op jit(solution)/shard_map/ppermute | solution.py:515
  48.0 1.9 %collective-permute-start.5 = (f32[2,32,128]{2,1,0:T(8,128)S(1)}, f32[2,32,128]{2,1,0:T(8,128)S(1)}, u32[]{:S(2)}, u32[]{:S(2)}) collective-permute-start(f32[2,32,128]{2,1,0:T(8,128)S(1)} %get-tuple-element.43), channel_id=1, source_target_pairs={{8,16},{16,8},{9,17},{17,9},{10,18},{18,10},{11,19},{19,11},{12,20... | collective-permute-start | bytes 98312 | tf_op jit(solution)/shard_map/ppermute | solution.py:515
  50.1 1.3 %collective-permute-start.6 = (f32[2,32,128]{2,1,0:T(8,128)S(1)}, f32[2,32,128]{2,1,0:T(8,128)S(1)}, u32[]{:S(2)}, u32[]{:S(2)}) collective-permute-start(f32[2,32,128]{2,1,0:T(8,128)S(1)} %get-tuple-element.45), channel_id=1, source_target_pairs={{0,1},{2,3},{4,5},{6,7},{1,0},{3,2},{5,4},{7,6},{8,9},{10,11},{12,... | collective-permute-start | bytes 98312 | tf_op jit(solution)/shard_map/ppermute | solution.py:515
  50.1 4.3 %collective-permute-start.7 = (f32[2,32,128]{2,1,0:T(8,128)S(1)}, f32[2,32,128]{2,1,0:T(8,128)S(1)}, u32[]{:S(2)}, u32[]{:S(2)}) collective-permute-start(f32[2,32,128]{2,1,0:T(8,128)S(1)} %get-tuple-element.46), channel_id=1, source_target_pairs={{1,2},{3,4},{5,6},{7,0},{2,1},{4,3},{6,5},{0,7},{9,10},{11,12},{13... | collective-permute-start | bytes 98312 | tf_op jit(solution)/shard_map/ppermute | solution.py:515
  63.3 11.4 %all-to-all-start.1 = ((f32[32,1,128]{2,1,0:T(1,128)}), f32[32,1,128]{2,1,0:T(1,128)S(1)}, u32[]{:S(2)}, u32[]{:S(2)}) async-start(f32[32,1,128]{2,1,0:T(1,128)} %bitcast.5), calls=%async_computation.1 | async-start | bytes 32768 | tf_op jit(solution)/shard_map/all_to_all | solution.py:615
  75.9 18.4 %copy-start = (f32[512,128]{1,0:T(8,128)S(1)}, f32[512,128]{1,0:T(8,128)}, u32[]{:S(2)}) copy-start(f32[512,128]{1,0:T(8,128)} %inn_ref.1) | copy-start | bytes 786436
  75.9 18.4 %copy-start.1 = (s32[512,128]{1,0:T(8,128)S(1)}, s32[512,128]{1,0:T(8,128)}, u32[]{:S(2)}) copy-start(s32[512,128]{1,0:T(8,128)} %off_ref.1) | copy-start | bytes 786436
  75.9 18.4 %all-to-all-start.2 = ((f32[32,32,128]{2,1,0:T(8,128)}), f32[32,32,128]{2,1,0:T(8,128)S(1)}, u32[]{:S(2)}, u32[]{:S(2)}) async-start(f32[32,32,128]{2,1,0:T(8,128)} %bitcast.7), calls=%async_computation.2 | async-start | bytes 1048576 | tf_op jit(solution)/shard_map/all_to_all | solution.py:619

commit v4 on v3

--- a/solution.py
+++ b/solution.py
@@ -81,10 +81,7 @@
 def route_kernel(devices, capacity, *refs):
     flags_ref, sources = refs[0], refs[1:6]
     send_ref, slot_ref, rows_ref, packed_ref = refs[6:10]
-    owner_ref, rid_ref, inn_ref, var_ref, off_ref = local = refs[10:15]
-    copies = fetch(sources, local, refs[15])
-    copies[0].wait()
-    copies[1].wait()
+    owner_ref, rid_ref, inn_ref, var_ref, off_ref = sources
     tiles = off_ref.shape[0]
     per_row = LANES // capacity
     hits = (owner_ref[...] == iota((devices, tiles), 0)).astype(F32)
@@ -101,8 +98,6 @@
     for device in range(devices):
         place = device * block + 2 * capacity
         send_ref[place : place + 1, :] = ids[device : device + 1, :]
-    for copy in copies[2:]:
-        copy.wait()
     sub = iota((SUB, LANES), 0)
     lane = iota((SUB, LANES), 1)
     tall = iota((LOW, LANES), 0)
@@ -194,10 +189,10 @@
 
 
 def faces_kernel(fields, flags_ref, *refs):
-    sources, low_ref, high_ref, first_ref, second_ref = refs[0:4], *refs[4:8]
-    lat_ref, lon_ref, std_ref, mask_ref = local = refs[8:12]
-    copies = fetch(sources, local, refs[12])
-    for copy in copies:
+    low_ref, high_ref, first_ref, second_ref = refs[9:13]
+    lat_ref, lon_ref, std_ref, mask_ref = local = refs[18:22]
+    copies = fetch(refs[0:9], local + refs[13:18], refs[22])
+    for copy in copies[0:4]:
         copy.wait()
     final = (iota((SUB, LANES), 0) == SUB - 1) & (flags_ref[0:1, :] == 1)
     for part, target in enumerate((low_ref, high_ref)):
@@ -215,6 +210,8 @@
     odd = flags_ref[2:3, :] == 1
     for plane in range(3 * fields):
         first_ref[plane], second_ref[plane] = by_parity(odd, low_ref[plane], high_ref[plane])
+    for copy in copies[4:]:
+        copy.wait()
 
 
 def turn_kernel(order, flags_ref, low_ref, high_ref, got_ref, other_ref, mid_ref, first_ref, second_ref):
@@ -270,7 +267,7 @@
     parts_ref,
     u_ref,
     wide_ref,
-    grid_ref,
+    omega_ref,
     rhs_ref,
     turn_ref,
     t_ref,
@@ -290,48 +287,80 @@
         wide_ref[plane, 0:RIM, :] = west
         wide_ref[plane, RIM : RIM + cols, :] = mid_ref[plane]
         wide_ref[plane, RIM + cols :, :] = east
-        for j in range(count):
-            x = wide_ref[plane, pl.ds(j, SUB, stride=count), :]
-            even = jnp.where(group % 2 == 0, x, pltpu.roll(x, REACH, 1))
-            odd = jnp.where(group % 2 == 1, x, pltpu.roll(x, LANES - REACH, 1))
-            for parity, y in enumerate((even, odd)):
-                turned = pltpu.roll(y, 2 * REACH, 1)
-                grid_ref[plane, at(j * STEP + parity), :] = jnp.where(group < 2, y, turned)
-                grid_ref[plane, at(j * STEP + 2 + parity), :] = jnp.where(group < 2, turned, y)
-
-    def group_sum(x):
-        x = x + pltpu.roll(x, 2 * REACH, 1)
-        return x + pltpu.roll(x, REACH, 1)
+
+    def replicate(x):
+        even = jnp.where(group % 2 == 0, x, pltpu.roll(x, REACH, 1))
+        odd = jnp.where(group % 2 == 1, x, pltpu.roll(x, LANES - REACH, 1))
+        even_far, odd_far = pltpu.roll(even, 2 * REACH, 1), pltpu.roll(odd, 2 * REACH, 1)
+        near = group < 2
+        return [
+            jnp.where(near, even, even_far),
+            jnp.where(near, odd, odd_far),
+            jnp.where(near, even_far, even),
+            jnp.where(near, odd_far, odd),
+        ]
+
+    def fold(x):
+        near, centre, even = group < 2, (group == 1) | (group == 2), group % 2 == 0
+        first = jnp.where(near, x[0], x[2]) + pltpu.roll(jnp.where(near, x[2], x[0]), 2 * REACH, 1)
+        second = jnp.where(centre, x[1], x[3]) + pltpu.roll(jnp.where(centre, x[3], x[1]), 2 * REACH, 1)
+        turned = pltpu.roll(jnp.where(even, second, first), LANES - REACH, 1)
+        return jnp.where(even, first, second) + turned
+
+    steps = range(STEP)
+
+    def load(ref, j):
+        return [ref[at(j * STEP + step), :] for step in steps]
+
+    def across(j, here, ahead):
+        face = load(east_ref, j)
+        return [face[step] * (ahead[step] - here[step]) for step in steps]
+
+    def seam_of(here, first):
+        return across(count - 1, here, [pltpu.roll(x, SUB - 1, 0) for x in first])
+
+    def advance(j, here, flux, west):
+        face = load(north_ref, j)
+        above = here[1:] + [pltpu.roll(here[0], LANES - 1, 1)]
+        rise = [face[step] * (above[step] - here[step]) for step in steps]
+        below = [pltpu.roll(rise[STEP - 1], 1, 1)] + rise[:-1]
+        return [here[step] + ((flux[step] - west[step]) + (rise[step] - below[step])) for step in steps]
+
+    def save(j, values):
+        for step in steps:
+            u_ref[at(j * STEP + step), :] = values[step]
 
     def diffuse():
-        def one_pass(index, carry):
-            here = [u_ref[at(step), :] for step in range(STEP)]
-            seam = []
-            for step in range(STEP):
-                final = (count - 1) * STEP + step
-                ahead = pltpu.roll(here[step], SUB - 1, 0)
-                seam.append(east_ref[at(final), :] * (ahead - u_ref[at(final), :]))
+        def two_passes(index, carry):
+            here = load(u_ref, 0)
+            seam = seam_of(load(u_ref, count - 1), here)
             west = [pltpu.roll(flux, 1, 0) for flux in seam]
+            before = start = behind = None
             for j in range(count):
-                base = j * STEP
                 if j + 1 < count:
-                    ahead = [u_ref[at(base + STEP + step), :] for step in range(STEP)]
-                    flux = [
-                        east_ref[at(base + step), :] * (ahead[step] - here[step]) for step in range(STEP)
-                    ]
+                    ahead = load(u_ref, j + 1)
+                    flux = across(j, here, ahead)
                 else:
                     ahead, flux = here, seam
-                above = here[1:] + [pltpu.roll(here[0], LANES - 1, 1)]
-                rise = [north_ref[at(base + step), :] * (above[step] - here[step]) for step in range(STEP)]
-                below = [pltpu.roll(rise[STEP - 1], 1, 1)] + rise[:-1]
-                for step in range(STEP):
-                    u_ref[at(base + step), :] = here[step] + (
-                        (flux[step] - west[step]) + (rise[step] - below[step])
-                    )
+                after = advance(j, here, flux, west)
                 west, here = flux, ahead
+                if j == 0:
+                    save(0, after)
+                else:
+                    cross = across(j - 1, before, after)
+                    if j == 1:
+                        start = cross
+                    else:
+                        save(j - 1, advance(j - 1, before, cross, behind))
+                    behind = cross
+                before = after
+            first = load(u_ref, 0)
+            seam = seam_of(before, first)
+            save(count - 1, advance(count - 1, before, seam, behind))
+            save(0, advance(0, first, start, [pltpu.roll(flux, 1, 0) for flux in seam]))
             return carry
 
-        lax.fori_loop(0, PASSES, one_pass, 0)
+        lax.fori_loop(0, PASSES // 2, two_passes, 0)
 
     zero = jnp.zeros((SUB, LANES), F32)
     own = [
@@ -347,57 +376,67 @@
     def tally():
         return {edges: zero for edges in spans}
 
-    def whole(sums, extra=None):
+    def whole(sums):
         out = zero
         for edges, members in spans.items():
-            keep = own[members[0]] if extra is None else own[members[0]] & extra
-            out = out + jnp.where(keep, sums[edges], 0.0)
+            out = out + jnp.where(own[members[0]], sums[edges], 0.0)
         return jnp.sum(jnp.sum(out, axis=1, keepdims=True), axis=0, keepdims=True)
 
     def ratio(top, bottom):
         return jnp.where(bottom > 0, top / jnp.where(bottom > 0, bottom, 1.0), 0.0)
 
-    once = group == 0
     sum_bb, sum_bw, sum_00, sum_01 = tally(), tally(), tally(), tally()
-    for index in range(total):
-        u_ref[at(index), :] = lam * scale_ref[at(index), :] * grid_ref[0, at(index), :]
+    for j in range(count):
+        omega_ref[at(j), :] = wide_ref[1, pl.ds(j, SUB, stride=count), :]
+        spread = replicate(wide_ref[0, pl.ds(j, SUB, stride=count), :])
+        for step in range(STEP):
+            index = j * STEP + step
+            u_ref[at(index), :] = lam * scale_ref[at(index), :] * spread[step]
     diffuse()
     for index in range(total):
         rhs = u_ref[at(index), :]
         rhs_ref[at(index), :] = rhs
         sum_bb[kind_of[index // STEP]] += rhs * rhs
     diffuse()
-    for index in range(total):
-        scale = scale_ref[at(index), :]
-        image = scale * u_ref[at(index), :]
-        seen = group_sum(lam * image)
-        weighted = grid_ref[1, at(index), :] * seen
-        image_ref[at(index), :] = image
-        t_ref[0, at(index), :] = seen
-        u_ref[at(index), :] = lam * scale * weighted
-        sum_00[kind_of[index // STEP]] += weighted * seen
+    for j in range(count):
+        terms = []
+        for index in range(j * STEP, (j + 1) * STEP):
+            image = scale_ref[at(index), :] * u_ref[at(index), :]
+            image_ref[at(index), :] = image
+            terms.append(lam * image)
+        seen = fold(terms)
+        weighted = omega_ref[at(j), :] * seen
+        t_ref[0, at(j), :] = seen
+        sum_00[kind_of[j]] += weighted * seen
+        spread = replicate(weighted)
+        for step in range(STEP):
+            index = j * STEP + step
+            u_ref[at(index), :] = lam * scale_ref[at(index), :] * spread[step]
     diffuse()
     for index in range(total):
         turn = u_ref[at(index), :]
         turn_ref[at(index), :] = turn
         sum_bw[kind_of[index // STEP]] += turn * rhs_ref[at(index), :]
     diffuse()
-    for index in range(total):
-        image = scale_ref[at(index), :] * u_ref[at(index), :]
-        image_next_ref[at(index), :] = image
-        seen = group_sum(lam * image)
-        t_ref[1, at(index), :] = seen
-        sum_01[kind_of[index // STEP]] += grid_ref[1, at(index), :] * t_ref[0, at(index), :] * seen
-    bb, bw, s00, s01 = whole(sum_bb), whole(sum_bw), whole(sum_00, once), whole(sum_01, once)
+    for j in range(count):
+        terms = []
+        for index in range(j * STEP, (j + 1) * STEP):
+            image = scale_ref[at(index), :] * u_ref[at(index), :]
+            image_next_ref[at(index), :] = image
+            terms.append(lam * image)
+        seen = fold(terms)
+        t_ref[1, at(j), :] = seen
+        sum_01[kind_of[j]] += omega_ref[at(j), :] * t_ref[0, at(j), :] * seen
+    bb, bw, s00, s01 = whole(sum_bb), whole(sum_bw), whole(sum_00), whole(sum_01)
     fit, seen_fit = ratio(bw, bb), ratio(s01, s00)
     left, seen_left = tally(), tally()
     for index in range(total):
-        kind = kind_of[index // STEP]
         gap = turn_ref[at(index), :] - fit * rhs_ref[at(index), :]
-        left[kind] += gap * gap
-        gap = t_ref[1, at(index), :] - seen_fit * t_ref[0, at(index), :]
-        seen_left[kind] += grid_ref[1, at(index), :] * (gap * gap)
-    rest, seen_rest = whole(left), whole(seen_left, once)
+        left[kind_of[index // STEP]] += gap * gap
+    for j in range(count):
+        gap = t_ref[1, at(j), :] - seen_fit * t_ref[0, at(j), :]
+        seen_left[kind_of[j]] += omega_ref[at(j), :] * (gap * gap)
+    rest, seen_rest = whole(left), whole(seen_left)
     wide = iota(parts_ref.shape, 1)
     parts = jnp.zeros(parts_ref.shape, F32)
     for position, number in enumerate((bb, s00, bw, s01, fit, seen_fit, rest, seen_rest)):
@@ -406,10 +445,7 @@
     edge = RIM // STEP
     for plane, target in enumerate((seen_ref, seen_next_ref)):
         for j in range(count):
-            x = t_ref[plane, at(j * STEP), :]
-            for step in range(1, STEP):
-                x = jnp.where(group == step, t_ref[plane, at(j * STEP + step), :], x)
-            line_ref[pl.ds(j, SUB, stride=count), :] = x
+            line_ref[pl.ds(j, SUB, stride=count), :] = t_ref[plane, at(j), :]
         flat = jnp.transpose(line_ref[RIM : RIM + cols, :])
         depth = REACH - 2 * edge
         for step in range(STEP):
@@ -548,24 +584,22 @@
     for line, flag in enumerate((last, lat_index * lon_count + lon_index, lat_index % 2, lon_index % 2)):
         flags = jnp.where(iota(flags.shape, 0) == line, flag.astype(jnp.int32), flags)
 
-    face_low, face_high, *face_ends = call(
+    tables = (owner.reshape(1, tiles), row_ids.reshape(1, tiles), innovation, inv_var, offsets)
+    face_low, face_high, *rest = call(
         functools.partial(faces_kernel, fields),
-        [((3 * fields, half, LANES), F32)] * 4,
-        (flags, lat_coef, lon_coef, std_scale, land_mask),
+        [((3 * fields, half, LANES), F32)] * 4 + [(x.shape, x.dtype) for x in tables],
+        (flags, lat_coef, lon_coef, std_scale, land_mask) + tables,
         scratch=[pltpu.VMEM(x.shape, x.dtype) for x in (lat_coef, lon_coef, std_scale, land_mask)]
-        + [pltpu.SemaphoreType.DMA((4,))],
-        hbm=(1, 2, 3, 4),
-    )
+        + [pltpu.SemaphoreType.DMA((9,))],
+        hbm=range(1, 10),
+    )
+    face_ends, tables = rest[0:2], rest[2:]
     block = 2 * capacity + 1
-    tables = (owner.reshape(1, tiles), row_ids.reshape(1, tiles), innovation, inv_var, offsets)
     send, slot = call(
         functools.partial(route_kernel, devices, capacity),
         [((devices * block, LANES), F32), ((tiles, LANES), F32)],
-        (flags,) + tables,
-        scratch=[pltpu.VMEM((tiles, 2 * LANES), F32), pltpu.VMEM((slots, 2 * LANES), F32)]
-        + [pltpu.VMEM(x.shape, x.dtype) for x in tables]
-        + [pltpu.SemaphoreType.DMA((len(tables),))],
-            hbm=range(1, 1 + len(tables)),
+        (flags, *tables),
+        scratch=[pltpu.VMEM((tiles, 2 * LANES), F32), pltpu.VMEM((slots, 2 * LANES), F32)],
         flops=10**9,
         nbytes=10**7,
     )
@@ -602,10 +636,10 @@
         scratch=(
             pltpu.VMEM(woven, F32),
             pltpu.VMEM((2, span, LANES), F32),
-            pltpu.VMEM((2,) + woven, F32),
+            pltpu.VMEM((span, LANES), F32),
             pltpu.VMEM(woven, F32),
             pltpu.VMEM(woven, F32),
-            pltpu.VMEM((2,) + woven, F32),
+            pltpu.VMEM((2, span, LANES), F32),
             pltpu.VMEM((span, LANES), F32),
         ),
         flops=10**9,
@@ -626,7 +660,7 @@
         scratch=(pltpu.VMEM((STEP, span, LANES), F32),),
         nbytes=10**6,
     )
-    (departure,) = call(depart_kernel, [((tiles, width), F32)], (back, slot, offsets, innovation))
+    (departure,) = call(depart_kernel, [((tiles, width), F32)], (back, slot, tables[4], tables[2]))
     return increment, departure
 
 

time: 95.9 us -> 95.1 us (level)
  Pallas kernels: 20.1 us -> 18.3 us
  waiting for transfers between devices: 46.3 us -> 47.5 us
    pallas_call x11, Pallas kernels: 20.1 us -> 18.3 us  [call(): pl.pallas_call(kernel, out_shape=[jax.ShapeDtypeStruct(shape, dtype) for...]
    ppermute x4, waiting for transfers between devices: 19.8 us -> 20.9 us  [swap(): lax.ppermute(first, axis, both[0])]
  transfers between devices with their start and end apart: 11 -> 11, of which waited for: 7 -> 7; matrix products, arithmetic and copies ran while one was open for 0% -> 0% of each run, Pallas kernels for 4% -> 2%
where the time goes in v4:
time: 95.1 us; the launch traced here: 94.7 us
  waiting for transfers between devices  47.5 us (50%)
  starting transfers between devices  27.9 us (29%)
  Pallas kernels  18.3 us (19%)
    ppermute x4, waiting for transfers between devices, swap(): lax.ppermute(first, axis, both[0])  20.9 us
    pallas_call x11, Pallas kernels, call(): pl.pallas_call(kernel, out_shape=[jax.ShapeDtypeStruct(shape, dtype) for...  18.3 us
    all_to_all x1, waiting for transfers between devices, analyse(): lax.all_to_all(back.reshape(devices, capacity, LANES), AXES, split_axis=0...  14.8 us
    ppermute x4, starting transfers between devices, swap(): lax.ppermute(first, axis, both[0])  9.12 us
    all_to_all x1, starting transfers between devices, analyse(): lax.all_to_all(send.reshape(devices, 1, block * LANES), AXES, split_axis=...  7.31 us
    all_to_all x1, waiting for transfers between devices, analyse(): parts = lax.all_to_all(parts, AXES, split_axis=0, concat_axis=0, tiled=True)  6.6 us
    ppermute x4, starting transfers between devices, swap(): lax.ppermute(second, axis, both[1])  4.55 us
    all_to_all x1, starting transfers between devices, analyse(): parts = lax.all_to_all(parts, AXES, split_axis=0, concat_axis=0, tiled=True)  4.3 us
  transfers between devices with their start and end apart: 11, of which 7 were waited for; matrix products, arithmetic and copies ran while one was open for 0% of the time, Pallas kernels for 2%

profile of v4, /device:TPU:0, one launch (start us, length us, event | category | flops | bytes accessed | tf_op | source)
XLA Modules:
  0.0 94.7 jit_solution(503092463921419988)
XLA Ops:
  0.7 0.1 select_select_fusion.flags_ref.refs_0_
  0.8 1.4 %shard_map.113 = (f32[12,32,128]{2,1,0:T(8,128)S(1)}, f32[12,32,128]{2,1,0:T(8,128)S(1)}, f32[12,32,128]{2,1,0:T(8,128)S(1)}, f32[12,32,128]{2,1,0:T(8,128)S(1)}...) custom-call(s32[8,128]{1,0:T(8,128)S(1)} %select_select_fusion.flags, ...), custom_call_target="tpu_custom_call" | custom-call | flops 1000 | bytes 100000 | tf_op jit(solution)/shard_map/pallas_call | solution.py:36
  2.2 4.5 %shard_map.116 = (f32[2080,128]{1,0:T(8,128)}, f32[512,128]{1,0:T(8,128)S(1)}) custom-call(s32[8,128]{1,0:T(8,128)S(1)} %select_select_fusion.flags_ref.refs_0_, s32[1,512]{1,0:T(1,128)S(1)} %get-tuple-element.44.refs_1_, s32[1,512]{1,0:T(1,128)S(1)} %get-tuple-element.45.refs_2_, f32[512,128]{1,0:T(8,128)S(1)} %get-tuple-element.46.refs_3_.inn_ref, ...), custom_call_target="tpu_custom_call" | custom-call | flops 1000000000 | bytes 10000000 | tf_op jit(solution)/shard_map/pallas_call | solution.py:36
  6.8 7.3 %all-to-all-start = ((f32[32,1,8320]{2,1,0:T(1,128)}), f32[32,1,8320]{2,1,0:T(1,128)S(1)}, u32[]{:S(2)}, u32[]{:S(2)}) async-start(f32[32,1,8320]{2,1,0:T(1,128)} %bitcast.2), calls=%async_computation | async-start | bytes 2129920 | tf_op jit(solution)/shard_map/all_to_all | solution.py:613
  14.1 0.0 copy-start
  14.1 1.8 %collective-permute-start = (f32[12,32,128]{2,1,0:T(8,128)S(1)}, f32[12,32,128]{2,1,0:T(8,128)S(1)}, u32[]{:S(2)}, u32[]{:S(2)}) collective-permute-start(f32[12,32,128]{2,1,0:T(8,128)S(1)} %get-tuple-element.36), channel_id=1, source_target_pairs={{0,8},{16,24},{8,0},{24,16},{1,9},{17,25},{9,1},{25,17},{2,10},{18... | collective-permute-start | bytes 589832 | tf_op jit(solution)/shard_map/ppermute | solution.py:551
  15.9 0.7 collective-permute-start.1
  16.6 19.6 %collective-permute-done.got_ref = f32[12,32,128]{2,1,0:T(8,128)S(1)} collective-permute-done((f32[12,32,128]{2,1,0:T(8,128)S(1)}, f32[12,32,128]{2,1,0:T(8,128)S(1)}, u32[]{:S(2)}, u32[]{:S(2)}) %collective-permute-start) | collective-permute-done | bytes 196640 | tf_op jit(solution)/shard_map/ppermute | solution.py:551
  36.2 0.0 collective-permute-done.1.other_ref
  36.2 0.3 shard_map.114
  36.5 0.1 collective-permute-start.2
  36.6 2.6 %collective-permute-start.3 = (f32[12,32,128]{2,1,0:T(8,128)S(1)}, f32[12,32,128]{2,1,0:T(8,128)S(1)}, u32[]{:S(2)}, u32[]{:S(2)}) collective-permute-start(f32[12,32,128]{2,1,0:T(8,128)S(1)} %get-tuple-element.40), channel_id=1, source_target_pairs={{1,2},{3,4},{5,6},{7,0},{2,1},{4,3},{6,5},{0,7},{9,10},{11,12},{13... | collective-permute-start | bytes 589832 | tf_op jit(solution)/shard_map/ppermute | solution.py:551
  39.2 2.1 %all-to-all-done = f32[32,1,8320]{2,1,0:T(1,128)S(1)} async-done(((f32[32,1,8320]{2,1,0:T(1,128)}), f32[32,1,8320]{2,1,0:T(1,128)S(1)}, u32[]{:S(2)}, u32[]{:S(2)}) %all-to-all-start) | async-done | bytes 1064992 | tf_op jit(solution)/shard_map/all_to_all | solution.py:613
  41.2 0.3 shard_map.117
  41.5 7.1 %collective-permute-start.4 = (f32[2,32,128]{2,1,0:T(8,128)S(1)}, f32[2,32,128]{2,1,0:T(8,128)S(1)}, u32[]{:S(2)}, u32[]{:S(2)}) collective-permute-start(f32[2,32,128]{2,1,0:T(8,128)S(1)} %get-tuple-element.52), channel_id=1, source_target_pairs={{0,8},{16,24},{8,0},{24,16},{1,9},{17,25},{9,1},{25,17},{2,10},{18... | collective-permute-start | bytes 98312 | tf_op jit(solution)/shard_map/ppermute | solution.py:551
  48.7 0.7 collective-permute-start.5
  49.3 1.2 %collective-permute-done.4.got_ref = f32[2,32,128]{2,1,0:T(8,128)S(1)} collective-permute-done((f32[2,32,128]{2,1,0:T(8,128)S(1)}, f32[2,32,128]{2,1,0:T(8,128)S(1)}, u32[]{:S(2)}, u32[]{:S(2)}) %collective-permute-start.4) | collective-permute-done | bytes 32800 | tf_op jit(solution)/shard_map/ppermute | solution.py:551
  50.6 0.0 collective-permute-done.5.other_ref
  50.6 0.1 shard_map.118
  50.7 0.1 collective-permute-start.6
  50.7 0.6 collective-permute-start.7
  51.4 0.0 copy-done
  51.4 0.1 broadcast_in_dim.27
  51.5 0.1 broadcast_in_dim.28
  51.5 0.0 collective-permute-done.2.got_ref
  51.6 0.0 collective-permute-done.3.other_ref
  51.6 0.3 shard_map.115
  51.9 0.1 collective-permute-done.6.got_ref
  51.9 3.1 %collective-permute-done.7.other_ref = f32[2,32,128]{2,1,0:T(8,128)S(1)} collective-permute-done((f32[2,32,128]{2,1,0:T(8,128)S(1)}, f32[2,32,128]{2,1,0:T(8,128)S(1)}, u32[]{:S(2)}, u32[]{:S(2)}) %collective-permute-start.7) | collective-permute-done | bytes 32800 | tf_op jit(solution)/shard_map/ppermute | solution.py:551
  55.1 7.6 %shard_map.119 = (f32[768,128]{1,0:T(8,128)S(1)}, f32[768,128]{1,0:T(8,128)S(1)}, f32[64,128]{1,0:T(8,128)S(1)}, f32[64,128]{1,0:T(8,128)S(1)}, f32[32,128]{1,0:T(8,128)}) custom-call(s32[8,128]{1,0:T(8,128)S(1)} %select_select_fusion.flags_ref.refs_0_, f32[768,128]{1,0:T(8,128)S(1)} %get-tuple-element.41.north_ref, ...), custom_call_target="tpu_custom_call" | custom-call | flops 1000000000 | bytes 10000000 | tf_op jit(solution)/shard_map/pallas_call | solution.py:36
  62.6 4.3 %all-to-all-start.1 = ((f32[32,1,128]{2,1,0:T(1,128)}), f32[32,1,128]{2,1,0:T(1,128)S(1)}, u32[]{:S(2)}, u32[]{:S(2)}) async-start(f32[32,1,128]{2,1,0:T(1,128)} %bitcast.5), calls=%async_computation.1 | async-start | bytes 32768 | tf_op jit(solution)/shard_map/all_to_all | solution.py:649
  67.0 0.5 shard_map.120.both_ref
  67.5 6.6 %all-to-all-done.1 = f32[32,1,128]{2,1,0:T(1,128)S(1)} async-done(((f32[32,1,128]{2,1,0:T(1,128)}), f32[32,1,128]{2,1,0:T(1,128)S(1)}, u32[]{:S(2)}, u32[]{:S(2)}) %all-to-all-start.1) | async-done | bytes 16416 | tf_op jit(solution)/shard_map/all_to_all | solution.py:649
  74.1 1.2 %shard_map.121 = (f32[1024,128]{1,0:T(8,128)}, f32[8,128]{1,0:T(8,128)S(1)}) custom-call(f32[32,128]{1,0:T(8,128)S(1)} %bitcast.12, f32[1024,256]{1,0:T(8,128)S(1)} %shard_map.120.both_ref), custom_call_target="tpu_custom_call" | custom-call | flops 1000 | bytes 1000000 | tf_op jit(solution)/shard_map/pallas_call | solution.py:36
  75.2 2.6 %all-to-all-start.2 = ((f32[32,32,128]{2,1,0:T(8,128)}), f32[32,32,128]{2,1,0:T(8,128)S(1)}, u32[]{:S(2)}, u32[]{:S(2)}) async-start(f32[32,32,128]{2,1,0:T(8,128)} %bitcast.7), calls=%async_computation.2 | async-start | bytes 1048576 | tf_op jit(solution)/shard_map/all_to_all | solution.py:653
  77.9 0.8 shard_map.122
  78.7 14.8 %all-to-all-done.2 = f32[32,32,128]{2,1,0:T(8,128)S(1)} async-done(((f32[32,32,128]{2,1,0:T(8,128)}), f32[32,32,128]{2,1,0:T(8,128)S(1)}, u32[]{:S(2)}, u32[]{:S(2)}) %all-to-all-start.2) | async-done | bytes 524320 | tf_op jit(solution)/shard_map/all_to_all | solution.py:653
  93.5 1.3 %shard_map.123 = f32[512,128]{1,0:T(8,128)} custom-call(f32[1024,128]{1,0:T(8,128)S(1)} %bitcast.11, f32[512,128]{1,0:T(8,128)S(1)} %get-tuple-element.65.slot_ref, s32[512,128]{1,0:T(8,128)S(1)} %get-tuple-element.48.refs_5_.off_ref, f32[512,128]{1,0:T(8,128)S(1)} %get-tuple-element.46.refs_3_.inn_ref), custom_call_target="tpu_custom_call" | custom-call | flops 1000 | bytes 100000 | tf_op jit(solution)/shard_map/pallas_call | solution.py:36
  (4 shorter events, 0.0 us)
Async XLA Ops:
  6.8 34.4 %all-to-all-start = ((f32[32,1,8320]{2,1,0:T(1,128)}), f32[32,1,8320]{2,1,0:T(1,128)S(1)}, u32[]{:S(2)}, u32[]{:S(2)}) async-start(f32[32,1,8320]{2,1,0:T(1,128)} %bitcast.2), calls=%async_computation | async-start | bytes 2129920 | tf_op jit(solution)/shard_map/all_to_all | solution.py:613
  14.1 37.3 %copy-start = (f32[4]{0:T(128)S(1)}, f32[4]{0:T(128)}, u32[]{:S(2)}) copy-start(f32[4]{0:T(128)} %param.14) | copy-start | bytes 52
  14.1 22.1 %collective-permute-start = (f32[12,32,128]{2,1,0:T(8,128)S(1)}, f32[12,32,128]{2,1,0:T(8,128)S(1)}, u32[]{:S(2)}, u32[]{:S(2)}) collective-permute-start(f32[12,32,128]{2,1,0:T(8,128)S(1)} %get-tuple-element.36), channel_id=1, source_target_pairs={{0,8},{16,24},{8,0},{24,16},{1,9},{17,25},{9,1},{25,17},{2,10},{18... | collective-permute-start | bytes 589832 | tf_op jit(solution)/shard_map/ppermute | solution.py:551
  15.9 20.3 %collective-permute-start.1 = (f32[12,32,128]{2,1,0:T(8,128)S(1)}, f32[12,32,128]{2,1,0:T(8,128)S(1)}, u32[]{:S(2)}, u32[]{:S(2)}) collective-permute-start(f32[12,32,128]{2,1,0:T(8,128)S(1)} %get-tuple-element.37), channel_id=1, source_target_pairs={{8,16},{16,8},{9,17},{17,9},{10,18},{18,10},{11,19},{19,11},{12,20... | collective-permute-start | bytes 589832 | tf_op jit(solution)/shard_map/ppermute | solution.py:551
  36.5 15.1 %collective-permute-start.2 = (f32[12,32,128]{2,1,0:T(8,128)S(1)}, f32[12,32,128]{2,1,0:T(8,128)S(1)}, u32[]{:S(2)}, u32[]{:S(2)}) collective-permute-start(f32[12,32,128]{2,1,0:T(8,128)S(1)} %get-tuple-element.39), channel_id=1, source_target_pairs={{0,1},{2,3},{4,5},{6,7},{1,0},{3,2},{5,4},{7,6},{8,9},{10,11},{12,... | collective-permute-start | bytes 589832 | tf_op jit(solution)/shard_map/ppermute | solution.py:551
  36.6 15.0 %collective-permute-start.3 = (f32[12,32,128]{2,1,0:T(8,128)S(1)}, f32[12,32,128]{2,1,0:T(8,128)S(1)}, u32[]{:S(2)}, u32[]{:S(2)}) collective-permute-start(f32[12,32,128]{2,1,0:T(8,128)S(1)} %get-tuple-element.40), channel_id=1, source_target_pairs={{1,2},{3,4},{5,6},{7,0},{2,1},{4,3},{6,5},{0,7},{9,10},{11,12},{13... | collective-permute-start | bytes 589832 | tf_op jit(solution)/shard_map/ppermute | solution.py:551
  41.5 9.0 %collective-permute-start.4 = (f32[2,32,128]{2,1,0:T(8,128)S(1)}, f32[2,32,128]{2,1,0:T(8,128)S(1)}, u32[]{:S(2)}, u32[]{:S(2)}) collective-permute-start(f32[2,32,128]{2,1,0:T(8,128)S(1)} %get-tuple-element.52), channel_id=1, source_target_pairs={{0,8},{16,24},{8,0},{24,16},{1,9},{17,25},{9,1},{25,17},{2,10},{18... | collective-permute-start | bytes 98312 | tf_op jit(solution)/shard_map/ppermute | solution.py:551
  48.7 1.9 %collective-permute-start.5 = (f32[2,32,128]{2,1,0:T(8,128)S(1)}, f32[2,32,128]{2,1,0:T(8,128)S(1)}, u32[]{:S(2)}, u32[]{:S(2)}) collective-permute-start(f32[2,32,128]{2,1,0:T(8,128)S(1)} %get-tuple-element.53), channel_id=1, source_target_pairs={{8,16},{16,8},{9,17},{17,9},{10,18},{18,10},{11,19},{19,11},{12,20... | collective-permute-start | bytes 98312 | tf_op jit(solution)/shard_map/ppermute | solution.py:551
  50.7 1.3 %collective-permute-start.6 = (f32[2,32,128]{2,1,0:T(8,128)S(1)}, f32[2,32,128]{2,1,0:T(8,128)S(1)}, u32[]{:S(2)}, u32[]{:S(2)}) collective-permute-start(f32[2,32,128]{2,1,0:T(8,128)S(1)} %get-tuple-element.55), channel_id=1, source_target_pairs={{0,1},{2,3},{4,5},{6,7},{1,0},{3,2},{5,4},{7,6},{8,9},{10,11},{12,... | collective-permute-start | bytes 98312 | tf_op jit(solution)/shard_map/ppermute | solution.py:551
  50.7 4.3 %collective-permute-start.7 = (f32[2,32,128]{2,1,0:T(8,128)S(1)}, f32[2,32,128]{2,1,0:T(8,128)S(1)}, u32[]{:S(2)}, u32[]{:S(2)}) collective-permute-start(f32[2,32,128]{2,1,0:T(8,128)S(1)} %get-tuple-element.56), channel_id=1, source_target_pairs={{1,2},{3,4},{5,6},{7,0},{2,1},{4,3},{6,5},{0,7},{9,10},{11,12},{13... | collective-permute-start | bytes 98312 | tf_op jit(solution)/shard_map/ppermute | solution.py:551
  62.6 11.4 %all-to-all-start.1 = ((f32[32,1,128]{2,1,0:T(1,128)}), f32[32,1,128]{2,1,0:T(1,128)S(1)}, u32[]{:S(2)}, u32[]{:S(2)}) async-start(f32[32,1,128]{2,1,0:T(1,128)} %bitcast.5), calls=%async_computation.1 | async-start | bytes 32768 | tf_op jit(solution)/shard_map/all_to_all | solution.py:649
  75.2 18.2 %all-to-all-start.2 = ((f32[32,32,128]{2,1,0:T(8,128)}), f32[32,32,128]{2,1,0:T(8,128)S(1)}, u32[]{:S(2)}, u32[]{:S(2)}) async-start(f32[32,32,128]{2,1,0:T(8,128)} %bitcast.7), calls=%async_computation.2 | async-start | bytes 1048576 | tf_op jit(solution)/shard_map/all_to_all | solution.py:653

commit v5 on v4

--- a/solution.py
+++ b/solution.py
@@ -133,7 +133,7 @@
         rows_ref[window, LANES : 2 * LANES] = jnp.where(sub < 4, pltpu.roll(first, 4, 0), second)
         return carry
 
-    lax.fori_loop(0, tiles // GROUP, expand, 0, unroll=32)
+    lax.fori_loop(0, tiles // GROUP, expand, 0, unroll=64)
     upper, lower = split(rows_ref[...])
     slots = devices * capacity
     place = (iota((slots, tiles), 0) == slot_row).astype(F32).astype(BF16)
@@ -548,7 +548,9 @@
     if periodic:
         pairs[1].append((count - 1, 0))
     both = [edges + [(target, source) for source, target in edges] for edges in pairs]
-    return lax.ppermute(first, axis, both[0]), lax.ppermute(second, axis, both[1])
+    got = lax.ppermute(first, axis, both[0])
+    other = lax.ppermute(second, axis, both[1])
+    return got, other
 
 
 def exchange(flags, low, high, first, second, order):

time: 95.1 us -> 94.3 us (level)
  no operation moved by 1% of the time
where the time goes in v5:
time: 94.3 us; the launch traced here: 93.9 us
  waiting for transfers between devices  47.5 us (50%)
  starting transfers between devices  27.9 us (30%)
  Pallas kernels  17.5 us (19%)
    ppermute x4, waiting for transfers between devices, swap(): got = lax.ppermute(first, axis, both[0])  20.9 us
    pallas_call x11, Pallas kernels, call(): pl.pallas_call(kernel, out_shape=[jax.ShapeDtypeStruct(shape, dtype) for...  17.5 us
    all_to_all x1, waiting for transfers between devices, analyse(): lax.all_to_all(back.reshape(devices, capacity, LANES), AXES, split_axis=0...  14.8 us
    ppermute x4, starting transfers between devices, swap(): got = lax.ppermute(first, axis, both[0])  9.11 us
    all_to_all x1, starting transfers between devices, analyse(): lax.all_to_all(send.reshape(devices, 1, block * LANES), AXES, split_axis=...  7.32 us
    all_to_all x1, waiting for transfers between devices, analyse(): parts = lax.all_to_all(parts, AXES, split_axis=0, concat_axis=0, tiled=True)  6.6 us
    ppermute x4, starting transfers between devices, swap(): other = lax.ppermute(second, axis, both[1])  4.55 us
    all_to_all x1, starting transfers between devices, analyse(): parts = lax.all_to_all(parts, AXES, split_axis=0, concat_axis=0, tiled=True)  4.3 us
  transfers between devices with their start and end apart: 11, of which 7 were waited for; matrix products, arithmetic and copies ran while one was open for 0% of the time, Pallas kernels for 2%

profile of v5, /device:TPU:0, one launch (start us, length us, event | category | flops | bytes accessed | tf_op | source)
XLA Modules:
  0.0 93.9 jit_solution(15690094879326524891)
XLA Ops:
  0.7 0.1 select_select_fusion.flags_ref.refs_0_
  0.8 1.4 %shard_map.113 = (f32[12,32,128]{2,1,0:T(8,128)S(1)}, f32[12,32,128]{2,1,0:T(8,128)S(1)}, f32[12,32,128]{2,1,0:T(8,128)S(1)}, f32[12,32,128]{2,1,0:T(8,128)S(1)}...) custom-call(s32[8,128]{1,0:T(8,128)S(1)} %select_select_fusion.flags, ...), custom_call_target="tpu_custom_call" | custom-call | flops 1000 | bytes 100000 | tf_op jit(solution)/shard_map/pallas_call | solution.py:36
  2.2 3.7 %shard_map.116 = (f32[2080,128]{1,0:T(8,128)}, f32[512,128]{1,0:T(8,128)S(1)}) custom-call(s32[8,128]{1,0:T(8,128)S(1)} %select_select_fusion.flags_ref.refs_0_, s32[1,512]{1,0:T(1,128)S(1)} %get-tuple-element.44.refs_1_, s32[1,512]{1,0:T(1,128)S(1)} %get-tuple-element.45.refs_2_, f32[512,128]{1,0:T(8,128)S(1)} %get-tuple-element.46.refs_3_.inn_ref, ...), custom_call_target="tpu_custom_call" | custom-call | flops 1000000000 | bytes 10000000 | tf_op jit(solution)/shard_map/pallas_call | solution.py:36
  5.9 7.3 %all-to-all-start = ((f32[32,1,8320]{2,1,0:T(1,128)}), f32[32,1,8320]{2,1,0:T(1,128)S(1)}, u32[]{:S(2)}, u32[]{:S(2)}) async-start(f32[32,1,8320]{2,1,0:T(1,128)} %bitcast.2), calls=%async_computation | async-start | bytes 2129920 | tf_op jit(solution)/shard_map/all_to_all | solution.py:615
  13.3 0.0 copy-start
  13.3 1.8 %collective-permute-start = (f32[12,32,128]{2,1,0:T(8,128)S(1)}, f32[12,32,128]{2,1,0:T(8,128)S(1)}, u32[]{:S(2)}, u32[]{:S(2)}) collective-permute-start(f32[12,32,128]{2,1,0:T(8,128)S(1)} %get-tuple-element.36), channel_id=1, source_target_pairs={{0,8},{16,24},{8,0},{24,16},{1,9},{17,25},{9,1},{25,17},{2,10},{18... | collective-permute-start | bytes 589832 | tf_op jit(solution)/shard_map/ppermute | solution.py:551
  15.1 0.7 collective-permute-start.1
  15.8 19.6 %collective-permute-done.got_ref = f32[12,32,128]{2,1,0:T(8,128)S(1)} collective-permute-done((f32[12,32,128]{2,1,0:T(8,128)S(1)}, f32[12,32,128]{2,1,0:T(8,128)S(1)}, u32[]{:S(2)}, u32[]{:S(2)}) %collective-permute-start) | collective-permute-done | bytes 196640 | tf_op jit(solution)/shard_map/ppermute | solution.py:551
  35.4 0.0 collective-permute-done.1.other_ref
  35.4 0.3 shard_map.114
  35.7 0.1 collective-permute-start.2
  35.7 2.6 %collective-permute-start.3 = (f32[12,32,128]{2,1,0:T(8,128)S(1)}, f32[12,32,128]{2,1,0:T(8,128)S(1)}, u32[]{:S(2)}, u32[]{:S(2)}) collective-permute-start(f32[12,32,128]{2,1,0:T(8,128)S(1)} %get-tuple-element.40), channel_id=1, source_target_pairs={{1,2},{3,4},{5,6},{7,0},{2,1},{4,3},{6,5},{0,7},{9,10},{11,12},{13... | collective-permute-start | bytes 589832 | tf_op jit(solution)/shard_map/ppermute | solution.py:552
  38.3 2.1 %all-to-all-done = f32[32,1,8320]{2,1,0:T(1,128)S(1)} async-done(((f32[32,1,8320]{2,1,0:T(1,128)}), f32[32,1,8320]{2,1,0:T(1,128)S(1)}, u32[]{:S(2)}, u32[]{:S(2)}) %all-to-all-start) | async-done | bytes 1064992 | tf_op jit(solution)/shard_map/all_to_all | solution.py:615
  40.4 0.3 shard_map.117
  40.7 7.1 %collective-permute-start.4 = (f32[2,32,128]{2,1,0:T(8,128)S(1)}, f32[2,32,128]{2,1,0:T(8,128)S(1)}, u32[]{:S(2)}, u32[]{:S(2)}) collective-permute-start(f32[2,32,128]{2,1,0:T(8,128)S(1)} %get-tuple-element.52), channel_id=1, source_target_pairs={{0,8},{16,24},{8,0},{24,16},{1,9},{17,25},{9,1},{25,17},{2,10},{18... | collective-permute-start | bytes 98312 | tf_op jit(solution)/shard_map/ppermute | solution.py:551
  47.8 0.7 collective-permute-start.5
  48.5 1.2 %collective-permute-done.4.got_ref = f32[2,32,128]{2,1,0:T(8,128)S(1)} collective-permute-done((f32[2,32,128]{2,1,0:T(8,128)S(1)}, f32[2,32,128]{2,1,0:T(8,128)S(1)}, u32[]{:S(2)}, u32[]{:S(2)}) %collective-permute-start.4) | collective-permute-done | bytes 32800 | tf_op jit(solution)/shard_map/ppermute | solution.py:551
  49.7 0.0 collective-permute-done.5.other_ref
  49.7 0.1 shard_map.118
  49.8 0.1 collective-permute-start.6
  49.9 0.6 collective-permute-start.7
  50.6 0.0 copy-done
  50.6 0.1 broadcast_in_dim.27
  50.6 0.1 broadcast_in_dim.28
  50.7 0.0 collective-permute-done.2.got_ref
  50.7 0.0 collective-permute-done.3.other_ref
  50.7 0.3 shard_map.115
  51.0 0.1 collective-permute-done.6.got_ref
  51.1 3.1 %collective-permute-done.7.other_ref = f32[2,32,128]{2,1,0:T(8,128)S(1)} collective-permute-done((f32[2,32,128]{2,1,0:T(8,128)S(1)}, f32[2,32,128]{2,1,0:T(8,128)S(1)}, u32[]{:S(2)}, u32[]{:S(2)}) %collective-permute-start.7) | collective-permute-done | bytes 32800 | tf_op jit(solution)/shard_map/ppermute | solution.py:552
  54.3 7.6 %shard_map.119 = (f32[768,128]{1,0:T(8,128)S(1)}, f32[768,128]{1,0:T(8,128)S(1)}, f32[64,128]{1,0:T(8,128)S(1)}, f32[64,128]{1,0:T(8,128)S(1)}, f32[32,128]{1,0:T(8,128)}) custom-call(s32[8,128]{1,0:T(8,128)S(1)} %select_select_fusion.flags_ref.refs_0_, f32[768,128]{1,0:T(8,128)S(1)} %get-tuple-element.41.north_ref, ...), custom_call_target="tpu_custom_call" | custom-call | flops 1000000000 | bytes 10000000 | tf_op jit(solution)/shard_map/pallas_call | solution.py:36
  61.8 4.3 %all-to-all-start.1 = ((f32[32,1,128]{2,1,0:T(1,128)}), f32[32,1,128]{2,1,0:T(1,128)S(1)}, u32[]{:S(2)}, u32[]{:S(2)}) async-start(f32[32,1,128]{2,1,0:T(1,128)} %bitcast.5), calls=%async_computation.1 | async-start | bytes 32768 | tf_op jit(solution)/shard_map/all_to_all | solution.py:651
  66.1 0.5 shard_map.120.both_ref
  66.6 6.6 %all-to-all-done.1 = f32[32,1,128]{2,1,0:T(1,128)S(1)} async-done(((f32[32,1,128]{2,1,0:T(1,128)}), f32[32,1,128]{2,1,0:T(1,128)S(1)}, u32[]{:S(2)}, u32[]{:S(2)}) %all-to-all-start.1) | async-done | bytes 16416 | tf_op jit(solution)/shard_map/all_to_all | solution.py:651
  73.2 1.2 %shard_map.121 = (f32[1024,128]{1,0:T(8,128)}, f32[8,128]{1,0:T(8,128)S(1)}) custom-call(f32[32,128]{1,0:T(8,128)S(1)} %bitcast.12, f32[1024,256]{1,0:T(8,128)S(1)} %shard_map.120.both_ref), custom_call_target="tpu_custom_call" | custom-call | flops 1000 | bytes 1000000 | tf_op jit(solution)/shard_map/pallas_call | solution.py:36
  74.4 2.6 %all-to-all-start.2 = ((f32[32,32,128]{2,1,0:T(8,128)}), f32[32,32,128]{2,1,0:T(8,128)S(1)}, u32[]{:S(2)}, u32[]{:S(2)}) async-start(f32[32,32,128]{2,1,0:T(8,128)} %bitcast.7), calls=%async_computation.2 | async-start | bytes 1048576 | tf_op jit(solution)/shard_map/all_to_all | solution.py:655
  77.0 0.8 shard_map.122
  77.9 14.8 %all-to-all-done.2 = f32[32,32,128]{2,1,0:T(8,128)S(1)} async-done(((f32[32,32,128]{2,1,0:T(8,128)}), f32[32,32,128]{2,1,0:T(8,128)S(1)}, u32[]{:S(2)}, u32[]{:S(2)}) %all-to-all-start.2) | async-done | bytes 524320 | tf_op jit(solution)/shard_map/all_to_all | solution.py:655
  92.7 1.3 %shard_map.123 = f32[512,128]{1,0:T(8,128)} custom-call(f32[1024,128]{1,0:T(8,128)S(1)} %bitcast.11, f32[512,128]{1,0:T(8,128)S(1)} %get-tuple-element.65.slot_ref, s32[512,128]{1,0:T(8,128)S(1)} %get-tuple-element.48.refs_5_.off_ref, f32[512,128]{1,0:T(8,128)S(1)} %get-tuple-element.46.refs_3_.inn_ref), custom_call_target="tpu_custom_call" | custom-call | flops 1000 | bytes 100000 | tf_op jit(solution)/shard_map/pallas_call | solution.py:36
  (4 shorter events, 0.0 us)
Async XLA Ops:
  5.9 34.5 %all-to-all-start = ((f32[32,1,8320]{2,1,0:T(1,128)}), f32[32,1,8320]{2,1,0:T(1,128)S(1)}, u32[]{:S(2)}, u32[]{:S(2)}) async-start(f32[32,1,8320]{2,1,0:T(1,128)} %bitcast.2), calls=%async_computation | async-start | bytes 2129920 | tf_op jit(solution)/shard_map/all_to_all | solution.py:615
  13.3 37.3 %copy-start = (f32[4]{0:T(128)S(1)}, f32[4]{0:T(128)}, u32[]{:S(2)}) copy-start(f32[4]{0:T(128)} %param.14) | copy-start | bytes 52
  13.3 22.1 %collective-permute-start = (f32[12,32,128]{2,1,0:T(8,128)S(1)}, f32[12,32,128]{2,1,0:T(8,128)S(1)}, u32[]{:S(2)}, u32[]{:S(2)}) collective-permute-start(f32[12,32,128]{2,1,0:T(8,128)S(1)} %get-tuple-element.36), channel_id=1, source_target_pairs={{0,8},{16,24},{8,0},{24,16},{1,9},{17,25},{9,1},{25,17},{2,10},{18... | collective-permute-start | bytes 589832 | tf_op jit(solution)/shard_map/ppermute | solution.py:551
  15.1 20.3 %collective-permute-start.1 = (f32[12,32,128]{2,1,0:T(8,128)S(1)}, f32[12,32,128]{2,1,0:T(8,128)S(1)}, u32[]{:S(2)}, u32[]{:S(2)}) collective-permute-start(f32[12,32,128]{2,1,0:T(8,128)S(1)} %get-tuple-element.37), channel_id=1, source_target_pairs={{8,16},{16,8},{9,17},{17,9},{10,18},{18,10},{11,19},{19,11},{12,20... | collective-permute-start | bytes 589832 | tf_op jit(solution)/shard_map/ppermute | solution.py:552
  35.7 15.1 %collective-permute-start.2 = (f32[12,32,128]{2,1,0:T(8,128)S(1)}, f32[12,32,128]{2,1,0:T(8,128)S(1)}, u32[]{:S(2)}, u32[]{:S(2)}) collective-permute-start(f32[12,32,128]{2,1,0:T(8,128)S(1)} %get-tuple-element.39), channel_id=1, source_target_pairs={{0,1},{2,3},{4,5},{6,7},{1,0},{3,2},{5,4},{7,6},{8,9},{10,11},{12,... | collective-permute-start | bytes 589832 | tf_op jit(solution)/shard_map/ppermute | solution.py:551
  35.7 15.0 %collective-permute-start.3 = (f32[12,32,128]{2,1,0:T(8,128)S(1)}, f32[12,32,128]{2,1,0:T(8,128)S(1)}, u32[]{:S(2)}, u32[]{:S(2)}) collective-permute-start(f32[12,32,128]{2,1,0:T(8,128)S(1)} %get-tuple-element.40), channel_id=1, source_target_pairs={{1,2},{3,4},{5,6},{7,0},{2,1},{4,3},{6,5},{0,7},{9,10},{11,12},{13... | collective-permute-start | bytes 589832 | tf_op jit(solution)/shard_map/ppermute | solution.py:552
  40.7 9.0 %collective-permute-start.4 = (f32[2,32,128]{2,1,0:T(8,128)S(1)}, f32[2,32,128]{2,1,0:T(8,128)S(1)}, u32[]{:S(2)}, u32[]{:S(2)}) collective-permute-start(f32[2,32,128]{2,1,0:T(8,128)S(1)} %get-tuple-element.52), channel_id=1, source_target_pairs={{0,8},{16,24},{8,0},{24,16},{1,9},{17,25},{9,1},{25,17},{2,10},{18... | collective-permute-start | bytes 98312 | tf_op jit(solution)/shard_map/ppermute | solution.py:551
  47.8 1.9 %collective-permute-start.5 = (f32[2,32,128]{2,1,0:T(8,128)S(1)}, f32[2,32,128]{2,1,0:T(8,128)S(1)}, u32[]{:S(2)}, u32[]{:S(2)}) collective-permute-start(f32[2,32,128]{2,1,0:T(8,128)S(1)} %get-tuple-element.53), channel_id=1, source_target_pairs={{8,16},{16,8},{9,17},{17,9},{10,18},{18,10},{11,19},{19,11},{12,20... | collective-permute-start | bytes 98312 | tf_op jit(solution)/shard_map/ppermute | solution.py:552
  49.8 1.3 %collective-permute-start.6 = (f32[2,32,128]{2,1,0:T(8,128)S(1)}, f32[2,32,128]{2,1,0:T(8,128)S(1)}, u32[]{:S(2)}, u32[]{:S(2)}) collective-permute-start(f32[2,32,128]{2,1,0:T(8,128)S(1)} %get-tuple-element.55), channel_id=1, source_target_pairs={{0,1},{2,3},{4,5},{6,7},{1,0},{3,2},{5,4},{7,6},{8,9},{10,11},{12,... | collective-permute-start | bytes 98312 | tf_op jit(solution)/shard_map/ppermute | solution.py:551
  49.9 4.3 %collective-permute-start.7 = (f32[2,32,128]{2,1,0:T(8,128)S(1)}, f32[2,32,128]{2,1,0:T(8,128)S(1)}, u32[]{:S(2)}, u32[]{:S(2)}) collective-permute-start(f32[2,32,128]{2,1,0:T(8,128)S(1)} %get-tuple-element.56), channel_id=1, source_target_pairs={{1,2},{3,4},{5,6},{7,0},{2,1},{4,3},{6,5},{0,7},{9,10},{11,12},{13... | collective-permute-start | bytes 98312 | tf_op jit(solution)/shard_map/ppermute | solution.py:552
  61.8 11.4 %all-to-all-start.1 = ((f32[32,1,128]{2,1,0:T(1,128)}), f32[32,1,128]{2,1,0:T(1,128)S(1)}, u32[]{:S(2)}, u32[]{:S(2)}) async-start(f32[32,1,128]{2,1,0:T(1,128)} %bitcast.5), calls=%async_computation.1 | async-start | bytes 32768 | tf_op jit(solution)/shard_map/all_to_all | solution.py:651
  74.4 18.2 %all-to-all-start.2 = ((f32[32,32,128]{2,1,0:T(8,128)}), f32[32,32,128]{2,1,0:T(8,128)S(1)}, u32[]{:S(2)}, u32[]{:S(2)}) async-start(f32[32,32,128]{2,1,0:T(8,128)} %bitcast.7), calls=%async_computation.2 | async-start | bytes 1048576 | tf_op jit(solution)/shard_map/all_to_all | solution.py:655
